TPU v7x, 32 devices: a whole 2x2x4 slice. The times are simulated.
32 devices in a mesh: grp: 2 (over x), seq: 8 (over z, y), dp: 2 (over core).
Axes of the slice: x: 2, y: 2, z: 4, core: 2. Of those that a mesh axis runs over, the one named last changes fastest.
Arguments:
- dec_query: bfloat16 [4, 1024, 2048], P(('grp', 'dp'), 'seq'), parts along dimension 0, may hold values from -9 to 9
- enc_key: bfloat16 [4, 4096, 2048], P(('grp', 'dp'), 'seq'), parts along dimension 0, may hold values from -4 to 4
- enc_value: bfloat16 [4, 4096, 2048], P(('grp', 'dp'), 'seq'), parts along dimension 0, may hold values from -6 to 6
- saved_out: bfloat16 [4, 1024, 2048], P(('grp', 'dp'), 'seq'), parts along dimension 0, may hold values from -3 to 3
- d_out: bfloat16 [4, 1024, 2048], P(('grp', 'dp'), 'seq'), parts along dimension 0, may hold values from -24 to 24
- dec_start: int32 [4, 33], P(('grp', 'dp')), parts along dimension 0, may hold values from 0 to 1024, as said below
- enc_start: int32 [4, 33], P(('grp', 'dp')), parts along dimension 0, may hold values from 0 to 4096, as said below
Outputs:
- d_query: bfloat16 [4, 1024, 2048], P(('grp', 'dp'), 'seq'), parts along dimension 0
- d_key: bfloat16 [4, 4096, 2048], P(('grp', 'dp'), 'seq'), parts along dimension 0
- d_value: bfloat16 [4, 4096, 2048], P(('grp', 'dp'), 'seq'), parts along dimension 0
There are 2 independent parts, one for each index of `grp`. A program takes and returns all parts, laid end to end along the dimension named above; each array names one. Nothing has to cross between parts.
Inputs may be any that keep to these rules, and one draw needn't show every extreme that they name: dec_start[b, 0] = 0 and dec_start[b, 32] = 1024; dec_start[b, k] = k * 32 plus a whole number from 0 to 16, so an example has 16 to 48 decoder tokens, and in every batch one example has exactly 48. enc_start[b, 0] = 0 and enc_start[b, 32] = 4096; enc_start[b, k] = k * 4 * 32 plus a whole number from 0 to 64, so an example has 64 to 192 encoder tokens, and in every batch one example has exactly 192.
All inputs are finite; a program needn't handle non-finite values.
Results may differ from a plain program's by a relative error of at most 0.005.
Values may be sent and summed in bfloat16 or wider, within the bound.
No kernel may reach another device: no remote copies, remote signals or barrier semaphores. Data moves between devices by JAX's collectives and lax.ppermute only.
A program may use at most 128 MiB of HBM per device.

v0:
```python
import jax
import jax.numpy as jnp
from jax import lax
from jax.sharding import PartitionSpec as P

H = 32
HD = 64
REACH = 128


masked_low = -1e30


def extended(cells, sides, width):
    for axis, dim in sides:
        count = lax.axis_size(axis)
        ends = count - 1
        head = lax.slice_in_dim(cells, 0, width, axis=dim)
        tail = lax.slice_in_dim(cells, cells.shape[dim] - width, cells.shape[dim], axis=dim)
        cells = jnp.concatenate(
            [
                lax.ppermute(tail, axis, [(i, (i + 1) % count) for i in range(ends)]),
                cells,
                lax.ppermute(head, axis, [((i + 1) % count, i) for i in range(ends)]),
            ],
            axis=dim,
        )
    return cells


def from_behind(shard, axis, by):
    devices = lax.axis_size(axis)
    pairs = [(i, i + by) for i in range(devices) if 0 <= i + by < devices]
    return lax.ppermute(shard, axis, pairs)


def example_ids(positions, starts, total):
    counts = jnp.sum((positions[:, None] >= starts[None, 1:-1]).astype(jnp.int32), axis=1)
    inside = (positions >= 0) & (positions < total)
    return jnp.where(inside, counts, -1)


def shards(dec_query, enc_key, enc_value, saved_out, d_out, dec_start, enc_start):
    q_rows = dec_query.shape[1]
    k_rows = enc_key.shape[1]
    row_width = dec_query.shape[2]
    head_count = H
    head_dim = HD
    seq_pos = lax.axis_index("seq")
    seq_count = lax.axis_size("seq")
    block_rows = 128
    rim_rows = -(-REACH // block_rows) * block_rows
    stacked = jnp.stack([enc_key[0], enc_value[0]])
    window = extended(stacked, (("seq", 1),), rim_rows)
    window_rows = k_rows + 2 * rim_rows
    n_blocks = window_rows // block_rows
    key_pos = seq_pos * k_rows - rim_rows + jnp.arange(window_rows, dtype=jnp.int32)
    key_ids = example_ids(key_pos, enc_start[0], seq_count * k_rows)
    query_pos = seq_pos * q_rows + jnp.arange(q_rows, dtype=jnp.int32)
    query_ids = example_ids(query_pos, dec_start[0], seq_count * q_rows)
    queries = dec_query[0].reshape(q_rows, head_count, head_dim)
    grads_out = d_out[0].reshape(q_rows, head_count, head_dim)
    outputs = saved_out[0].reshape(q_rows, head_count, head_dim)
    out_dot = jnp.sum(grads_out.astype(jnp.float32) * outputs.astype(jnp.float32), axis=2).T

    def key_block(block_idx):
        row_start = block_idx * block_rows
        keys_blk = lax.dynamic_slice_in_dim(window[0], row_start, block_rows, 0).reshape(
            block_rows, head_count, head_dim
        )
        values_blk = lax.dynamic_slice_in_dim(window[1], row_start, block_rows, 0).reshape(
            block_rows, head_count, head_dim
        )
        ids_blk = lax.dynamic_slice_in_dim(key_ids, row_start, block_rows, 0)
        allowed = query_ids[:, None] == ids_blk[None, :]
        return (keys_blk, values_blk, allowed)

    def stats_step(running, block_idx):
        keys_blk, values_blk, allowed = key_block(block_idx)
        prev_max, prev_sum = running
        scores = jnp.einsum("qhd,khd->hqk", queries, keys_blk, preferred_element_type=jnp.float32)
        masked = jnp.where(allowed[None], scores, masked_low)
        new_max = jnp.maximum(prev_max, jnp.max(masked, axis=2))
        weights = jnp.where(allowed[None], jnp.exp(masked - new_max[:, :, None]), 0.0)
        result = (new_max, prev_sum * jnp.exp(prev_max - new_max) + jnp.sum(weights, axis=2))
        return (result, None)

    start_stats = (
        jnp.full((head_count, q_rows), masked_low, jnp.float32),
        jnp.zeros((head_count, q_rows), jnp.float32),
    )
    (row_max, row_sum), _ = lax.scan(stats_step, start_stats, jnp.arange(n_blocks, dtype=jnp.int32))
    log_total = row_max + jnp.log(row_sum)

    def grad_step(dq_total, block_idx):
        keys_blk, values_blk, allowed = key_block(block_idx)
        scores = jnp.einsum("qhd,khd->hqk", queries, keys_blk, preferred_element_type=jnp.float32)
        masked = jnp.where(allowed[None], scores, masked_low)
        weights = jnp.where(allowed[None], jnp.exp(masked - log_total[:, :, None]), 0.0)
        weights_low = weights.astype(jnp.bfloat16)
        d_probs = jnp.einsum(
            "qhd,khd->hqk", grads_out, values_blk, preferred_element_type=jnp.float32
        )
        d_scores = (weights * (d_probs - out_dot[:, :, None])).astype(jnp.bfloat16)
        dq_new = dq_total + jnp.einsum(
            "hqk,khd->qhd", d_scores, keys_blk, preferred_element_type=jnp.float32
        )
        dk_blk = jnp.einsum("hqk,qhd->khd", d_scores, queries, preferred_element_type=jnp.float32)
        dv_blk = jnp.einsum(
            "hqk,qhd->khd", weights_low, grads_out, preferred_element_type=jnp.float32
        )
        return (
            dq_new,
            jnp.stack(
                [dk_blk.reshape(block_rows, row_width), dv_blk.reshape(block_rows, row_width)]
            ),
        )

    start_query = jnp.zeros((q_rows, head_count, head_dim), jnp.float32)
    dq_final, pieces = lax.scan(grad_step, start_query, jnp.arange(n_blocks, dtype=jnp.int32))
    rim_blocks = rim_rows // block_rows
    own_blocks = k_rows // block_rows
    left_part = pieces[:rim_blocks]
    own_part = pieces[rim_blocks : rim_blocks + own_blocks]
    right_part = pieces[rim_blocks + own_blocks :]
    from_next = from_behind(left_part, "seq", -1)
    from_prev = from_behind(right_part.astype(jnp.bfloat16), "seq", 1).astype(right_part.dtype)
    filler = jnp.zeros((own_blocks - rim_blocks, 2, block_rows, row_width), jnp.float32)
    summed = (
        own_part
        + jnp.concatenate([from_prev, filler], axis=0)
        + jnp.concatenate([filler, from_next], axis=0)
    )
    grad_key = summed[:, 0].reshape(k_rows, row_width).astype(jnp.bfloat16)[None]
    grad_value = summed[:, 1].reshape(k_rows, row_width).astype(jnp.bfloat16)[None]
    grad_query = dq_final.reshape(q_rows, row_width).astype(jnp.bfloat16)[None]
    return (grad_query, grad_key, grad_value)


def solution(mesh):
    return jax.shard_map(
        shards,
        mesh=mesh,
        in_specs=(
            P(("grp", "dp"), "seq", None),
            P(("grp", "dp"), "seq", None),
            P(("grp", "dp"), "seq", None),
            P(("grp", "dp"), "seq", None),
            P(("grp", "dp"), "seq", None),
            P(("grp", "dp"), None),
            P(("grp", "dp"), None),
        ),
        out_specs=(
            P(("grp", "dp"), "seq", None),
            P(("grp", "dp"), "seq", None),
            P(("grp", "dp"), "seq", None),
        ),
        check_vma=False,
    )
```

profile of v0, /device:TPU:16, one launch (start us, length us, event | category | flops | bytes accessed | tf_op | source)
XLA Modules:
  0.0 241.4 jit_solution(860510484492957975)
XLA Ops:
  0.6 2.9 %copy.35 = bf16[1,512,2048]{1,2,0:T(8,128)(2,1)S(1)} copy(bf16[1,512,2048]{2,1,0:T(8,128)(2,1)} %param.12) | data formatting | bytes 4194304 | tf_op args[1]
  3.5 4.6 %copy.36 = bf16[1,512,2048]{1,2,0:T(8,128)(2,1)} copy(bf16[1,512,2048]{2,1,0:T(8,128)(2,1)} %param.13) | data formatting | bytes 4194304 | tf_op args[2]
  8.1 2.9 %pad_maximum_fusion.2 = (bf16[2,128,2048]{1,2,0:T(8,128)(2,1)}, bf16[2,128,2048]{1,2,0:T(8,128)(2,1)}) fusion(bf16[1,512,2048]{1,2,0:T(8,128)(2,1)} %copy.36, bf16[1,512,2048]{1,2,0:T(8,128)(2,1)S(1)} %copy.35), kind=kLoop, calls=%fused_computation.27 | loop fusion | flops 4194304 | bytes 6291456 | tf_op jit(solution)/shard_map/slice | solution.py:19
  11.0 3.5 %collective-permute-start = (bf16[2,128,2048]{1,2,0:T(8,128)(2,1)}, bf16[2,128,2048]{1,2,0:T(8,128)(2,1)}, u32[]{:S(2)}, u32[]{:S(2)}) collective-permute-start(bf16[2,128,2048]{1,2,0:T(8,128)(2,1)} %get-tuple-element.223), channel_id=1, source_target_pairs={{0,2},{2,4},{4,6},{6,8},{8,10},{10,12},{12,14},{1,3},{3,5},{5,7},{... | collective-permute-start | bytes 3145736 | tf_op jit(solution)/shard_map/ppermute | solution.py:22
  14.6 3.3 %collective-permute-start.1 = (bf16[2,128,2048]{1,2,0:T(8,128)(2,1)}, bf16[2,128,2048]{1,2,0:T(8,128)(2,1)}, u32[]{:S(2)}, u32[]{:S(2)}) collective-permute-start(bf16[2,128,2048]{1,2,0:T(8,128)(2,1)} %get-tuple-element.224), channel_id=1, source_target_pairs={{2,0},{4,2},{6,4},{8,6},{10,8},{12,10},{14,12},{3,1},{5,3},{7,5},{... | collective-permute-start | bytes 3145736 | tf_op jit(solution)/shard_map/ppermute | solution.py:24
  18.6 1.2 copy.39
  20.3 39.4 %collective-permute-done = bf16[2,128,2048]{1,2,0:T(8,128)(2,1)} collective-permute-done((bf16[2,128,2048]{1,2,0:T(8,128)(2,1)}, bf16[2,128,2048]{1,2,0:T(8,128)(2,1)}, u32[]{:S(2)}, u32[]{:S(2)}) %collective-permute-start) | collective-permute-done | bytes 1048608 | tf_op jit(solution)/shard_map/ppermute | solution.py:22
  59.7 1.9 collective-permute-done.1
  61.6 6.4 %pad_maximum_fusion = bf16[2,768,2048]{1,2,0:T(8,128)(2,1)} fusion(bf16[2,128,2048]{1,2,0:T(8,128)(2,1)} %collective-permute-done.1, bf16[1,512,2048]{1,2,0:T(8,128)(2,1)} %copy.36, bf16[1,512,2048]{1,2,0:T(8,128)(2,1)} %copy-done, bf16[2,128,2048]{1,2,0:T(8,128)(2,1)} %collective-permute-done), kind=kLoop, calls=%fused_computation.24 | loop fusion | flops 25165824 | bytes 12582912 | tf_op jit(solution)/shard_map/concatenate | solution.py:20
  68.0 27.7 %while.26 = (s32[]{:T(128)}, f32[32,128]{1,0:T(8,128)S(1)}, f32[32,128]{1,0:T(8,128)S(1)}, s32[128]{0:T(128)S(1)}, s32[6]{0:T(128)S(1)}, /*index=5*/s32[768]{0:T...) while((s32[]{:T(128)}, f32[32,128]{1,0:T(8,128)S(1)}, ...), condition=%wide.region_5.6_spmd.clone, body=%wide.region_2.0_spmd.clone.sunk | while | flops 70291464 | bytes 12847306 | solution.py:92
  69.4 2.1 slice.68
  72.6 0.6 dynamic_slice.39
  74.0 2.1 slice.68
  77.2 0.6 dynamic_slice.39
  78.7 2.1 slice.68
  81.9 0.6 dynamic_slice.39
  83.3 2.1 slice.68
  86.5 0.6 dynamic_slice.39
  87.9 2.1 slice.68
  91.1 0.6 dynamic_slice.39
  92.5 2.1 slice.68
  95.7 57.7 %while.27 = (s32[]{:T(128)}, f32[128,32,64]{0,2,1:T(8,128)S(1)}, f32[6,2,128,2048]{2,3,1,0:T(8,128)}, bf16[2,768,2048]{1,2,0:T(8,128)(2,1)}, s32[6]{0:T(128)S(1)...) while((s32[]{:T(128)}, f32[128,32,64]{0,2,1:T(8,128)S(1)}, ...), condition=%wide.region_8.9_spmd.clone, body=%wide.region_7.8_spmd.clone.sunk | while | flops 340279296 | bytes 36243684 | solution.py:120
  95.7 0.6 dynamic_slice.42
  97.1 3.3 %fusion.59 = (bf16[1,768,2048]{1,2,0:T(8,128)(2,1)S(1)}, bf16[1,768,2048]{1,2,0:T(8,128)(2,1)S(1)}) fusion(bf16[2,768,2048]{1,2,0:T(8,128)(2,1)} %get-tuple-element.422), kind=kLoop, calls=%fused_computation.38.clone.1 | loop fusion | bytes 12582912 | tf_op jit(solution)/shard_map/while/body/eval_jaxpr/slice | solution.py:71
  100.5 0.7 fusion.60
  101.7 0.8 fusion.63
  103.1 0.8 fusion.64
  103.9 1.5 fusion.65
  106.8 3.3 %fusion.59 = (bf16[1,768,2048]{1,2,0:T(8,128)(2,1)S(1)}, bf16[1,768,2048]{1,2,0:T(8,128)(2,1)S(1)}) fusion(bf16[2,768,2048]{1,2,0:T(8,128)(2,1)} %get-tuple-element.422), kind=kLoop, calls=%fused_computation.38.clone.1 | loop fusion | bytes 12582912 | tf_op jit(solution)/shard_map/while/body/eval_jaxpr/slice | solution.py:71
  110.1 0.7 fusion.60
  111.3 0.8 fusion.63
  112.7 0.8 fusion.64
  113.5 1.4 fusion.65
  116.3 3.3 %fusion.59 = (bf16[1,768,2048]{1,2,0:T(8,128)(2,1)S(1)}, bf16[1,768,2048]{1,2,0:T(8,128)(2,1)S(1)}) fusion(bf16[2,768,2048]{1,2,0:T(8,128)(2,1)} %get-tuple-element.422), kind=kLoop, calls=%fused_computation.38.clone.1 | loop fusion | bytes 12582912 | tf_op jit(solution)/shard_map/while/body/eval_jaxpr/slice | solution.py:71
  119.7 0.7 fusion.60
  120.9 0.8 fusion.63
  122.3 0.8 fusion.64
  123.1 1.5 fusion.65
  126.0 3.3 %fusion.59 = (bf16[1,768,2048]{1,2,0:T(8,128)(2,1)S(1)}, bf16[1,768,2048]{1,2,0:T(8,128)(2,1)S(1)}) fusion(bf16[2,768,2048]{1,2,0:T(8,128)(2,1)} %get-tuple-element.422), kind=kLoop, calls=%fused_computation.38.clone.1 | loop fusion | bytes 12582912 | tf_op jit(solution)/shard_map/while/body/eval_jaxpr/slice | solution.py:71
  129.3 0.7 fusion.60
  130.5 0.8 fusion.63
  131.9 0.8 fusion.64
  132.7 1.5 fusion.65
  135.6 3.3 %fusion.59 = (bf16[1,768,2048]{1,2,0:T(8,128)(2,1)S(1)}, bf16[1,768,2048]{1,2,0:T(8,128)(2,1)S(1)}) fusion(bf16[2,768,2048]{1,2,0:T(8,128)(2,1)} %get-tuple-element.422), kind=kLoop, calls=%fused_computation.38.clone.1 | loop fusion | bytes 12582912 | tf_op jit(solution)/shard_map/while/body/eval_jaxpr/slice | solution.py:71
  138.9 0.7 fusion.60
  140.1 0.8 fusion.63
  141.5 0.8 fusion.64
  142.3 1.5 fusion.65
  145.2 3.3 %fusion.59 = (bf16[1,768,2048]{1,2,0:T(8,128)(2,1)S(1)}, bf16[1,768,2048]{1,2,0:T(8,128)(2,1)S(1)}) fusion(bf16[2,768,2048]{1,2,0:T(8,128)(2,1)} %get-tuple-element.422), kind=kLoop, calls=%fused_computation.38.clone.1 | loop fusion | bytes 12582912 | tf_op jit(solution)/shard_map/while/body/eval_jaxpr/slice | solution.py:71
  148.6 0.7 fusion.60
  149.8 0.8 fusion.63
  151.1 0.8 fusion.64
  151.9 1.5 fusion.65
  153.4 3.0 %slice.47 = f32[1,2,128,2048]{2,3,1,0:T(8,128)} slice(f32[6,2,128,2048]{2,3,1,0:T(8,128)} %get-tuple-element.107), slice={[0:1], [0:2], [0:128], [0:2048]} | slice | bytes 4194304 | tf_op jit(solution)/shard_map/slice | solution.py:123
  156.4 2.4 %collective-permute-start.3 = (f32[1,2,128,2048]{2,3,1,0:T(8,128)}, f32[1,2,128,2048]{2,3,1,0:T(8,128)}, u32[]{:S(2)}, u32[]{:S(2)}) collective-permute-start(f32[1,2,128,2048]{2,3,1,0:T(8,128)} %slice.47), channel_id=1, source_target_pairs={{2,0},{4,2},{6,4},{8,6},{10,8},{12,10},{14,12},{3,1},{5,3},{7,5},{... | collective-permute-start | bytes 6291464 | tf_op jit(solution)/shard_map/ppermute | solution.py:34
  158.9 1.7 slice.60
  160.6 3.4 %collective-permute-start.2 = (bf16[1,2,128,2048]{2,3,1,0:T(8,128)(2,1)S(1)}, bf16[1,2,128,2048]{2,3,1,0:T(8,128)(2,1)}, u32[]{:S(2)}, u32[]{:S(2)}) collective-permute-start(bf16[1,2,128,2048]{2,3,1,0:T(8,128)(2,1)S(1)} %slice.60), channel_id=1, source_target_pairs={{0,2},{2,4},{4,6},{6,8},{8,10},{10,12},{12,14},{1,3},{3,5},{5,7},{... | collective-permute-start | bytes 3145736 | tf_op jit(solution)/shard_map/ppermute | solution.py:34
  164.1 1.0 copy.42
  165.1 62.3 %collective-permute-done.2 = bf16[1,2,128,2048]{2,3,1,0:T(8,128)(2,1)} collective-permute-done((bf16[1,2,128,2048]{2,3,1,0:T(8,128)(2,1)S(1)}, bf16[1,2,128,2048]{2,3,1,0:T(8,128)(2,1)}, u32[]{:S(2)}, u32[]{:S(2)}) %collective-permute-start.2) | collective-permute-done | bytes 1048608 | tf_op jit(solution)/shard_map/ppermute | solution.py:34
  227.4 1.3 collective-permute-done.3
  228.7 4.6 %add_convert_fusion = bf16[4,2,128,2048]{2,3,1,0:T(8,128)(2,1)S(1)} fusion(f32[1,2,128,2048]{2,3,1,0:T(8,128)} %collective-permute-done.3, f32[6,2,128,2048]{2,3,1,0:T(8,128)} %get-tuple-element.107, bf16[1,2,128,2048]{2,3,1,0:T(8,128)(2,1)} %collective-permute-done.2), kind=kLoop, calls=%fused_computation.23 | loop fusion | flops 8388608 | bytes 15728640 | tf_op jit(solution)/shard_map/convert.4
  233.3 1.6 fusion.11
  234.9 3.9 %copy.41 = bf16[4,1,128,2048]{3,2,0,1:T(8,128)(2,1)} copy(bf16[4,1,128,2048]{2,3,1,0:T(8,128)(2,1)} %get-tuple-element.221) | data formatting | bytes 4194304 | tf_op jit(solution)/shard_map/slice | solution.py:135
  238.8 2.6 %copy.40 = bf16[4,1,128,2048]{3,2,0,1:T(8,128)(2,1)} copy(bf16[4,1,128,2048]{2,3,1,0:T(8,128)(2,1)S(1)} %get-tuple-element.222) | data formatting | bytes 4194304 | tf_op jit(solution)/shard_map/slice | solution.py:134
  (113 shorter events, 19.9 us)
Async XLA Ops:
  3.5 4.6 %copy-start = (bf16[1,512,2048]{1,2,0:T(8,128)(2,1)}, bf16[1,512,2048]{1,2,0:T(8,128)(2,1)S(1)}, u32[]{:S(2)}) copy-start(bf16[1,512,2048]{1,2,0:T(8,128)(2,1)S(1)} %copy.35) | copy-start | bytes 6291460
  8.1 9.8 %copy-start.3 = (s32[1,33]{1,0:T(1,128)S(1)}, s32[1,33]{1,0:T(1,128)}, u32[]{:S(2)}) copy-start(s32[1,33]{1,0:T(1,128)} %param.16) | copy-start | bytes 400
  8.1 9.9 %copy-start.1 = (bf16[1,128,2048]{2,1,0:T(8,128)(2,1)S(1)}, bf16[1,128,2048]{2,1,0:T(8,128)(2,1)}, u32[]{:S(2)}) copy-start(bf16[1,128,2048]{2,1,0:T(8,128)(2,1)} %param.11) | copy-start | bytes 1572868
  8.1 10.2 %copy-start.2 = (bf16[1,128,2048]{2,1,0:T(8,128)(2,1)S(1)}, bf16[1,128,2048]{2,1,0:T(8,128)(2,1)}, u32[]{:S(2)}) copy-start(bf16[1,128,2048]{2,1,0:T(8,128)(2,1)} %param.15) | copy-start | bytes 1572868
  11.0 8.9 %copy-start.4 = (s32[1,33]{1,0:T(1,128)S(1)}, s32[1,33]{1,0:T(1,128)}, u32[]{:S(2)}) copy-start(s32[1,33]{1,0:T(1,128)} %param.17) | copy-start | bytes 400
  11.0 48.7 %collective-permute-start = (bf16[2,128,2048]{1,2,0:T(8,128)(2,1)}, bf16[2,128,2048]{1,2,0:T(8,128)(2,1)}, u32[]{:S(2)}, u32[]{:S(2)}) collective-permute-start(bf16[2,128,2048]{1,2,0:T(8,128)(2,1)} %get-tuple-element.223), channel_id=1, source_target_pairs={{0,2},{2,4},{4,6},{6,8},{8,10},{10,12},{12,14},{1,3},{3,5},{5,7},{... | collective-permute-start | bytes 3145736 | tf_op jit(solution)/shard_map/ppermute | solution.py:22
  14.6 47.0 %collective-permute-start.1 = (bf16[2,128,2048]{1,2,0:T(8,128)(2,1)}, bf16[2,128,2048]{1,2,0:T(8,128)(2,1)}, u32[]{:S(2)}, u32[]{:S(2)}) collective-permute-start(bf16[2,128,2048]{1,2,0:T(8,128)(2,1)} %get-tuple-element.224), channel_id=1, source_target_pairs={{2,0},{4,2},{6,4},{8,6},{10,8},{12,10},{14,12},{3,1},{5,3},{7,5},{... | collective-permute-start | bytes 3145736 | tf_op jit(solution)/shard_map/ppermute | solution.py:24
  156.4 72.2 %collective-permute-start.3 = (f32[1,2,128,2048]{2,3,1,0:T(8,128)}, f32[1,2,128,2048]{2,3,1,0:T(8,128)}, u32[]{:S(2)}, u32[]{:S(2)}) collective-permute-start(f32[1,2,128,2048]{2,3,1,0:T(8,128)} %slice.47), channel_id=1, source_target_pairs={{2,0},{4,2},{6,4},{8,6},{10,8},{12,10},{14,12},{3,1},{5,3},{7,5},{... | collective-permute-start | bytes 6291464 | tf_op jit(solution)/shard_map/ppermute | solution.py:34
  160.6 66.8 %collective-permute-start.2 = (bf16[1,2,128,2048]{2,3,1,0:T(8,128)(2,1)S(1)}, bf16[1,2,128,2048]{2,3,1,0:T(8,128)(2,1)}, u32[]{:S(2)}, u32[]{:S(2)}) collective-permute-start(bf16[1,2,128,2048]{2,3,1,0:T(8,128)(2,1)S(1)} %slice.60), channel_id=1, source_target_pairs={{0,2},{2,4},{4,6},{6,8},{8,10},{10,12},{12,14},{1,3},{3,5},{5,7},{... | collective-permute-start | bytes 3145736 | tf_op jit(solution)/shard_map/ppermute | solution.py:34
where the time goes:
time: 243 us; the launch traced here: 241 us
  waiting for transfers between devices  105 us (43%)
  local copies, waits for them, and re-layouts  64.1 us (26%)
  other arithmetic  27.2 us (11%)
  matrix products  23.2 us (10%)
  starting transfers between devices  12.7 us (5%)
  loops' own time  8.55 us (4%)
    ppermute x2, waiting for transfers between devices, from_behind(): return lax.ppermute(shard, axis, pairs)  63.5 us
    ppermute x1, waiting for transfers between devices, extended(): lax.ppermute(tail, axis, [(i, (i + 1) % count) for i in range(ends)])  39.4 us
    slice x6, local copies, waits for them, and re-layouts, key_block(): window[1]  19.5 us
    slice x6, local copies, waits for them, and re-layouts, key_block(): window[0]  12.6 us
    unnamed x15, local copies, waits for them, and re-layouts  9.03 us
    dynamic_update_slice x6, other arithmetic, shards(): lax.scan(grad_step, start_query, jnp.arange(n_blocks, dtype=jnp.int32))  8.86 us
    dynamic_slice x12, local copies, waits for them, and re-layouts, shards(): lax.scan(stats_step, start_stats, jnp.arange(n_blocks, dtype=jnp.int32))  7.01 us
    concatenate x1, other arithmetic, extended(): jnp.concatenate([lax.ppermute(tail, axis, [(i, (i + 1) % count) for i in...  6.41 us
  transfers between devices with their start and end apart: 4, of which 4 were waited for; matrix products, arithmetic and copies ran while one was open for 2% of the time, Pallas kernels for 0%

commit v1 on v0

v1 whole, which is shorter than its diff:
```python
import functools

import jax
import jax.numpy as jnp
from jax import lax
from jax.experimental import pallas as pl
from jax.experimental.pallas import tpu as pltpu
from jax.sharding import PartitionSpec as P

H = 32
HD = 64
LANES = 256
PER = LANES // HD

low = -1e30
high = 1e30


def dot_nt(a, b):
    return lax.dot_general(a, b, (((1,), (1,)), ((), ())), preferred_element_type=jnp.float32)


def dot_nn(a, b):
    return lax.dot_general(a, b, (((1,), (0,)), ((), ())), preferred_element_type=jnp.float32)


def dot_tn(a, b):
    return lax.dot_general(a, b, (((0,), (0,)), ((), ())), preferred_element_type=jnp.float32)


def spread(rows):
    head = lax.broadcasted_iota(jnp.int32, rows.shape, 1) // HD
    return jnp.concatenate([jnp.where(head == h, rows, jnp.zeros_like(rows)) for h in range(PER)], axis=0)


def gather_heads(full):
    slots = full.shape[0] // PER
    head = lax.broadcasted_iota(jnp.int32, (slots, full.shape[1]), 1) // HD
    out = full[:slots]
    for h in range(1, PER):
        out = jnp.where(head == h, full[h * slots : (h + 1) * slots], out)
    return out


def slot_of(slots):
    return lax.rem(lax.broadcasted_iota(jnp.int32, (1, PER * slots), 1), slots)


def row_dots(outs, spread_grads):
    slots = outs.shape[0]
    full = dot_nt(outs, spread_grads)
    row = lax.broadcasted_iota(jnp.int32, full.shape, 0)
    lane = lax.rem(lax.broadcasted_iota(jnp.int32, full.shape, 1), slots)
    return jnp.sum(jnp.where(row == lane, full, 0.0), axis=0, keepdims=True)


def log_add(a, b):
    top = jnp.maximum(a, b)
    return top + jnp.log(jnp.exp(a - top) + jnp.exp(b - top))


def row_ids(rows, lanes):
    return lax.broadcasted_iota(jnp.int32, (rows, lanes), 0)


def interior_kernel(n_ex, gq, gk, start_ref, q_ref, o_ref, g_ref, k_ref, v_ref, dq_ref, dk_ref, dv_ref, dqe_ref, dke_ref, dve_ref):
    slots = 2 * gq
    win = gk + gk // 2
    slot = slot_of(slots)
    for c in range(q_ref.shape[1] // LANES):
        cols = slice(c * LANES, (c + 1) * LANES)
        parts = []
        for i in range(n_ex - 1):
            q0, k0 = i * gq, i * gk
            d_lo, d_hi = start_ref[0, i] - q0, start_ref[0, i + 1] - q0
            e_lo, e_hi = start_ref[1, i] - k0, start_ref[1, i + 1] - k0
            keys = k_ref[k0 : k0 + win, cols]
            vals = v_ref[k0 : k0 + win, cols]
            qs = spread(q_ref[q0 : q0 + slots, cols])
            gs = spread(g_ref[q0 : q0 + slots, cols])
            s = dot_nt(keys, qs)
            row = row_ids(win, LANES)
            s = jnp.where((row >= e_lo) & (row < e_hi), s, low)
            top = jnp.max(s, axis=0, keepdims=True)
            e = jnp.exp(s - top)
            total = jnp.sum(e, axis=0, keepdims=True)
            inv = jnp.where((slot >= d_lo) & (slot < d_hi), 1.0 / total, 0.0)
            p = e * inv
            dots = row_dots(o_ref[q0 : q0 + slots, cols], gs)
            dp = dot_nt(vals, gs)
            ds = (p * (dp - dots)).astype(jnp.bfloat16)
            dv = dot_nn(p.astype(jnp.bfloat16), gs)
            dk = dot_nn(ds, qs)
            dq = gather_heads(dot_tn(ds, keys))
            parts.append((dq, dk, dv))
        edge = gk // 2
        for which, (ref, ext) in enumerate(((dk_ref, dke_ref), (dv_ref, dve_ref))):
            for i in range(n_ex - 1):
                part = parts[i][1 + which]
                first = part[:edge]
                if i > 0:
                    first = first + parts[i - 1][1 + which][gk:]
                first = first.astype(ref.dtype)
                ref[i * gk : i * gk + edge, cols] = first
                ref[i * gk + edge : (i + 1) * gk, cols] = part[edge:gk].astype(ref.dtype)
                if i == 0:
                    ext[:edge, cols] = first
            tail = parts[n_ex - 2][1 + which][gk:].astype(ref.dtype)
            ext[edge : 2 * edge, cols] = tail
        for i in range(n_ex):
            piece = None
            if i < n_ex - 1:
                piece = parts[i][0][:gq]
            if i > 0:
                other = parts[i - 1][0][gq:]
                piece = other if piece is None else piece + other
            piece = piece.astype(dq_ref.dtype)
            dq_ref[i * gq : (i + 1) * gq, cols] = piece
            if i == 0:
                dqe_ref[:gq, cols] = piece
            if i == n_ex - 1:
                dqe_ref[gq:, cols] = piece


def own_scores(keys_a, keys_b, qs, start_ref, n_ex, gq, gk, swap):
    slots = 2 * gq
    sa = dot_nt(keys_a, qs)
    sb = dot_nt(keys_b, qs)
    slot_a = lax.rem(lax.broadcasted_iota(jnp.int32, sa.shape, 1), slots)
    slot_b = lax.rem(lax.broadcasted_iota(jnp.int32, sb.shape, 1), slots)
    in_a = slot_a >= gq if swap else slot_a < gq
    in_b = slot_b < gq if swap else slot_b >= gq
    a_lo = start_ref[1, n_ex - 1] - (n_ex - 1) * gk
    b_hi = start_ref[1, 0]
    sa = jnp.where(in_a & (row_ids(*sa.shape) >= a_lo), sa, low)
    sb = jnp.where(in_b & (row_ids(*sb.shape) < b_hi), sb, low)
    return sa, sb


def log_sum(sa, sb):
    top = jnp.maximum(jnp.max(sa, axis=0, keepdims=True), jnp.max(sb, axis=0, keepdims=True))
    total = jnp.sum(jnp.exp(sa - top), axis=0, keepdims=True) + jnp.sum(jnp.exp(sb - top), axis=0, keepdims=True)
    return top + jnp.log(total)


def stats_kernel(n_ex, gq, gk, start_ref, qa_ref, qb_ref, oa_ref, ob_ref, ga_ref, gb_ref, ka_ref, kb_ref, stat_ref):
    for c in range(qa_ref.shape[1] // LANES):
        cols = slice(c * LANES, (c + 1) * LANES)
        qs = spread(jnp.concatenate([qa_ref[:, cols], qb_ref[:, cols]], axis=0))
        gs = spread(jnp.concatenate([ga_ref[:, cols], gb_ref[:, cols]], axis=0))
        sa, sb = own_scores(ka_ref[:, cols], kb_ref[:, cols], qs, start_ref, n_ex, gq, gk, False)
        stat_ref[0:1, cols] = log_sum(sa, sb)
        stat_ref[1:2, cols] = row_dots(jnp.concatenate([oa_ref[:, cols], ob_ref[:, cols]], axis=0), gs)


def pick(flag, a, b):
    return jnp.where(flag, a, b)


def remote_kernel(n_ex, gq, gk, start_ref, re_ref, ro_ref, te_ref, to_ref, ka_ref, kb_ref, va_ref, vb_ref, me_ref, mo_ref, stat_ref):
    slots = 2 * gq
    even = start_ref[0, n_ex + 1] == 0
    slot = slot_of(slots)
    for c in range(re_ref.shape[1] // LANES):
        cols = slice(c * LANES, (c + 1) * LANES)
        re, ro = re_ref[:, cols], ro_ref[:, cols]
        before, after = pick(even, ro, re), pick(even, re, ro)
        te, to = te_ref[:, cols], to_ref[:, cols]
        tbefore, tafter = pick(even, to, te), pick(even, te, to)
        stat = jnp.where(slot < gq, tbefore, tafter)
        qs = spread(jnp.concatenate([before[:gq], after[:gq]], axis=0))
        gs = spread(jnp.concatenate([before[gq:], after[gq:]], axis=0))
        keys_a, keys_b = ka_ref[:, cols], kb_ref[:, cols]
        sa, sb = own_scores(keys_a, keys_b, qs, start_ref, n_ex, gq, gk, True)
        mine = log_sum(sa, sb)
        d_lo = start_ref[0, n_ex + 2]
        d_hi = start_ref[0, n_ex] - n_ex * gq + gq
        whole = jnp.where((slot >= d_lo) & (slot < d_hi), log_add(mine, stat[0:1]), high)
        dots = stat[1:2]
        dsa = (jnp.exp(sa - whole) * (dot_nt(va_ref[:, cols], gs) - dots)).astype(jnp.bfloat16)
        dsb = (jnp.exp(sb - whole) * (dot_nt(vb_ref[:, cols], gs) - dots)).astype(jnp.bfloat16)
        dq = gather_heads(dot_tn(dsa, keys_a) + dot_tn(dsb, keys_b)).astype(jnp.bfloat16)
        hi = mine.astype(jnp.bfloat16)
        rest = mine - hi.astype(jnp.float32)
        mid = rest.astype(jnp.bfloat16)
        tail = (rest - mid.astype(jnp.float32)).astype(jnp.bfloat16)
        three = lax.broadcasted_iota(jnp.int32, (16, LANES), 0)
        logs = jnp.where(
            three == 0, hi.astype(jnp.float32), jnp.where(three == 1, mid.astype(jnp.float32), tail.astype(jnp.float32))
        ).astype(jnp.bfloat16)
        to_before, to_after = dq[:gq], dq[gq:]
        me_ref[:gq, cols] = pick(even, to_after, to_before)
        mo_ref[:gq, cols] = pick(even, to_before, to_after)
        me_ref[gq:, cols] = logs
        mo_ref[gq:, cols] = logs
        stat_ref[0:1, cols] = whole
        stat_ref[1:2, cols] = dots


def edge_kernel(
    n_ex, gq, gk, start_ref, re_ref, ro_ref, me_ref, mo_ref, own_ref, far_ref, qa_ref, qb_ref, ga_ref, gb_ref,
    ka_ref, kb_ref, va_ref, vb_ref, dqe_ref, dke_ref, dve_ref, dq_in, dk_in, dv_in, dq_out, dk_out, dv_out,
    dq_buf, dk_buf, dv_buf, sems,
):
    slots = 2 * gq
    edge = gk // 2
    even = start_ref[0, n_ex + 1] == 0
    has_next = start_ref[1, n_ex + 1] == 1
    slot = slot_of(slots)
    width = re_ref.shape[1]
    step = pl.program_id(0)
    for c in range(width // LANES):
        cols = slice(c * LANES, (c + 1) * LANES)
        re, ro = re_ref[:, cols], ro_ref[:, cols]
        before, after = pick(even, ro, re), pick(even, re, ro)
        me, mo = me_ref[:, cols].astype(jnp.float32), mo_ref[:, cols].astype(jnp.float32)
        mbefore, mafter = pick(even, mo, me), pick(even, me, mo)
        log_before = mbefore[gq : gq + 1] + mbefore[gq + 1 : gq + 2] + mbefore[gq + 2 : gq + 3]
        log_after = mafter[gq : gq + 1] + mafter[gq + 1 : gq + 2] + mafter[gq + 2 : gq + 3]
        log_after = jnp.where(has_next, log_after, low)
        own = log_add(own_ref[0:1, cols], jnp.where(slot < gq, log_after, log_before))
        a_lo = start_ref[0, n_ex - 1] - (n_ex - 1) * gq
        b_hi = start_ref[0, 0] + gq
        own = jnp.where((slot >= a_lo) & (slot < b_hi), own, high)
        far = far_ref[0:1, cols]
        own_d, far_d = own_ref[1:2, cols], far_ref[1:2, cols]
        qa, qb, ga, gb = qa_ref[:, cols], qb_ref[:, cols], ga_ref[:, cols], gb_ref[:, cols]
        sides = (
            (qa, after[:gq], ga, after[gq:], ka_ref, va_ref, own, far, own_d, far_d),
            (before[:gq], qb, before[gq:], gb, kb_ref, vb_ref, far, own, far_d, own_d),
        )
        done = []
        for side, (q_1, q_2, g_1, g_2, k_ref, v_ref, log_1, log_2, d_1, d_2) in enumerate(sides):
            qs = spread(jnp.concatenate([q_1, q_2], axis=0))
            gs = spread(jnp.concatenate([g_1, g_2], axis=0))
            whole = jnp.where(slot < gq, log_1, log_2)
            dots = jnp.where(slot < gq, d_1, d_2)
            keys = k_ref[:, cols]
            s = dot_nt(keys, qs)
            row = row_ids(*s.shape)
            if side == 0:
                s = jnp.where(row >= start_ref[1, n_ex - 1] - (n_ex - 1) * gk, s, low)
            else:
                s = jnp.where(row < start_ref[1, 0], s, low)
            p = jnp.exp(s - whole)
            ds = (p * (dot_nt(v_ref[:, cols], gs) - dots)).astype(jnp.bfloat16)
            dv = dot_nn(p.astype(jnp.bfloat16), gs)
            dk = dot_nn(ds, qs)
            dq = gather_heads(dot_tn(ds, keys))
            done.append((dq, dk, dv))
        wide = pl.ds(pl.multiple_of(step * width, width) + c * LANES, LANES)
        f32 = jnp.float32
        for which, (buf, ext) in enumerate(((dk_buf, dke_ref), (dv_buf, dve_ref))):
            part_r, part_l = done[0][1 + which], done[1][1 + which]
            buf[:edge, wide] = (part_l + ext[:edge, cols].astype(f32)).astype(buf.dtype)
            buf[edge : 2 * edge, wide] = (part_r[:edge] + ext[edge:, cols].astype(f32)).astype(buf.dtype)
            buf[2 * edge :, wide] = part_r[edge:].astype(buf.dtype)
        dq_a = done[0][0][:gq] + mafter[:gq] + dqe_ref[gq:, cols].astype(f32)
        half = gq // 2
        dq_b = done[1][0][gq:] + mbefore[:gq] + dqe_ref[:gq, cols].astype(f32)
        dq_buf[:gq, wide] = dq_b.astype(dq_buf.dtype)
        dq_buf[gq:, wide] = dq_a.astype(dq_buf.dtype)

    def copies(at):
        cols = pl.ds(pl.multiple_of(at * width, width), width)
        last = (n_ex - 1) * gk
        out = []
        for j, (buf, ref) in enumerate(((dk_buf, dk_out), (dv_buf, dv_out))):
            out.append(pltpu.make_async_copy(buf.at[pl.ds(0, edge), cols], ref.at[pl.ds(0, edge), cols], sems.at[at, 2 * j]))
            out.append(pltpu.make_async_copy(buf.at[pl.ds(edge, gk), cols], ref.at[pl.ds(last, gk), cols], sems.at[at, 2 * j + 1]))
        out.append(pltpu.make_async_copy(dq_buf.at[pl.ds(0, gq), cols], dq_out.at[pl.ds(0, gq), cols], sems.at[at, 4]))
        out.append(pltpu.make_async_copy(dq_buf.at[pl.ds(gq, gq), cols], dq_out.at[pl.ds((n_ex - 1) * gq, gq), cols], sems.at[at, 5]))
        return out

    for copy in copies(step):
        copy.start()

    @pl.when(step == pl.num_programs(0) - 1)
    def _():
        for at in range(dk_buf.shape[1] // width):
            for copy in copies(at):
                copy.wait()


def call(kernel, steps, width, ins, outs, scratch=(), aliases=None, flops=0, nbytes=0):
    def spec(entry):
        if entry is None:
            return pl.BlockSpec(memory_space=pl.ANY)
        rows, index = entry
        return pl.BlockSpec((rows, width), lambda g, s, index=index: (index, g))

    return pl.pallas_call(
        kernel,
        out_shape=[shape for _, shape in outs],
        grid_spec=pltpu.PrefetchScalarGridSpec(
            num_scalar_prefetch=1,
            grid=(steps,),
            in_specs=[spec(entry) for entry in ins],
            out_specs=[spec(entry) for entry, _ in outs],
            scratch_shapes=list(scratch),
        ),
        input_output_aliases=aliases or {},
        compiler_params=pltpu.CompilerParams(dimension_semantics=("arbitrary",), vmem_limit_bytes=40 * 1024 * 1024),
        cost_estimate=pl.CostEstimate(flops=flops, bytes_accessed=nbytes, transcendentals=0),
    )


def shards(dec_query, enc_key, enc_value, saved_out, d_out, dec_start, enc_start):
    q, k, v, o, g = dec_query[0], enc_key[0], enc_value[0], saved_out[0], d_out[0]
    q_rows, feats = q.shape
    k_rows = k.shape[0]
    pos = lax.axis_index("seq")
    count = lax.axis_size("seq")
    n_ex = (dec_start.shape[1] - 1) // count
    gq, gk = q_rows // n_ex, k_rows // n_ex
    edge = gk // 2
    even = lax.rem(pos, 2) == 0
    bf16, f32 = jnp.bfloat16, jnp.float32

    def swap_even(x):
        return lax.ppermute(x, "seq", [(i, i ^ 1) for i in range(count) if i ^ 1 < count])

    def swap_odd(x):
        pairs = []
        for i in range(1, count - 1, 2):
            pairs += [(i, i + 1), (i + 1, i)]
        return lax.ppermute(x, "seq", pairs)

    starts = jnp.concatenate([dec_start, enc_start], axis=0)
    rows = jnp.array([q_rows, k_rows], jnp.int32)
    near = lax.dynamic_slice(starts, (0, pos * n_ex), (2, n_ex + 1)) - pos * rows[:, None]
    prior = lax.dynamic_slice(starts, (0, jnp.maximum(pos * n_ex - 1, 0)), (1, 1))[0, 0] - pos * q_rows + gq
    prior = jnp.where(pos > 0, prior, gq)
    extra = jnp.stack([lax.rem(pos, 2), prior, (pos < count - 1).astype(jnp.int32), jnp.int32(0)]).reshape(2, 2)
    table = jnp.concatenate([near, extra.astype(jnp.int32)], axis=1)

    last = (n_ex - 1) * gq
    at_e, at_o = jnp.where(even, last, 0), jnp.where(even, 0, last)

    def message(at):
        return jnp.concatenate([lax.dynamic_slice(q, (at, 0), (gq, feats)), lax.dynamic_slice(g, (at, 0), (gq, feats))], axis=0)

    raw_e = swap_even(message(at_e))
    raw_o = swap_odd(message(at_o))

    width = 512
    steps = feats // width
    stat_shape = jax.ShapeDtypeStruct((2, feats), f32)
    a_q, b_q = (gq, n_ex - 1), (gq, 0)
    a_k, b_k = (gk, n_ex - 1), (edge, 0)
    (own,) = call(
        functools.partial(stats_kernel, n_ex, gq, gk), steps, width,
        [a_q, b_q, a_q, b_q, a_q, b_q, a_k, b_k],
        [((2, 0), stat_shape)], flops=int(4e8), nbytes=int(2e6),
    )(table, q, q, o, o, g, g, k, k)
    stat_e = swap_even(own)
    stat_o = swap_odd(own)

    msg_shape = jax.ShapeDtypeStruct((gq + 16, feats), bf16)
    raw = (2 * gq, 0)
    stat = (2, 0)
    msg = (gq + 16, 0)
    to_e, to_o, far = call(
        functools.partial(remote_kernel, n_ex, gq, gk), steps, width,
        [raw, raw, stat, stat, a_k, b_k, a_k, b_k],
        [(msg, msg_shape), (msg, msg_shape), (stat, stat_shape)], flops=int(8e8), nbytes=int(3e6),
    )(table, raw_e, raw_o, stat_e, stat_o, k, k, v, v)
    back_e = swap_even(to_e)
    back_o = swap_odd(to_o)

    full_q, full_k = (q_rows, 0), (k_rows, 0)
    q_shape, k_shape = jax.ShapeDtypeStruct(q.shape, bf16), jax.ShapeDtypeStruct(k.shape, bf16)
    dq, dk, dv, dqe, dke, dve = call(
        functools.partial(interior_kernel, n_ex, gq, gk), steps, width,
        [full_q, full_q, full_q, full_k, full_k],
        [
            (full_q, q_shape), (full_k, k_shape), (full_k, k_shape),
            ((2 * gq, 0), jax.ShapeDtypeStruct((2 * gq, feats), bf16)),
            ((gk, 0), jax.ShapeDtypeStruct((gk, feats), bf16)),
            ((gk, 0), jax.ShapeDtypeStruct((gk, feats), bf16)),
        ],
        flops=int(4e9), nbytes=int(11e6),
    )(table, q, o, g, k, v)

    dq, dk, dv = call(
        functools.partial(edge_kernel, n_ex, gq, gk), steps, width,
        [raw, raw, msg, msg, stat, stat, a_q, b_q, a_q, b_q, a_k, b_k, a_k, b_k, (2 * gq, 0), (gk, 0), (gk, 0), None, None, None],
        [(None, q_shape), (None, k_shape), (None, k_shape)],
        scratch=[
            pltpu.VMEM((2 * gq, feats), bf16), pltpu.VMEM((gk + edge, feats), bf16), pltpu.VMEM((gk + edge, feats), bf16),
            pltpu.SemaphoreType.DMA((steps, 6)),
        ],
        aliases={18: 0, 19: 1, 20: 2},
        flops=int(1e9), nbytes=int(6e6),
    )(table, raw_e, raw_o, back_e, back_o, own, far, q, q, g, g, k, k, v, v, dqe, dke, dve, dq, dk, dv)
    return dq[None], dk[None], dv[None]


def solution(mesh):
    spec = P(("grp", "dp"), "seq", None)
    return jax.shard_map(
        shards,
        mesh=mesh,
        in_specs=(spec,) * 5 + (P(("grp", "dp"), None),) * 2,
        out_specs=(spec,) * 3,
        check_vma=False,
    )
```

time: 243 us -> 50.9 us (0.21)
  waiting for transfers between devices: 105 us -> 3.25 us
  local copies, waits for them, and re-layouts: 64.1 us -> 5.11 us
  Pallas kernels: 0 us -> 27.2 us
  other arithmetic: 27.2 us -> 0.28 us
  matrix products: 23.2 us -> 0 us
  loops' own time: 8.55 us -> 0 us
    ppermute x4 -> x6, waiting for transfers between devices: 105 us -> 3.25 us  [the longest x3 1.73 us: swap_even(): lax.ppermute(x, 'seq', [(i, i ^ 1) for i in range(count) if i ^ 1 < count])]
    slice x17 -> x0, local copies, waits for them, and re-layouts: 45 us -> none  [the longest x6 19.5 us: key_block(): window[1]]
    pallas_call x0 -> x4, Pallas kernels: none -> 27.2 us  [the longest x1 11.9 us: shards(): call(functools.partial(interior_kernel, n_ex, gq, gk), steps, width, [ful...]
    dot_general x36 -> x0, matrix products: 23.2 us -> none  [the longest x6 4.87 us: grad_step(): jnp.einsum('hqk,qhd->khd', weights_low, grads_out, preferred_element_type...]
    dynamic_update_slice x6 -> x0, other arithmetic: 8.86 us -> none  [shards(): lax.scan(grad_step, start_query, jnp.arange(n_blocks, dtype=jnp.int32))]
    another operation x2 -> x0, loops' own time: 8.55 us -> none  [the longest x1 4.33 us: shards(): lax.scan(stats_step, start_stats, jnp.arange(n_blocks, dtype=jnp.int32))]
    dynamic_slice x36 -> x2, local copies, waits for them, and re-layouts: 8.67 us -> 1.87 us  [the longest x1 1.28 us: message(): lax.dynamic_slice(g, (at, 0), (gq, feats))]
    concatenate x1 -> x4, other arithmetic: 6.41 us -> 0.12 us  [the longest x1 0.08 us: shards(): table = jnp.concatenate([near, extra.astype(jnp.int32)], axis=1)]
  transfers between devices with their start and end apart: 4 -> 6, of which waited for: 4 -> 2; matrix products, arithmetic and copies ran while one was open for 2% -> 2% of each run, Pallas kernels for 0% -> 29%
where the time goes in v1:
time: 50.9 us; the launch traced here: 50 us
  Pallas kernels  27.2 us (53%)
  starting transfers between devices  12.8 us (25%)
  local copies, waits for them, and re-layouts  5.11 us (10%)
  waiting for transfers between devices  3.25 us (6%)
  between operations  1.46 us (3%)
    pallas_call x1, Pallas kernels, shards(): call(functools.partial(interior_kernel, n_ex, gq, gk), steps, width, [ful...  11.9 us
    ppermute x3, starting transfers between devices, swap_odd(): return lax.ppermute(x, 'seq', pairs)  9.63 us
    pallas_call x1, Pallas kernels, shards(): call(functools.partial(edge_kernel, n_ex, gq, gk), steps, width, [raw, ra...  7.51 us
    pallas_call x1, Pallas kernels, shards(): call(functools.partial(remote_kernel, n_ex, gq, gk), steps, width, [raw,...  5.25 us
    unnamed x16, local copies, waits for them, and re-layouts  3.15 us
    ppermute x3, starting transfers between devices, swap_even(): lax.ppermute(x, 'seq', [(i, i ^ 1) for i in range(count) if i ^ 1 < count])  3.14 us
    pallas_call x1, Pallas kernels, shards(): call(functools.partial(stats_kernel, n_ex, gq, gk), steps, width, [a_q, b...  2.5 us
    ppermute x3, waiting for transfers between devices, swap_even(): lax.ppermute(x, 'seq', [(i, i ^ 1) for i in range(count) if i ^ 1 < count])  1.73 us
  transfers between devices with their start and end apart: 6, of which 2 were waited for; matrix products, arithmetic and copies ran while one was open for 2% of the time, Pallas kernels for 29%

profile of v1, /device:TPU:16, one launch (start us, length us, event | category | flops | bytes accessed | tf_op | source)
XLA Modules:
  0.0 50.0 jit_solution(11567870822879741974)
XLA Ops:
  0.6 0.0 copy-start.7
  0.6 0.0 copy-start.5
  0.7 0.0 copy-start.6
  0.7 0.0 copy-start
  0.7 1.3 %dynamic-slice_bitcast_fusion = (bf16[32,2048]{1,0:T(8,128)(2,1)S(1)}, bf16[32,2048]{1,0:T(8,128)(2,1)S(1)}, bf16[32,2048]{1,0:T(8,128)(2,1)S(1)}, bf16[32,2048]{1,0:T(8,128)(2,1)S(1)}) fusion(bf16[1,128,2048]{2,1,0:T(8,128)(2,1)} %param.12, s32[]{:T(128)S(6)} %select_n.22, s32[]{:T(128)S(6)} %select_n.21, bf16[1,128,2048]{2,1,0:T(8,128)(2,1)} %param.8), kind=kLoop, calls=%fused_computation.2 | loop fusion | bytes 1048584 | tf_op jit(solution)/shard_map/dynamic_slice | solution.py:341
  2.0 1.6 %collective-permute-start = (bf16[64,2048]{1,0:T(8,128)(2,1)S(1)}, bf16[64,2048]{1,0:T(8,128)(2,1)S(1)}, u32[]{:S(2)}, u32[]{:S(2)}) collective-permute-start(bf16[64,2048]{1,0:T(8,128)(2,1)S(1)} %pad_maximum_fusion), channel_id=1, source_target_pairs={{0,2},{2,0},{4,6},{6,4},{8,10},{10,8},{12,14},{14,12},{1,3},{3,1},... | collective-permute-start | bytes 786440 | tf_op jit(solution)/shard_map/ppermute | solution.py:321
  3.6 2.3 %collective-permute-start.1 = (bf16[64,2048]{1,0:T(8,128)(2,1)S(1)}, bf16[64,2048]{1,0:T(8,128)(2,1)S(1)}, u32[]{:S(2)}, u32[]{:S(2)}) collective-permute-start(bf16[64,2048]{1,0:T(8,128)(2,1)S(1)} %pad_maximum_fusion.1), channel_id=1, source_target_pairs={{2,4},{4,2},{6,8},{8,6},{10,12},{12,10},{3,5},{5,3},{7,9},{9,7},{1... | collective-permute-start | bytes 786440 | tf_op jit(solution)/shard_map/ppermute | solution.py:327
  5.9 0.0 copy-done.7
  5.9 0.0 copy-done.5
  6.0 0.0 copy-done.6
  6.0 0.6 %constant_dynamic-slice_fusion = s32[1,1]{1,0:T(1,128)} fusion(s32[2,33]{1,0:T(2,128)S(1)} %pad_add_fusion, s32[]{:T(128)S(6)} %max.3), kind=kLoop, calls=%fused_computation.6 | loop fusion | bytes 12 | tf_op jit(solution)/shard_map/dynamic_slice | solution.py:332
  7.2 0.1 fusion
  7.3 0.1 pad_add_fusion.2
  7.4 0.1 reshape.15
  7.5 0.1 pad_add_fusion.1.start_ref
  7.5 0.0 copy-done
  7.5 0.0 copy-start.2
  7.5 1.0 %copy-done.2 = bf16[1,128,2048]{2,1,0:T(8,128)(2,1)S(1)} copy-done((bf16[1,128,2048]{2,1,0:T(8,128)(2,1)S(1)}, bf16[1,128,2048]{2,1,0:T(8,128)(2,1)}, u32[]{:S(2)}) %copy-start.2) | copy-done | bytes 524312
  8.6 0.0 copy-start.3
  8.6 1.0 %copy-done.3 = bf16[1,128,2048]{2,1,0:T(8,128)(2,1)S(1)} copy-done((bf16[1,128,2048]{2,1,0:T(8,128)(2,1)S(1)}, bf16[1,128,2048]{2,1,0:T(8,128)(2,1)}, u32[]{:S(2)}) %copy-start.3) | copy-done | bytes 524312
  9.6 0.0 copy-start.4
  9.6 1.0 %copy-done.4 = bf16[1,128,2048]{2,1,0:T(8,128)(2,1)S(1)} copy-done((bf16[1,128,2048]{2,1,0:T(8,128)(2,1)S(1)}, bf16[1,128,2048]{2,1,0:T(8,128)(2,1)}, u32[]{:S(2)}) %copy-start.4) | copy-done | bytes 524312
  10.7 0.0 copy-start.1
  10.7 2.5 %shard_map.103.own_ref = f32[2,2048]{1,0:T(2,128)S(1)} custom-call(s32[2,7]{1,0:T(2,128)S(1)} %pad_add_fusion.1.start_ref, bf16[128,2048]{1,0:T(8,128)(2,1)S(1)} %bitcast.37, bf16[128,2048]{1,0:T(8,128)(2,1)S(1)} %bitcast.38, bf16[128,2048]{1,0:T(8,128)(2,1)S(1)} %bitcast.42, bf16[128,2048]{1,0:T(8,128)(2,1)S(1)} %bitcast.43, ...), custom_call_target="tpu_custom_call" | custom-call | flops 400000000 | bytes 2000000 | tf_op jit(solution)/shard_map/pallas_call | solution.py:351
  13.2 4.4 %collective-permute-start.3 = (f32[2,2048]{1,0:T(2,128)S(1)}, f32[2,2048]{1,0:T(2,128)S(1)}, u32[]{:S(2)}, u32[]{:S(2)}) collective-permute-start(f32[2,2048]{1,0:T(2,128)S(1)} %shard_map.103.own_ref), channel_id=1, source_target_pairs={{2,4},{4,2},{6,8},{8,6},{10,12},{12,10},{3,5},{5,3},{7,9},{9,7},{1... | collective-permute-start | bytes 49160 | tf_op jit(solution)/shard_map/ppermute | solution.py:327
  17.6 0.6 %collective-permute-start.2 = (f32[2,2048]{1,0:T(2,128)S(1)}, f32[2,2048]{1,0:T(2,128)S(1)}, u32[]{:S(2)}, u32[]{:S(2)}) collective-permute-start(f32[2,2048]{1,0:T(2,128)S(1)} %shard_map.103.own_ref), channel_id=1, source_target_pairs={{0,2},{2,0},{4,6},{6,4},{8,10},{10,8},{12,14},{14,12},{1,3},{3,1},... | collective-permute-start | bytes 49160 | tf_op jit(solution)/shard_map/ppermute | solution.py:321
  18.2 1.5 %collective-permute-done.3.to_ref = f32[2,2048]{1,0:T(2,128)S(1)} collective-permute-done((f32[2,2048]{1,0:T(2,128)S(1)}, f32[2,2048]{1,0:T(2,128)S(1)}, u32[]{:S(2)}, u32[]{:S(2)}) %collective-permute-start.3) | collective-permute-done | bytes 16416 | tf_op jit(solution)/shard_map/ppermute | solution.py:327
  19.7 1.7 %collective-permute-done.2.te_ref = f32[2,2048]{1,0:T(2,128)S(1)} collective-permute-done((f32[2,2048]{1,0:T(2,128)S(1)}, f32[2,2048]{1,0:T(2,128)S(1)}, u32[]{:S(2)}, u32[]{:S(2)}) %collective-permute-start.2) | collective-permute-done | bytes 16416 | tf_op jit(solution)/shard_map/ppermute | solution.py:321
  21.4 0.0 collective-permute-done.re_ref
  21.4 0.0 collective-permute-done.1.ro_ref
  21.5 0.0 copy-done.1
  21.5 5.3 %shard_map.104 = (bf16[48,2048]{1,0:T(8,128)(2,1)S(1)}, bf16[48,2048]{1,0:T(8,128)(2,1)S(1)}, f32[2,2048]{1,0:T(2,128)S(1)}) custom-call(s32[2,7]{1,0:T(2,128)S(1)} %pad_add_fusion.1.start_ref, bf16[64,2048]{1,0:T(8,128)(2,1)S(1)} %collective-permute-done.re_ref, bf16[64,2048]{1,0:T(8,128)(2,1)S(1)} %collective-permute-done.1.ro_ref, ...), custom_call_target="tpu_custom_call" | custom-call | flops 800000000 | bytes 3000000 | tf_op jit(solution)/shard_map/pallas_call | solution.py:363
  26.7 1.0 %collective-permute-start.4 = (bf16[48,2048]{1,0:T(8,128)(2,1)S(1)}, bf16[48,2048]{1,0:T(8,128)(2,1)S(1)}, u32[]{:S(2)}, u32[]{:S(2)}) collective-permute-start(bf16[48,2048]{1,0:T(8,128)(2,1)S(1)} %get-tuple-element.15), channel_id=1, source_target_pairs={{0,2},{2,0},{4,6},{6,4},{8,10},{10,8},{12,14},{14,12},{1,3},{3,1},... | collective-permute-start | bytes 589832 | tf_op jit(solution)/shard_map/ppermute | solution.py:321
  27.7 2.9 %collective-permute-start.5 = (bf16[48,2048]{1,0:T(8,128)(2,1)S(1)}, bf16[48,2048]{1,0:T(8,128)(2,1)S(1)}, u32[]{:S(2)}, u32[]{:S(2)}) collective-permute-start(bf16[48,2048]{1,0:T(8,128)(2,1)S(1)} %get-tuple-element.16), channel_id=1, source_target_pairs={{2,4},{4,2},{6,8},{8,6},{10,12},{12,10},{3,5},{5,3},{7,9},{9,7},{1... | collective-permute-start | bytes 589832 | tf_op jit(solution)/shard_map/ppermute | solution.py:327
  30.6 11.9 %shard_map.105 = (bf16[128,2048]{1,0:T(8,128)(2,1)}, bf16[512,2048]{1,0:T(8,128)(2,1)}, bf16[512,2048]{1,0:T(8,128)(2,1)}, bf16[64,2048]{1,0:T(8,128)(2,1)S(1)},...) custom-call(s32[2,7]{1,0:T(2,128)S(1)} %pad_add_fusion.1.start_ref, bf16[128,2048]{1,0:T(8,128)(2,1)S(1)} %bitcast.39, ...), custom_call_target="tpu_custom_call" | custom-call | flops 4000000000 | bytes 11000000 | tf_op jit(solution)/shard_map/pallas_call | solution.py:373
  42.5 0.0 collective-permute-done.4.me_ref
  42.5 0.0 collective-permute-done.5.mo_ref
  42.5 7.5 %shard_map.106 = (bf16[128,2048]{1,0:T(8,128)(2,1)}, bf16[512,2048]{1,0:T(8,128)(2,1)}, bf16[512,2048]{1,0:T(8,128)(2,1)}) custom-call(s32[2,7]{1,0:T(2,128)S(1)} %pad_add_fusion.1.start_ref, bf16[64,2048]{1,0:T(8,128)(2,1)S(1)} %collective-permute-done.re_ref, ...), custom_call_target="tpu_custom_call", output_to_operand_aliasing={{0}: (18, {}), {1}: (19, {}), {2}: (20, {})} | custom-call | flops 1000000000 | bytes 6000000 | tf_op jit(solution)/shard_map/pallas_call | solution.py:385
  (4 shorter events, 0.1 us)
Async XLA Ops:
  0.6 5.3 %copy-start.7 = (s32[2]{0:T(128)S(1)}, s32[2]{0:T(128)}, u32[]{:S(2)}) copy-start(s32[2]{0:T(128)} %constant.38.clone) | copy-start | bytes 28
  0.6 5.3 %copy-start.5 = (s32[1,33]{1,0:T(1,128)S(1)}, s32[1,33]{1,0:T(1,128)}, u32[]{:S(2)}) copy-start(s32[1,33]{1,0:T(1,128)} %param.14) | copy-start | bytes 400
  0.7 5.3 %copy-start.6 = (s32[1,33]{1,0:T(1,128)S(1)}, s32[1,33]{1,0:T(1,128)}, u32[]{:S(2)}) copy-start(s32[1,33]{1,0:T(1,128)} %param.13) | copy-start | bytes 400
  0.7 6.9 %copy-start = (bf16[1,512,2048]{2,1,0:T(8,128)(2,1)S(1)}, bf16[1,512,2048]{2,1,0:T(8,128)(2,1)}, u32[]{:S(2)}) copy-start(bf16[1,512,2048]{2,1,0:T(8,128)(2,1)} %param.9) | copy-start | bytes 6291460
  2.0 19.4 %collective-permute-start = (bf16[64,2048]{1,0:T(8,128)(2,1)S(1)}, bf16[64,2048]{1,0:T(8,128)(2,1)S(1)}, u32[]{:S(2)}, u32[]{:S(2)}) collective-permute-start(bf16[64,2048]{1,0:T(8,128)(2,1)S(1)} %pad_maximum_fusion), channel_id=1, source_target_pairs={{0,2},{2,0},{4,6},{6,4},{8,10},{10,8},{12,14},{14,12},{1,3},{3,1},... | collective-permute-start | bytes 786440 | tf_op jit(solution)/shard_map/ppermute | solution.py:321
  3.6 17.8 %collective-permute-start.1 = (bf16[64,2048]{1,0:T(8,128)(2,1)S(1)}, bf16[64,2048]{1,0:T(8,128)(2,1)S(1)}, u32[]{:S(2)}, u32[]{:S(2)}) collective-permute-start(bf16[64,2048]{1,0:T(8,128)(2,1)S(1)} %pad_maximum_fusion.1), channel_id=1, source_target_pairs={{2,4},{4,2},{6,8},{8,6},{10,12},{12,10},{3,5},{5,3},{7,9},{9,7},{1... | collective-permute-start | bytes 786440 | tf_op jit(solution)/shard_map/ppermute | solution.py:327
  7.5 1.0 %copy-start.2 = (bf16[1,128,2048]{2,1,0:T(8,128)(2,1)S(1)}, bf16[1,128,2048]{2,1,0:T(8,128)(2,1)}, u32[]{:S(2)}) copy-start(bf16[1,128,2048]{2,1,0:T(8,128)(2,1)} %param.12) | copy-start | bytes 1572868
  8.6 1.0 %copy-start.3 = (bf16[1,128,2048]{2,1,0:T(8,128)(2,1)S(1)}, bf16[1,128,2048]{2,1,0:T(8,128)(2,1)}, u32[]{:S(2)}) copy-start(bf16[1,128,2048]{2,1,0:T(8,128)(2,1)} %param.8) | copy-start | bytes 1572868
  9.6 1.0 %copy-start.4 = (bf16[1,128,2048]{2,1,0:T(8,128)(2,1)S(1)}, bf16[1,128,2048]{2,1,0:T(8,128)(2,1)}, u32[]{:S(2)}) copy-start(bf16[1,128,2048]{2,1,0:T(8,128)(2,1)} %param.11) | copy-start | bytes 1572868
  10.7 10.8 %copy-start.1 = (bf16[1,512,2048]{2,1,0:T(8,128)(2,1)S(1)}, bf16[1,512,2048]{2,1,0:T(8,128)(2,1)}, u32[]{:S(2)}) copy-start(bf16[1,512,2048]{2,1,0:T(8,128)(2,1)} %param.10) | copy-start | bytes 6291460
  13.2 6.5 %collective-permute-start.3 = (f32[2,2048]{1,0:T(2,128)S(1)}, f32[2,2048]{1,0:T(2,128)S(1)}, u32[]{:S(2)}, u32[]{:S(2)}) collective-permute-start(f32[2,2048]{1,0:T(2,128)S(1)} %shard_map.103.own_ref), channel_id=1, source_target_pairs={{2,4},{4,2},{6,8},{8,6},{10,12},{12,10},{3,5},{5,3},{7,9},{9,7},{1... | collective-permute-start | bytes 49160 | tf_op jit(solution)/shard_map/ppermute | solution.py:327
  17.6 3.8 %collective-permute-start.2 = (f32[2,2048]{1,0:T(2,128)S(1)}, f32[2,2048]{1,0:T(2,128)S(1)}, u32[]{:S(2)}, u32[]{:S(2)}) collective-permute-start(f32[2,2048]{1,0:T(2,128)S(1)} %shard_map.103.own_ref), channel_id=1, source_target_pairs={{0,2},{2,0},{4,6},{6,4},{8,10},{10,8},{12,14},{14,12},{1,3},{3,1},... | collective-permute-start | bytes 49160 | tf_op jit(solution)/shard_map/ppermute | solution.py:321
  26.7 15.8 %collective-permute-start.4 = (bf16[48,2048]{1,0:T(8,128)(2,1)S(1)}, bf16[48,2048]{1,0:T(8,128)(2,1)S(1)}, u32[]{:S(2)}, u32[]{:S(2)}) collective-permute-start(bf16[48,2048]{1,0:T(8,128)(2,1)S(1)} %get-tuple-element.15), channel_id=1, source_target_pairs={{0,2},{2,0},{4,6},{6,4},{8,10},{10,8},{12,14},{14,12},{1,3},{3,1},... | collective-permute-start | bytes 589832 | tf_op jit(solution)/shard_map/ppermute | solution.py:321
  27.7 14.8 %collective-permute-start.5 = (bf16[48,2048]{1,0:T(8,128)(2,1)S(1)}, bf16[48,2048]{1,0:T(8,128)(2,1)S(1)}, u32[]{:S(2)}, u32[]{:S(2)}) collective-permute-start(bf16[48,2048]{1,0:T(8,128)(2,1)S(1)} %get-tuple-element.16), channel_id=1, source_target_pairs={{2,4},{4,2},{6,8},{8,6},{10,12},{12,10},{3,5},{5,3},{7,9},{9,7},{1... | collective-permute-start | bytes 589832 | tf_op jit(solution)/shard_map/ppermute | solution.py:327

commit v2 on v0

v2 whole, which is shorter than its diff:
```python
import functools

import jax
import jax.numpy as jnp
from jax import lax
from jax.experimental import pallas as pl
from jax.experimental.pallas import tpu as pltpu
from jax.sharding import PartitionSpec as P

H = 32
HD = 64
LANES = 256
PER = LANES // HD

low = -1e30
high = 1e30
BATCH = 2
SPLIT = 4


def dot_nt(a, b):
    return lax.dot_general(a, b, (((1,), (1,)), ((), ())), preferred_element_type=jnp.float32)


def dot_nn(a, b):
    return lax.dot_general(a, b, (((1,), (0,)), ((), ())), preferred_element_type=jnp.float32)


def dot_tn(a, b):
    return lax.dot_general(a, b, (((0,), (0,)), ((), ())), preferred_element_type=jnp.float32)


def spread(rows):
    head = lax.broadcasted_iota(jnp.int32, rows.shape, 1) // HD
    return jnp.concatenate([jnp.where(head == h, rows, jnp.zeros_like(rows)) for h in range(PER)], axis=0)


def gather_heads(full):
    slots = full.shape[0] // PER
    head = lax.broadcasted_iota(jnp.int32, (slots, full.shape[1]), 1) // HD
    out = full[:slots]
    for h in range(1, PER):
        out = jnp.where(head == h, full[h * slots : (h + 1) * slots], out)
    return out


def slot_of(slots):
    return lax.rem(lax.broadcasted_iota(jnp.int32, (1, PER * slots), 1), slots)


def row_dots(outs, spread_grads):
    slots = outs.shape[0]
    full = dot_nt(outs, spread_grads)
    row = lax.broadcasted_iota(jnp.int32, full.shape, 0)
    lane = lax.rem(lax.broadcasted_iota(jnp.int32, full.shape, 1), slots)
    return jnp.sum(jnp.where(row == lane, full, 0.0), axis=0, keepdims=True)


def log_add(a, b):
    top = jnp.maximum(a, b)
    return top + jnp.log(jnp.exp(a - top) + jnp.exp(b - top))


def row_ids(rows, lanes):
    return lax.broadcasted_iota(jnp.int32, (rows, lanes), 0)


def run_skewed(units):
    live, queue = [], list(units)
    while queue or live:
        if queue:
            live.append(queue.pop(0))
        for unit in list(live):
            try:
                next(unit)
            except StopIteration:
                live.remove(unit)


def each_group(groups, batch, units_of):
    @pl.loop(0, groups // batch)
    def _(at):
        units = []
        for c in range(batch):
            start = at * (batch * LANES) + c * LANES
            units += units_of(pl.ds(pl.multiple_of(start, LANES), LANES))
        run_skewed(units)


class Bounds:
    def __init__(self, shape, table):
        self.n_ex, self.gq, self.gk, self.count = shape
        self.dec_ref, self.enc_ref, pos_ref = table
        self.pos = pos_ref[0]
        self.even = lax.rem(self.pos, 2) == 0
        self.has_next = self.pos < self.count - 1

    def dec(self, i):
        return self.dec_ref[0, self.pos * self.n_ex + i] - self.pos * (self.n_ex * self.gq)

    def enc(self, i):
        return self.enc_ref[0, self.pos * self.n_ex + i] - self.pos * (self.n_ex * self.gk)

    def prior(self):
        at = jnp.maximum(self.pos * self.n_ex - 1, 0)
        rows = self.dec_ref[0, at] - self.pos * (self.n_ex * self.gq) + self.gq
        return jnp.where(self.pos > 0, rows, self.gq)

    def far_lanes(self, slot):
        hi = self.dec(self.n_ex) - self.n_ex * self.gq + self.gq
        return (slot >= self.prior()) & (slot < hi)

    def own_lanes(self, slot):
        lo = self.dec(self.n_ex - 1) - (self.n_ex - 1) * self.gq
        return (slot >= lo) & (slot < self.dec(0) + self.gq)


def edge_mask(bounds, s, far):
    gq, gk = bounds.gq, bounds.gk
    edge = gk // 2
    slot = slot_of(2 * gq)
    first = slot < gq
    in_a, in_b = (~first, first) if far else (first, ~first)
    row = row_ids(edge, LANES)
    a_lo = bounds.enc(bounds.n_ex - 1) - (bounds.n_ex - 1) * gk
    s0 = jnp.where(in_a & (row >= a_lo), s[:edge], low)
    s1 = jnp.where(in_a, s[edge:gk], low)
    s2 = jnp.where(in_b & (row < bounds.enc(0)), s[gk:], low)
    return s0, s1, s2


def exp_sum(s0, s1, s2):
    top = jnp.max(jnp.maximum(jnp.maximum(s0, s1), s2), axis=0, keepdims=True)
    e0, e1, e2 = jnp.exp(s0 - top), jnp.exp(s1 - top), jnp.exp(s2 - top)
    return top, e0, e1, e2, jnp.sum(e0 + e1 + e2, axis=0, keepdims=True)


def interior_kernel(shape, lo, hi, *refs):
    table, (_, q_ref, o_ref, g_ref, k_ref, v_ref), refs = refs[:3], refs[3:9], refs[9:]
    if lo > 0:
        refs = refs[6:]
    dq_out, dk_out, dv_out, dqe_ref, dke_ref, dve_ref, dq_buf, dk_buf, dv_buf, sems = refs
    bounds = Bounds(shape, table)
    n_ex, gq, gk = bounds.n_ex, bounds.gq, bounds.gk
    slots = 2 * gq
    edge = gk // 2
    win = gk + edge
    slot = slot_of(slots)
    bf16 = jnp.bfloat16

    def unit(i, cols, held):
        q0, k0 = i * gq, i * gk
        d_lo, d_hi = bounds.dec(i) - q0, bounds.dec(i + 1) - q0
        e_lo, e_hi = bounds.enc(i) - k0, bounds.enc(i + 1) - k0 - gk
        keys = k_ref[k0 : k0 + win, cols]
        qs = spread(q_ref[q0 : q0 + slots, cols])
        s = dot_nt(keys, qs)
        gs = spread(g_ref[q0 : q0 + slots, cols])
        dots = row_dots(o_ref[q0 : q0 + slots, cols], gs)
        dp = dot_nt(v_ref[k0 : k0 + win, cols], gs)
        yield
        row = row_ids(edge, LANES)
        s0 = jnp.where(row >= e_lo, s[:edge], low)
        s2 = jnp.where(row < e_hi, s[gk:], low)
        _, e0, e1, e2, total = exp_sum(s0, s[edge:gk], s2)
        yield
        inv = jnp.where((slot >= d_lo) & (slot < d_hi), 1.0 / total, 0.0)
        p = jnp.concatenate([e0, e1, e2], axis=0) * inv
        p_low = p.astype(bf16)
        yield
        dv = dot_nn(p_low, gs)
        ds = (p * (dp - dots)).astype(bf16)
        yield
        dk = dot_nn(ds, qs)
        dq = gather_heads(dot_tn(ds, keys))
        yield
        for which, (ref, ext, part) in enumerate(((dk_buf, dke_ref, dk), (dv_buf, dve_ref, dv))):
            first = part[:edge]
            if i > 0:
                first = first + held[(i - 1, which)]
                ref[k0 : k0 + edge, cols] = first.astype(bf16)
            else:
                ext[:edge, cols] = first.astype(bf16)
            ref[k0 + edge : k0 + gk, cols] = part[edge:gk].astype(bf16)
            if i < n_ex - 2:
                held[(i, which)] = part[gk:]
            else:
                ext[edge:, cols] = part[gk:].astype(bf16)
        first = dq[:gq]
        if i > 0:
            dq_buf[q0 : q0 + gq, cols] = (first + held[(i - 1, 2)]).astype(bf16)
        else:
            dqe_ref[:gq, cols] = first.astype(bf16)
        if i < n_ex - 2:
            held[(i, 2)] = dq[gq:]
        else:
            dqe_ref[gq:, cols] = dq[gq:].astype(bf16)
        yield

    def copies(at):
        cols = pl.ds(pl.multiple_of(at * (BATCH * LANES), LANES), BATCH * LANES)
        out = []
        k_rows, q_rows = pl.ds(edge, (n_ex - 1) * gk - edge), pl.ds(gq, (n_ex - 2) * gq)
        for j, (buf, ref, rows) in enumerate(((dk_buf, dk_out, k_rows), (dv_buf, dv_out, k_rows), (dq_buf, dq_out, q_rows))):
            out.append(pltpu.make_async_copy(buf.at[rows, cols], ref.at[rows, cols], sems.at[at, j]))
        return out

    @pl.loop(lo // BATCH, hi // BATCH)
    def _(at):
        units = []
        for c in range(BATCH):
            cols = pl.ds(pl.multiple_of(at * (BATCH * LANES) + c * LANES, LANES), LANES)
            held = {}
            units += [unit(i, cols, held) for i in range(n_ex - 1)]
        run_skewed(units)
        for copy in copies(at):
            copy.start()

    @pl.loop(lo // BATCH, hi // BATCH)
    def _(at):
        for copy in copies(at):
            copy.wait()


def stats_kernel(shape, *refs):
    *table, q_hbm, o_hbm, g_hbm, k_hbm, stat_ref, q_ref, o_ref, g_ref, k_ref, sems = refs
    bounds = Bounds(shape, table)
    n_ex, gq, gk = bounds.n_ex, bounds.gq, bounds.gk
    edge = gk // 2
    last = (n_ex - 1) * gq

    def moved(src, dst, rows, sem):
        return pltpu.make_async_copy(src.at[pl.ds(*rows)], dst.at[pl.ds(*rows)], sems.at[sem])

    ends = [
        pltpu.make_async_copy(k_hbm.at[pl.ds((n_ex - 1) * gk, gk)], k_ref.at[pl.ds(0, gk)], sems.at[0]),
        pltpu.make_async_copy(k_hbm.at[pl.ds(0, edge)], k_ref.at[pl.ds(gk, edge)], sems.at[1]),
    ]
    rest = []
    for j, (src, dst) in enumerate(((q_hbm, q_ref), (g_hbm, g_ref), (o_hbm, o_ref))):
        ends.append(moved(src, dst, (last, gq), 3 * j + 2))
        ends.append(moved(src, dst, (0, gq), 3 * j + 3))
        rest.append(moved(src, dst, (gq, last - gq), 3 * j + 4))
    for copy in ends + rest:
        copy.start()
    for copy in ends:
        copy.wait()

    def both(ref, cols):
        return jnp.concatenate([ref[last:, cols], ref[:gq, cols]], axis=0)

    def unit(cols):
        qs = spread(both(q_ref, cols))
        s = dot_nt(k_ref[:, cols], qs)
        yield
        dots = row_dots(both(o_ref, cols), spread(both(g_ref, cols)))
        yield
        top, _, _, _, total = exp_sum(*edge_mask(bounds, s, False))
        stat_ref[0:1, cols] = top + jnp.log(total)
        stat_ref[1:2, cols] = dots
        yield

    each_group(q_ref.shape[1] // LANES, 4, lambda cols: [unit(cols)])
    for copy in rest:
        copy.wait()


def pick(flag, a, b):
    return jnp.where(flag, a, b)


def remote_kernel(shape, *refs):
    *table, _, re_ref, ro_ref, te_ref, to_ref, k_ref, v_ref, me_ref, mo_ref, stat_ref = refs
    bounds = Bounds(shape, table)
    n_ex, gq, gk = bounds.n_ex, bounds.gq, bounds.gk
    edge = gk // 2
    even = bounds.even
    slot = slot_of(2 * gq)
    bf16, f32 = jnp.bfloat16, jnp.float32
    last = (n_ex - 1) * gk

    def ends(ref, cols):
        return jnp.concatenate([ref[last:, cols], ref[:edge, cols]], axis=0)

    def unit(cols):
        re, ro = re_ref[:, cols], ro_ref[:, cols]
        before, after = pick(even, ro, re), pick(even, re, ro)
        qs = spread(jnp.concatenate([before[:gq], after[:gq]], axis=0))
        keys = ends(k_ref, cols)
        s = dot_nt(keys, qs)
        gs = spread(jnp.concatenate([before[gq:], after[gq:]], axis=0))
        dp = dot_nt(ends(v_ref, cols), gs)
        yield
        te, to = te_ref[:, cols], to_ref[:, cols]
        tbefore, tafter = pick(even, to, te), pick(even, te, to)
        stat = jnp.where(slot < gq, tbefore, tafter)
        top, e0, e1, e2, total = exp_sum(*edge_mask(bounds, s, True))
        mine = top + jnp.log(total)
        yield
        whole = log_add(mine, stat[0:1])
        dots = stat[1:2]
        scale = jnp.where(bounds.far_lanes(slot), jnp.exp(top - whole), 0.0)
        p = jnp.concatenate([e0, e1, e2], axis=0) * scale
        ds = (p * (dp - dots)).astype(bf16)
        stat_ref[0:1, cols] = jnp.where(bounds.far_lanes(slot), whole, high)
        stat_ref[1:2, cols] = dots
        yield
        dq = gather_heads(dot_tn(ds, keys)).astype(bf16)
        hi = mine.astype(bf16).astype(f32)
        mid = (mine - hi).astype(bf16).astype(f32)
        tail = mine - hi - mid
        three = lax.broadcasted_iota(jnp.int32, (8, LANES), 0)
        logs = jnp.where(three == 0, hi, jnp.where(three == 1, mid, tail)).astype(bf16)
        yield
        me_ref[:gq, cols] = pick(even, dq[gq:], dq[:gq])
        mo_ref[:gq, cols] = pick(even, dq[:gq], dq[gq:])
        me_ref[gq:, cols] = logs
        mo_ref[gq:, cols] = logs
        yield

    each_group(re_ref.shape[1] // LANES, 4, lambda cols: [unit(cols)])


def edge_kernel(shape, *refs):
    *table, re_ref, ro_ref, me_ref, mo_ref, own_ref, far_ref, q_ref, g_ref, k_ref, v_ref = refs[:13]
    dqe_ref, dke_ref, dve_ref, _, _, _, dq_out, dk_out, dv_out, dq_buf, dk_buf, dv_buf, sems = refs[13:]
    bounds = Bounds(shape, table)
    n_ex, gq, gk = bounds.n_ex, bounds.gq, bounds.gk
    edge = gk // 2
    even = bounds.even
    slot = slot_of(2 * gq)
    bf16, f32 = jnp.bfloat16, jnp.float32
    last_q, last_k = (n_ex - 1) * gq, (n_ex - 1) * gk

    def unit(side, cols):
        far = pick(even, re_ref[:, cols], ro_ref[:, cols]) if side == 0 else pick(even, ro_ref[:, cols], re_ref[:, cols])
        back = (me_ref, mo_ref) if side == 0 else (mo_ref, me_ref)
        if side == 0:
            pieces = [(q_ref[last_q:, cols], far[:gq]), (g_ref[last_q:, cols], far[gq:])]
            keys, vals = k_ref[last_k:, cols], v_ref[last_k:, cols]
        else:
            pieces = [(far[:gq], q_ref[:gq, cols]), (far[gq:], g_ref[:gq, cols])]
            keys, vals = k_ref[:edge, cols], v_ref[:edge, cols]
        qs, gs = (spread(jnp.concatenate(pair, axis=0)) for pair in pieces)
        s = dot_nt(keys, qs)
        dp = dot_nt(vals, gs)
        yield
        logs = pick(even, back[0][gq:, cols].astype(f32), back[1][gq:, cols].astype(f32))
        log_far = logs[0:1] + logs[1:2] + logs[2:3]
        if side == 0:
            log_far = jnp.where(bounds.has_next, log_far, low)
        log_own = log_add(own_ref[0:1, cols], log_far)
        log_own = jnp.where(bounds.own_lanes(slot), log_own, high)
        mine = slot < gq if side == 0 else slot >= gq
        whole = jnp.where(mine, log_own, far_ref[0:1, cols])
        dots = jnp.where(mine, own_ref[1:2, cols], far_ref[1:2, cols])
        row = row_ids(edge, LANES)
        if side == 0:
            s = jnp.concatenate([jnp.where(row >= bounds.enc(n_ex - 1) - last_k, s[:edge], low), s[edge:]], axis=0)
        else:
            s = jnp.where(row < bounds.enc(0), s, low)
        p = jnp.exp(s - whole)
        p_low = p.astype(bf16)
        yield
        dv = dot_nn(p_low, gs)
        ds = (p * (dp - dots)).astype(bf16)
        yield
        dk = dot_nn(ds, qs)
        dq = gather_heads(dot_tn(ds, keys))
        yield
        for buf, ext, part in ((dk_buf, dke_ref, dk), (dv_buf, dve_ref, dv)):
            if side == 0:
                buf[edge:gk, cols] = (part[:edge] + ext[edge:, cols].astype(f32)).astype(bf16)
                buf[gk:, cols] = part[edge:].astype(bf16)
            else:
                buf[:edge, cols] = (part + ext[:edge, cols].astype(f32)).astype(bf16)
        rows = slice(gq, 2 * gq) if side == 0 else slice(0, gq)
        add = pick(even, back[0][:gq, cols].astype(f32), back[1][:gq, cols].astype(f32))
        part = dq[:gq] if side == 0 else dq[gq:]
        dq_buf[rows, cols] = (part + add + dqe_ref[rows, cols].astype(f32)).astype(bf16)
        yield

    def copies(at):
        cols = pl.ds(pl.multiple_of(at * (BATCH * LANES), LANES), BATCH * LANES)
        out = []
        for j, (buf, ref) in enumerate(((dk_buf, dk_out), (dv_buf, dv_out))):
            out.append(pltpu.make_async_copy(buf.at[pl.ds(0, edge), cols], ref.at[pl.ds(0, edge), cols], sems.at[at, 2 * j]))
            out.append(pltpu.make_async_copy(buf.at[pl.ds(edge, gk), cols], ref.at[pl.ds(last_k, gk), cols], sems.at[at, 2 * j + 1]))
        out.append(pltpu.make_async_copy(dq_buf.at[pl.ds(0, gq), cols], dq_out.at[pl.ds(0, gq), cols], sems.at[at, 4]))
        out.append(pltpu.make_async_copy(dq_buf.at[pl.ds(gq, gq), cols], dq_out.at[pl.ds(last_q, gq), cols], sems.at[at, 5]))
        return out

    turns = q_ref.shape[1] // LANES // BATCH

    @pl.loop(0, turns)
    def _(at):
        units = []
        for c in range(BATCH):
            cols = pl.ds(pl.multiple_of(at * (BATCH * LANES) + c * LANES, LANES), LANES)
            units += [unit(0, cols), unit(1, cols)]
        run_skewed(units)
        for copy in copies(at):
            copy.start()

    @pl.loop(0, turns)
    def _(at):
        for copy in copies(at):
            copy.wait()


inside = pl.BlockSpec(memory_space=pltpu.VMEM)
anywhere = pl.BlockSpec(memory_space=pl.ANY)
off_chip = pl.BlockSpec(memory_space=pltpu.HBM)


def call(kernel, ins, outs, scratch=(), aliases=None, flops=0, nbytes=0):
    return pl.pallas_call(
        kernel,
        out_shape=[shape for _, shape in outs],
        in_specs=[pl.BlockSpec(memory_space=pltpu.SMEM)] * 3 + list(ins),
        out_specs=[spec for spec, _ in outs],
        scratch_shapes=list(scratch),
        input_output_aliases=aliases or {},
        compiler_params=pltpu.CompilerParams(vmem_limit_bytes=40 * 1024 * 1024),
        cost_estimate=pl.CostEstimate(flops=flops, bytes_accessed=nbytes, transcendentals=0),
    )


def shards(dec_query, enc_key, enc_value, saved_out, d_out, dec_start, enc_start):
    q, k, v, o, g = dec_query[0], enc_key[0], enc_value[0], saved_out[0], d_out[0]
    q_rows, feats = q.shape
    k_rows = k.shape[0]
    pos = lax.axis_index("seq")
    count = lax.axis_size("seq")
    n_ex = (dec_start.shape[1] - 1) // count
    gq, gk = q_rows // n_ex, k_rows // n_ex
    edge = gk // 2
    groups = feats // LANES
    even = lax.rem(pos, 2) == 0
    bf16, f32 = jnp.bfloat16, jnp.float32
    shape = (n_ex, gq, gk, count)

    def swap_even(x):
        return lax.ppermute(x, "seq", [(i, i ^ 1) for i in range(count) if i ^ 1 < count])

    def swap_odd(x):
        pairs = []
        for i in range(1, count - 1, 2):
            pairs += [(i, i + 1), (i + 1, i)]
        return lax.ppermute(x, "seq", pairs)

    table = (dec_start, enc_start, pos.astype(jnp.int32)[None])
    last = (n_ex - 1) * gq
    at_e, at_o = jnp.where(even, last, 0), jnp.where(even, 0, last)

    def message(at):
        return jnp.concatenate([lax.dynamic_slice(q, (at, 0), (gq, feats)), lax.dynamic_slice(g, (at, 0), (gq, feats))], axis=0)

    raw_e = swap_even(message(at_e))
    raw_o = swap_odd(message(at_o))

    def like(rows, kind=bf16):
        return jax.ShapeDtypeStruct((rows, feats), kind)

    def vmem(rows):
        return pltpu.VMEM((rows, feats), bf16)

    own, q, o, g = call(
        functools.partial(stats_kernel, shape), [off_chip] * 4, [(inside, like(2, f32))] + [(inside, like(q_rows))] * 3,
        scratch=[vmem(gk + edge), pltpu.SemaphoreType.DMA((11,))],
        flops=int(4e8), nbytes=int(2e6),
    )(*table, *(pltpu.with_memory_space_constraint(x, pltpu.HBM) for x in (q, o, g, k)))
    stat_e = swap_even(own)
    stat_o = swap_odd(own)

    def interior(lo, hi, after, before=()):
        return call(
            functools.partial(interior_kernel, shape, lo, hi),
            [anywhere] + [inside] * 5 + ([anywhere] * 3 + [inside] * 3 if before else []),
            [(anywhere, like(q_rows)), (anywhere, like(k_rows)), (anywhere, like(k_rows)),
             (inside, like(2 * gq)), (inside, like(gk)), (inside, like(gk))],
            scratch=[vmem(q_rows), vmem(k_rows), vmem(k_rows), pltpu.SemaphoreType.DMA((groups // BATCH, 3))],
            aliases={9 + j: j for j in range(6)} if before else {},
            flops=int(5e8) * (hi - lo), nbytes=int(1e6) * (hi - lo),
        )(*table, after, q, o, g, k, v, *before)

    part = interior(0, SPLIT, own)
    to_e, to_o, far = call(
        functools.partial(remote_kernel, shape), [anywhere] + [inside] * 6,
        [(inside, like(gq + 8)), (inside, like(gq + 8)), (inside, like(2, f32))],
        flops=int(8e8), nbytes=int(3e6),
    )(*table, part[3], raw_e, raw_o, stat_e, stat_o, k, v)
    back_e = swap_even(to_e)
    back_o = swap_odd(to_o)
    if SPLIT < groups:
        part = interior(SPLIT, groups, far, part)
    dq, dk, dv, dqe, dke, dve = part
    dq, dk, dv = call(
        functools.partial(edge_kernel, shape), [inside] * 13 + [anywhere] * 3,
        [(anywhere, like(q_rows)), (anywhere, like(k_rows)), (anywhere, like(k_rows))],
        scratch=[vmem(2 * gq), vmem(gk + edge), vmem(gk + edge), pltpu.SemaphoreType.DMA((groups // BATCH, 6))],
        aliases={16: 0, 17: 1, 18: 2},
        flops=int(1e9), nbytes=int(6e6),
    )(*table, raw_e, raw_o, back_e, back_o, own, far, q, g, k, v, dqe, dke, dve, dq, dk, dv)
    return dq[None], dk[None], dv[None]


def solution(mesh):
    spec = P(("grp", "dp"), "seq", None)
    return jax.shard_map(
        shards,
        mesh=mesh,
        in_specs=(spec,) * 5 + (P(("grp", "dp"), None),) * 2,
        out_specs=(spec,) * 3,
        check_vma=False,
    )
```

time: 243 us -> 36.8 us (0.15)
  the two profiles are of different devices: /device:TPU:16 before, /device:TPU:8 now
where the time goes in v2:
time: 36.8 us; the launch traced here: 36.6 us
  Pallas kernels  19 us (52%)
  starting transfers between devices  13.6 us (37%)
  waiting for transfers between devices  1.95 us (5%)
  local copies, waits for them, and re-layouts  1.16 us (3%)
  between operations  0.78 us (2%)
    pallas_call x2, Pallas kernels, interior(): call(functools.partial(interior_kernel, shape, lo, hi), [anywhere] + [ins...  8.8 us
    ppermute x3, starting transfers between devices, swap_even(): lax.ppermute(x, 'seq', [(i, i ^ 1) for i in range(count) if i ^ 1 < count])  7.63 us
    ppermute x3, starting transfers between devices, swap_odd(): return lax.ppermute(x, 'seq', pairs)  6 us
    pallas_call x1, Pallas kernels, shards(): call(functools.partial(edge_kernel, shape), [inside] * 13 + [anywhere] *...  4.62 us
    pallas_call x1, Pallas kernels, shards(): call(functools.partial(stats_kernel, shape), [off_chip] * 4, [(inside, li...  3.09 us
    pallas_call x1, Pallas kernels, shards(): call(functools.partial(remote_kernel, shape), [anywhere] + [inside] * 6,...  2.53 us
    ppermute x3, waiting for transfers between devices, swap_odd(): return lax.ppermute(x, 'seq', pairs)  1.93 us
    dynamic_slice x1, local copies, waits for them, and re-layouts, message(): lax.dynamic_slice(g, (at, 0), (gq, feats))  1.14 us
  transfers between devices with their start and end apart: 6, of which 2 were waited for; matrix products, arithmetic and copies ran while one was open for 0% of the time, Pallas kernels for 32%

profile of v2, /device:TPU:8, one launch (start us, length us, event | category | flops | bytes accessed | tf_op | source)
XLA Modules:
  0.0 36.6 jit_solution(6329427339951531248)
XLA Ops:
  0.6 0.0 copy-start.2
  0.6 0.0 copy-start.3
  0.7 1.1 %dynamic-slice_bitcast_fusion = (bf16[32,2048]{1,0:T(8,128)(2,1)S(1)}, bf16[32,2048]{1,0:T(8,128)(2,1)S(1)}, bf16[32,2048]{1,0:T(8,128)(2,1)S(1)}, bf16[32,2048]{1,0:T(8,128)(2,1)S(1)}) fusion(bf16[1,128,2048]{2,1,0:T(8,128)(2,1)} %param.11, s32[]{:T(128)S(6)} %select_n.12, s32[]{:T(128)S(6)} %select_n.11, bf16[1,128,2048]{2,1,0:T(8,128)(2,1)} %param.7), kind=kLoop, calls=%fused_computation.2 | loop fusion | bytes 1048584 | tf_op jit(solution)/shard_map/dynamic_slice | solution.py:457
  1.8 1.6 %collective-permute-start = (bf16[64,2048]{1,0:T(8,128)(2,1)S(1)}, bf16[64,2048]{1,0:T(8,128)(2,1)S(1)}, u32[]{:S(2)}, u32[]{:S(2)}) collective-permute-start(bf16[64,2048]{1,0:T(8,128)(2,1)S(1)} %pad_maximum_fusion), channel_id=1, source_target_pairs={{0,2},{2,0},{4,6},{6,4},{8,10},{10,8},{12,14},{14,12},{1,3},{3,1},... | collective-permute-start | bytes 786440 | tf_op jit(solution)/shard_map/ppermute | solution.py:444
  3.4 0.0 copy-start
  3.4 0.0 copy-start.1
  3.4 2.2 %collective-permute-start.1 = (bf16[64,2048]{1,0:T(8,128)(2,1)S(1)}, bf16[64,2048]{1,0:T(8,128)(2,1)S(1)}, u32[]{:S(2)}, u32[]{:S(2)}) collective-permute-start(bf16[64,2048]{1,0:T(8,128)(2,1)S(1)} %pad_maximum_fusion.1), channel_id=1, source_target_pairs={{2,4},{4,2},{6,8},{8,6},{10,12},{12,10},{3,5},{5,3},{7,9},{9,7},{1... | collective-permute-start | bytes 786440 | tf_op jit(solution)/shard_map/ppermute | solution.py:450
  5.6 0.0 copy-done.2
  5.7 0.0 copy-done.3
  5.7 3.1 %shard_map.94 = (f32[2,2048]{1,0:T(2,128)S(1)}, bf16[128,2048]{1,0:T(8,128)(2,1)S(1)}, bf16[128,2048]{1,0:T(8,128)(2,1)S(1)}, bf16[128,2048]{1,0:T(8,128)(2,1)S(1)}) custom-call(s32[1,33]{1,0:T(1,128)S(1)} %copy-done.2, s32[1,33]{1,0:T(1,128)S(1)} %copy-done.3, s32[1]{0:T(128)} %bitcast.refs_2_, bf16[128,2048]{1,0:T(8,128)(2,1)} %bitcast.30, ...), custom_call_target="tpu_custom_call" | custom-call | flops 400000000 | bytes 2000000 | tf_op jit(solution)/shard_map/pallas_call | solution.py:468
  8.8 3.1 %collective-permute-start.2 = (f32[2,2048]{1,0:T(2,128)S(1)}, f32[2,2048]{1,0:T(2,128)S(1)}, u32[]{:S(2)}, u32[]{:S(2)}) collective-permute-start(f32[2,2048]{1,0:T(2,128)S(1)} %get-tuple-element.25.refs_3_.refs_7_), channel_id=1, source_target_pairs={{0,2},{2,0},{4,6},{6,4},{8,10},{10,8},{12,14},{14,12},{1,3},{3,1},... | collective-permute-start | bytes 49160 | tf_op jit(solution)/shard_map/ppermute | solution.py:444
  11.9 1.9 %collective-permute-start.3 = (f32[2,2048]{1,0:T(2,128)S(1)}, f32[2,2048]{1,0:T(2,128)S(1)}, u32[]{:S(2)}, u32[]{:S(2)}) collective-permute-start(f32[2,2048]{1,0:T(2,128)S(1)} %get-tuple-element.25.refs_3_.refs_7_), channel_id=1, source_target_pairs={{2,4},{4,2},{6,8},{8,6},{10,12},{12,10},{3,5},{5,3},{7,9},{9,7},{1... | collective-permute-start | bytes 49160 | tf_op jit(solution)/shard_map/ppermute | solution.py:450
  13.8 0.0 copy-done
  13.8 0.0 copy-done.1
  13.8 4.4 %shard_map.95 = (bf16[128,2048]{1,0:T(8,128)(2,1)}, bf16[512,2048]{1,0:T(8,128)(2,1)}, bf16[512,2048]{1,0:T(8,128)(2,1)}, bf16[64,2048]{1,0:T(8,128)(2,1)S(1)}, ...) custom-call(s32[1,33]{1,0:T(1,128)S(1)} %copy-done.2, s32[1,33]{1,0:T(1,128)S(1)} %copy-done.3, ...), custom_call_target="tpu_custom_call" | custom-call | flops 2000000000 | bytes 4000000 | tf_op jit(solution)/shard_map/pallas_call | solution.py:477
  18.2 0.0 collective-permute-done.2.refs_6_
  18.2 0.2 collective-permute-done.3.refs_7_
  18.4 0.0 collective-permute-done.refs_4_.refs_3_
  18.4 0.0 collective-permute-done.1.refs_5_.refs_4_
  18.4 2.5 %shard_map.96 = (bf16[40,2048]{1,0:T(8,128)(2,1)S(1)}, bf16[40,2048]{1,0:T(8,128)(2,1)S(1)}, f32[2,2048]{1,0:T(2,128)S(1)}) custom-call(s32[1,33]{1,0:T(1,128)S(1)} %copy-done.2, s32[1,33]{1,0:T(1,128)S(1)} %copy-done.3, s32[1]{0:T(128)} %bitcast.refs_2_, bf16[64,2048]{1,0:T(8,128)(2,1)S(1)} %get-tuple-element.29.refs_3_.refs_12_, ...), custom_call_target="tpu_custom_call" | custom-call | flops 800000000 | bytes 3000000 | tf_op jit(solution)/shard_map/pallas_call | solution.py:488
  20.9 3.0 %collective-permute-start.4 = (bf16[40,2048]{1,0:T(8,128)(2,1)S(1)}, bf16[40,2048]{1,0:T(8,128)(2,1)S(1)}, u32[]{:S(2)}, u32[]{:S(2)}) collective-permute-start(bf16[40,2048]{1,0:T(8,128)(2,1)S(1)} %get-tuple-element.30), channel_id=1, source_target_pairs={{0,2},{2,0},{4,6},{6,4},{8,10},{10,8},{12,14},{14,12},{1,3},{3,1},... | collective-permute-start | bytes 491528 | tf_op jit(solution)/shard_map/ppermute | solution.py:444
  23.9 1.9 %collective-permute-start.5 = (bf16[40,2048]{1,0:T(8,128)(2,1)S(1)}, bf16[40,2048]{1,0:T(8,128)(2,1)S(1)}, u32[]{:S(2)}, u32[]{:S(2)}) collective-permute-start(bf16[40,2048]{1,0:T(8,128)(2,1)S(1)} %get-tuple-element.31), channel_id=1, source_target_pairs={{2,4},{4,2},{6,8},{8,6},{10,12},{12,10},{3,5},{5,3},{7,9},{9,7},{1... | collective-permute-start | bytes 491528 | tf_op jit(solution)/shard_map/ppermute | solution.py:450
  25.8 4.4 %shard_map.97 = (bf16[128,2048]{1,0:T(8,128)(2,1)}, bf16[512,2048]{1,0:T(8,128)(2,1)}, bf16[512,2048]{1,0:T(8,128)(2,1)}, bf16[64,2048]{1,0:T(8,128)(2,1)S(1)}, ...) custom-call(s32[1,33]{1,0:T(1,128)S(1)} %copy-done.2, ...), custom_call_target="tpu_custom_call", output_to_operand_aliasing={{0}: (9, {}), {1}: (10, {}), {2}: (11, {}), {3}: (12, {}), ... | custom-call | flops 2000000000 | bytes 4000000 | tf_op jit(solution)/shard_map/pallas_call | solution.py:477
  30.2 0.0 collective-permute-done.4.refs_5_
  30.2 1.8 %collective-permute-done.5.refs_6_ = bf16[40,2048]{1,0:T(8,128)(2,1)S(1)} collective-permute-done((bf16[40,2048]{1,0:T(8,128)(2,1)S(1)}, bf16[40,2048]{1,0:T(8,128)(2,1)S(1)}, u32[]{:S(2)}, u32[]{:S(2)}) %collective-permute-start.5) | collective-permute-done | bytes 163872 | tf_op jit(solution)/shard_map/ppermute | solution.py:450
  32.0 4.6 %shard_map.98 = (bf16[128,2048]{1,0:T(8,128)(2,1)}, bf16[512,2048]{1,0:T(8,128)(2,1)}, bf16[512,2048]{1,0:T(8,128)(2,1)}) custom-call(s32[1,33]{1,0:T(1,128)S(1)} %copy-done.2, s32[1,33]{1,0:T(1,128)S(1)} %copy-done.3, s32[1]{0:T(128)} %bitcast.refs_2_, ...), custom_call_target="tpu_custom_call", output_to_operand_aliasing={{0}: (16, {}), {1}: (17, {}), {2}: (18, {})} | custom-call | flops 1000000000 | bytes 6000000 | tf_op jit(solution)/shard_map/pallas_call | solution.py:498
  (2 shorter events, 0.0 us)
Async XLA Ops:
  0.6 5.0 %copy-start.2 = (s32[1,33]{1,0:T(1,128)S(1)}, s32[1,33]{1,0:T(1,128)}, u32[]{:S(2)}) copy-start(s32[1,33]{1,0:T(1,128)} %refs_0_.9) | copy-start | bytes 400
  0.6 5.0 %copy-start.3 = (s32[1,33]{1,0:T(1,128)S(1)}, s32[1,33]{1,0:T(1,128)}, u32[]{:S(2)}) copy-start(s32[1,33]{1,0:T(1,128)} %refs_1_.9) | copy-start | bytes 400
  1.8 16.5 %collective-permute-start = (bf16[64,2048]{1,0:T(8,128)(2,1)S(1)}, bf16[64,2048]{1,0:T(8,128)(2,1)S(1)}, u32[]{:S(2)}, u32[]{:S(2)}) collective-permute-start(bf16[64,2048]{1,0:T(8,128)(2,1)S(1)} %pad_maximum_fusion), channel_id=1, source_target_pairs={{0,2},{2,0},{4,6},{6,4},{8,10},{10,8},{12,14},{14,12},{1,3},{3,1},... | collective-permute-start | bytes 786440 | tf_op jit(solution)/shard_map/ppermute | solution.py:444
  3.4 10.3 %copy-start = (bf16[1,512,2048]{2,1,0:T(8,128)(2,1)S(1)}, bf16[1,512,2048]{2,1,0:T(8,128)(2,1)}, u32[]{:S(2)}) copy-start(bf16[1,512,2048]{2,1,0:T(8,128)(2,1)} %param.8) | copy-start | bytes 6291460
  3.4 10.4 %copy-start.1 = (bf16[1,512,2048]{2,1,0:T(8,128)(2,1)S(1)}, bf16[1,512,2048]{2,1,0:T(8,128)(2,1)}, u32[]{:S(2)}) copy-start(bf16[1,512,2048]{2,1,0:T(8,128)(2,1)} %param.9) | copy-start | bytes 6291460
  3.4 14.9 %collective-permute-start.1 = (bf16[64,2048]{1,0:T(8,128)(2,1)S(1)}, bf16[64,2048]{1,0:T(8,128)(2,1)S(1)}, u32[]{:S(2)}, u32[]{:S(2)}) collective-permute-start(bf16[64,2048]{1,0:T(8,128)(2,1)S(1)} %pad_maximum_fusion.1), channel_id=1, source_target_pairs={{2,4},{4,2},{6,8},{8,6},{10,12},{12,10},{3,5},{5,3},{7,9},{9,7},{1... | collective-permute-start | bytes 786440 | tf_op jit(solution)/shard_map/ppermute | solution.py:450
  8.8 9.4 %collective-permute-start.2 = (f32[2,2048]{1,0:T(2,128)S(1)}, f32[2,2048]{1,0:T(2,128)S(1)}, u32[]{:S(2)}, u32[]{:S(2)}) collective-permute-start(f32[2,2048]{1,0:T(2,128)S(1)} %get-tuple-element.25.refs_3_.refs_7_), channel_id=1, source_target_pairs={{0,2},{2,0},{4,6},{6,4},{8,10},{10,8},{12,14},{14,12},{1,3},{3,1},... | collective-permute-start | bytes 49160 | tf_op jit(solution)/shard_map/ppermute | solution.py:444
  11.9 6.5 %collective-permute-start.3 = (f32[2,2048]{1,0:T(2,128)S(1)}, f32[2,2048]{1,0:T(2,128)S(1)}, u32[]{:S(2)}, u32[]{:S(2)}) collective-permute-start(f32[2,2048]{1,0:T(2,128)S(1)} %get-tuple-element.25.refs_3_.refs_7_), channel_id=1, source_target_pairs={{2,4},{4,2},{6,8},{8,6},{10,12},{12,10},{3,5},{5,3},{7,9},{9,7},{1... | collective-permute-start | bytes 49160 | tf_op jit(solution)/shard_map/ppermute | solution.py:450
  20.9 9.3 %collective-permute-start.4 = (bf16[40,2048]{1,0:T(8,128)(2,1)S(1)}, bf16[40,2048]{1,0:T(8,128)(2,1)S(1)}, u32[]{:S(2)}, u32[]{:S(2)}) collective-permute-start(bf16[40,2048]{1,0:T(8,128)(2,1)S(1)} %get-tuple-element.30), channel_id=1, source_target_pairs={{0,2},{2,0},{4,6},{6,4},{8,10},{10,8},{12,14},{14,12},{1,3},{3,1},... | collective-permute-start | bytes 491528 | tf_op jit(solution)/shard_map/ppermute | solution.py:444
  23.9 8.1 %collective-permute-start.5 = (bf16[40,2048]{1,0:T(8,128)(2,1)S(1)}, bf16[40,2048]{1,0:T(8,128)(2,1)S(1)}, u32[]{:S(2)}, u32[]{:S(2)}) collective-permute-start(bf16[40,2048]{1,0:T(8,128)(2,1)S(1)} %get-tuple-element.31), channel_id=1, source_target_pairs={{2,4},{4,2},{6,8},{8,6},{10,12},{12,10},{3,5},{5,3},{7,9},{9,7},{1... | collective-permute-start | bytes 491528 | tf_op jit(solution)/shard_map/ppermute | solution.py:450

commit v3 on v2

v3 whole, which is shorter than its diff:
```python
import functools

import jax
import jax.numpy as jnp
from jax import lax
from jax.experimental import pallas as pl
from jax.experimental.pallas import tpu as pltpu
from jax.sharding import PartitionSpec as P

H = 32
HD = 64
LANES = 256
PER = LANES // HD

low = -1e30
high = 1e30
BATCH = 4


def dot_nt(a, b):
    return lax.dot_general(a, b, (((1,), (1,)), ((), ())), preferred_element_type=jnp.float32)


def dot_nn(a, b):
    return lax.dot_general(a, b, (((1,), (0,)), ((), ())), preferred_element_type=jnp.float32)


def dot_tn(a, b):
    return lax.dot_general(a, b, (((0,), (0,)), ((), ())), preferred_element_type=jnp.float32)


def spread(rows):
    head = lax.broadcasted_iota(jnp.int32, rows.shape, 1) // HD
    return jnp.concatenate([jnp.where(head == h, rows, jnp.zeros_like(rows)) for h in range(PER)], axis=0)


def gather_heads(full):
    slots = full.shape[0] // PER
    head = lax.broadcasted_iota(jnp.int32, (slots, full.shape[1]), 1) // HD
    out = full[:slots]
    for h in range(1, PER):
        out = jnp.where(head == h, full[h * slots : (h + 1) * slots], out)
    return out


def slot_of(slots):
    return lax.rem(lax.broadcasted_iota(jnp.int32, (1, PER * slots), 1), slots)


def row_dots(outs, spread_grads):
    slots = outs.shape[0]
    full = dot_nt(outs, spread_grads)
    row = lax.broadcasted_iota(jnp.int32, full.shape, 0)
    lane = lax.rem(lax.broadcasted_iota(jnp.int32, full.shape, 1), slots)
    return jnp.sum(jnp.where(row == lane, full, 0.0), axis=0, keepdims=True)


def log_add(a, b):
    top = jnp.maximum(a, b)
    return top + jnp.log(jnp.exp(a - top) + jnp.exp(b - top))


def row_ids(rows, lanes):
    return lax.broadcasted_iota(jnp.int32, (rows, lanes), 0)


def run_skewed(units):
    live, queue = [], list(units)
    while queue or live:
        if queue:
            live.append(queue.pop(0))
        for unit in list(live):
            try:
                next(unit)
            except StopIteration:
                live.remove(unit)


def each_group(groups, batch, units_of):
    @pl.loop(0, groups // batch)
    def _(at):
        units = []
        for c in range(batch):
            start = at * (batch * LANES) + c * LANES
            units += units_of(pl.ds(pl.multiple_of(start, LANES), LANES))
        run_skewed(units)


class Bounds:
    def __init__(self, shape, table):
        self.n_ex, self.gq, self.gk, self.count = shape
        self.dec_ref, self.enc_ref, pos_ref = table
        self.pos = pos_ref[0]
        self.even = lax.rem(self.pos, 2) == 0
        self.has_next = self.pos < self.count - 1

    def dec(self, i):
        return self.dec_ref[0, self.pos * self.n_ex + i] - self.pos * (self.n_ex * self.gq)

    def enc(self, i):
        return self.enc_ref[0, self.pos * self.n_ex + i] - self.pos * (self.n_ex * self.gk)

    def prior(self):
        at = jnp.maximum(self.pos * self.n_ex - 1, 0)
        rows = self.dec_ref[0, at] - self.pos * (self.n_ex * self.gq) + self.gq
        return jnp.where(self.pos > 0, rows, self.gq)

    def far_lanes(self, slot):
        hi = self.dec(self.n_ex) - self.n_ex * self.gq + self.gq
        return (slot >= self.prior()) & (slot < hi)

    def own_lanes(self, slot):
        lo = self.dec(self.n_ex - 1) - (self.n_ex - 1) * self.gq
        return (slot >= lo) & (slot < self.dec(0) + self.gq)


def edge_mask(bounds, s, far):
    gq, gk = bounds.gq, bounds.gk
    edge = gk // 2
    slot = slot_of(2 * gq)
    first = slot < gq
    in_a, in_b = (~first, first) if far else (first, ~first)
    row = row_ids(edge, LANES)
    a_lo = bounds.enc(bounds.n_ex - 1) - (bounds.n_ex - 1) * gk
    s0 = jnp.where(in_a & (row >= a_lo), s[:edge], low)
    s1 = jnp.where(in_a, s[edge:gk], low)
    s2 = jnp.where(in_b & (row < bounds.enc(0)), s[gk:], low)
    return s0, s1, s2


def exp_sum(s0, s1, s2):
    top = jnp.max(jnp.maximum(jnp.maximum(s0, s1), s2), axis=0, keepdims=True)
    e0, e1, e2 = jnp.exp(s0 - top), jnp.exp(s1 - top), jnp.exp(s2 - top)
    return top, e0, e1, e2, jnp.sum(e0 + e1 + e2, axis=0, keepdims=True)


def interior_kernel(shape, *refs):
    table, (_, q_ref, o_ref, g_ref, k_ref, v_ref), refs = refs[:3], refs[3:9], refs[9:]
    dq_out, dk_out, dv_out, dqe_ref, dke_ref, dve_ref, dq_buf, dk_buf, dv_buf, sems = refs
    bounds = Bounds(shape, table)
    n_ex, gq, gk = bounds.n_ex, bounds.gq, bounds.gk
    slots = 2 * gq
    edge = gk // 2
    win = gk + edge
    slot = slot_of(slots)
    bf16 = jnp.bfloat16

    def unit(i, cols, held):
        q0, k0 = i * gq, i * gk
        d_lo, d_hi = bounds.dec(i) - q0, bounds.dec(i + 1) - q0
        e_lo, e_hi = bounds.enc(i) - k0, bounds.enc(i + 1) - k0 - gk
        keys = k_ref[k0 : k0 + win, cols]
        qs = spread(q_ref[q0 : q0 + slots, cols])
        s = dot_nt(keys, qs)
        gs = spread(g_ref[q0 : q0 + slots, cols])
        dots = row_dots(o_ref[q0 : q0 + slots, cols], gs)
        dp = dot_nt(v_ref[k0 : k0 + win, cols], gs)
        yield
        row = row_ids(edge, LANES)
        s0 = jnp.where(row >= e_lo, s[:edge], low)
        s2 = jnp.where(row < e_hi, s[gk:], low)
        _, e0, e1, e2, total = exp_sum(s0, s[edge:gk], s2)
        yield
        inv = jnp.where((slot >= d_lo) & (slot < d_hi), 1.0 / total, 0.0)
        p = jnp.concatenate([e0, e1, e2], axis=0) * inv
        p_low = p.astype(bf16)
        yield
        dv = dot_nn(p_low, gs)
        ds = (p * (dp - dots)).astype(bf16)
        yield
        dk = dot_nn(ds, qs)
        dq = gather_heads(dot_tn(ds, keys))
        yield
        for which, (ref, ext, part) in enumerate(((dk_buf, dke_ref, dk), (dv_buf, dve_ref, dv))):
            first = part[:edge]
            if i > 0:
                first = first + held[(i - 1, which)]
                ref[k0 : k0 + edge, cols] = first.astype(bf16)
            else:
                ext[:edge, cols] = first.astype(bf16)
            ref[k0 + edge : k0 + gk, cols] = part[edge:gk].astype(bf16)
            if i < n_ex - 2:
                held[(i, which)] = part[gk:]
            else:
                ext[edge:, cols] = part[gk:].astype(bf16)
        first = dq[:gq]
        if i > 0:
            dq_buf[q0 : q0 + gq, cols] = (first + held[(i - 1, 2)]).astype(bf16)
        else:
            dqe_ref[:gq, cols] = first.astype(bf16)
        if i < n_ex - 2:
            held[(i, 2)] = dq[gq:]
        else:
            dqe_ref[gq:, cols] = dq[gq:].astype(bf16)
        yield

    def copies(at):
        cols = pl.ds(pl.multiple_of(at * (BATCH * LANES), LANES), BATCH * LANES)
        out = []
        k_rows, q_rows = pl.ds(edge, (n_ex - 1) * gk - edge), pl.ds(gq, (n_ex - 2) * gq)
        for j, (buf, ref, rows) in enumerate(((dk_buf, dk_out, k_rows), (dv_buf, dv_out, k_rows), (dq_buf, dq_out, q_rows))):
            out.append(pltpu.make_async_copy(buf.at[rows, cols], ref.at[rows, cols], sems.at[at, j]))
        return out

    @pl.loop(0, q_ref.shape[1] // LANES // BATCH)
    def _(at):
        units = []
        for c in range(BATCH):
            cols = pl.ds(pl.multiple_of(at * (BATCH * LANES) + c * LANES, LANES), LANES)
            held = {}
            units += [unit(i, cols, held) for i in range(n_ex - 1)]
        run_skewed(units)
        for copy in copies(at):
            copy.start()

    @pl.loop(0, q_ref.shape[1] // LANES // BATCH)
    def _(at):
        for copy in copies(at):
            copy.wait()


def three_parts(x):
    hi = x.astype(jnp.bfloat16).astype(jnp.float32)
    mid = (x - hi).astype(jnp.bfloat16).astype(jnp.float32)
    return [hi, mid, x - hi - mid]


def as_rows(parts):
    row = lax.broadcasted_iota(jnp.int32, (8, LANES), 0)
    out = jnp.zeros((8, LANES), jnp.float32)
    for i, part in enumerate(parts):
        out = jnp.where(row == i, part, out)
    return out.astype(jnp.bfloat16)


def stats_kernel(shape, pos_ref, dec_hbm, enc_hbm, q_hbm, o_hbm, g_hbm, k_hbm, me_ref, mo_ref, stat_ref, q_ref, o_ref, g_ref, k_ref, dec_ref, enc_ref, sems):
    bounds = Bounds(shape, (dec_ref, enc_ref, pos_ref))
    n_ex, gq, gk = bounds.n_ex, bounds.gq, bounds.gk
    edge = gk // 2
    last = (n_ex - 1) * gq
    at_e = pl.multiple_of(jnp.where(bounds.even, last, 0), gq)
    at_o = pl.multiple_of(jnp.where(bounds.even, 0, last), gq)

    jobs = [
        (dec_hbm, dec_ref, None, None), (enc_hbm, enc_ref, None, None),
        (k_hbm, k_ref, (n_ex - 1) * gk, (0, gk)), (k_hbm, k_ref, 0, (gk, edge)),
    ]
    for src, dst in ((q_hbm, q_ref), (g_hbm, g_ref), (o_hbm, o_ref)):
        jobs += [(src, dst, last, (last, gq)), (src, dst, 0, (0, gq))]
    first = len(jobs)
    jobs += [(q_hbm, me_ref, at_e, (0, gq)), (g_hbm, me_ref, at_e, (gq, gq)), (q_hbm, mo_ref, at_o, (0, gq)), (g_hbm, mo_ref, at_o, (gq, gq))]
    jobs += [(src, dst, gq, (gq, last - gq)) for src, dst in ((q_hbm, q_ref), (g_hbm, g_ref), (o_hbm, o_ref))]
    copies = []
    for i, (src, dst, at, to) in enumerate(jobs):
        if to is not None:
            src, dst = src.at[pl.ds(at, to[1])], dst.at[pl.ds(*to)]
        copies.append(pltpu.make_async_copy(src, dst, sems.at[i]))
    for copy in copies:
        copy.start()
    for copy in copies[:first]:
        copy.wait()

    def both(ref, cols):
        return jnp.concatenate([ref[last:, cols], ref[:gq, cols]], axis=0)

    def unit(cols):
        qs = spread(both(q_ref, cols))
        s = dot_nt(k_ref[:, cols], qs)
        yield
        dots = row_dots(both(o_ref, cols), spread(both(g_ref, cols)))
        yield
        top, _, _, _, total = exp_sum(*edge_mask(bounds, s, False))
        logs = top + jnp.log(total)
        stat_ref[0:1, cols] = logs
        stat_ref[1:2, cols] = dots
        rows = as_rows(three_parts(logs) + three_parts(dots))
        me_ref[2 * gq :, cols] = rows
        mo_ref[2 * gq :, cols] = rows
        yield

    each_group(q_ref.shape[1] // LANES, 4, lambda cols: [unit(cols)])
    for copy in copies[first:]:
        copy.wait()


def pick(flag, a, b):
    return jnp.where(flag, a, b)


def edge_rows(ref, cols, gk):
    return jnp.concatenate([ref[ref.shape[0] - gk :, cols], ref[: gk // 2, cols]], axis=0)


def remote_kernel(shape, *refs):
    *table, _, re_ref, ro_ref, k_ref, v_ref, me_ref, mo_ref, p_ref, ds_ref = refs
    bounds = Bounds(shape, table)
    gq, gk = bounds.gq, bounds.gk
    even = bounds.even
    slot = slot_of(2 * gq)
    bf16, f32 = jnp.bfloat16, jnp.float32

    def unit(cols):
        re, ro = re_ref[: 2 * gq, cols], ro_ref[: 2 * gq, cols]
        before, after = pick(even, ro, re), pick(even, re, ro)
        qs = spread(jnp.concatenate([before[:gq], after[:gq]], axis=0))
        keys = edge_rows(k_ref, cols, gk)
        s = dot_nt(keys, qs)
        gs = spread(jnp.concatenate([before[gq:], after[gq:]], axis=0))
        dp = dot_nt(edge_rows(v_ref, cols, gk), gs)
        yield
        te, to = re_ref[2 * gq :, cols].astype(f32), ro_ref[2 * gq :, cols].astype(f32)
        tbefore, tafter = pick(even, to, te), pick(even, te, to)
        stat = jnp.where(slot < gq, tbefore, tafter)
        top, e0, e1, e2, total = exp_sum(*edge_mask(bounds, s, True))
        mine = top + jnp.log(total)
        yield
        whole = log_add(mine, stat[0:1] + stat[1:2] + stat[2:3])
        dots = stat[3:4] + stat[4:5] + stat[5:6]
        scale = jnp.where(bounds.far_lanes(slot), jnp.exp(top - whole), 0.0)
        p = jnp.concatenate([e0, e1, e2], axis=0) * scale
        ds = (p * (dp - dots)).astype(bf16)
        p_ref[:, cols] = p.astype(bf16)
        ds_ref[:, cols] = ds
        yield
        dq = gather_heads(dot_tn(ds, keys)).astype(bf16)
        logs = as_rows(three_parts(mine))
        yield
        me_ref[:gq, cols] = pick(even, dq[gq:], dq[:gq])
        mo_ref[:gq, cols] = pick(even, dq[:gq], dq[gq:])
        me_ref[gq:, cols] = logs
        mo_ref[gq:, cols] = logs
        yield

    each_group(re_ref.shape[1] // LANES, 4, lambda cols: [unit(cols)])


def ready_kernel(shape, *refs):
    *table, re_ref, ro_ref, own_ref, q_ref, g_ref, k_ref, v_ref, p_far, ds_far, dke_ref, dve_ref, p_ref, ds_ref, dk_ref, dv_ref = refs
    bounds = Bounds(shape, table)
    gq, gk = bounds.gq, bounds.gk
    edge = gk // 2
    even = bounds.even
    slot = slot_of(2 * gq)
    f32 = jnp.float32

    def far_unit(cols):
        re, ro = re_ref[: 2 * gq, cols], ro_ref[: 2 * gq, cols]
        before, after = pick(even, ro, re), pick(even, re, ro)
        gs = spread(jnp.concatenate([before[gq:], after[gq:]], axis=0))
        dv = dot_nn(p_far[:, cols], gs)
        yield
        qs = spread(jnp.concatenate([before[:gq], after[:gq]], axis=0))
        dk = dot_nn(ds_far[:, cols], qs)
        yield
        for ref, ext, part in ((dv_ref, dve_ref, dv), (dk_ref, dke_ref, dk)):
            ref[:edge, cols] = part[:edge] + ext[edge:, cols].astype(f32)
            ref[edge:gk, cols] = part[edge:gk]
            ref[gk:, cols] = part[gk:] + ext[:edge, cols].astype(f32)
        yield

    def own_unit(cols):
        qs = spread(both(q_ref, cols))
        s = dot_nt(edge_rows(k_ref, cols, gk), qs)
        gs = spread(both(g_ref, cols))
        dp = dot_nt(edge_rows(v_ref, cols, gk), gs)
        yield
        logs = jnp.where(bounds.own_lanes(slot), own_ref[0:1, cols], high)
        p = jnp.exp(jnp.concatenate(edge_mask(bounds, s, False), axis=0) - logs)
        p_ref[:, cols] = p
        yield
        ds_ref[:, cols] = p * (dp - own_ref[1:2, cols])
        yield

    def both(ref, cols):
        return jnp.concatenate([ref[ref.shape[0] - gq :, cols], ref[:gq, cols]], axis=0)

    each_group(re_ref.shape[1] // LANES, 4, lambda cols: [own_unit(cols), far_unit(cols)])


def edge_kernel(shape, *refs):
    *table, me_ref, mo_ref, own_ref, q_ref, g_ref, k_ref, p_ref, ds_ref, dka_ref, dva_ref, dqe_ref = refs[:14]
    _, _, _, dq_out, dk_out, dv_out, dq_buf, dk_buf, dv_buf, sems = refs[14:]
    bounds = Bounds(shape, table)
    n_ex, gq, gk = bounds.n_ex, bounds.gq, bounds.gk
    edge = gk // 2
    even = bounds.even
    slot = slot_of(2 * gq)
    bf16, f32 = jnp.bfloat16, jnp.float32
    last_q, last_k = (n_ex - 1) * gq, (n_ex - 1) * gk

    def both(ref, cols):
        return jnp.concatenate([ref[last_q:, cols], ref[:gq, cols]], axis=0)

    def unit(cols):
        me, mo = me_ref[gq:, cols].astype(f32), mo_ref[gq:, cols].astype(f32)
        before, after = pick(even, mo, me), pick(even, me, mo)
        before = before[0:1] + before[1:2] + before[2:3]
        after = jnp.where(bounds.has_next, after[0:1] + after[1:2] + after[2:3], low)
        own = own_ref[0:1, cols]
        share = jnp.exp(own - log_add(own, jnp.where(slot < gq, after, before)))
        share = jnp.where(bounds.own_lanes(slot), share, 0.0)
        gs = spread(both(g_ref, cols))
        dv = dot_nn((p_ref[:, cols] * share).astype(bf16), gs)
        yield
        qs = spread(both(q_ref, cols))
        ds = (ds_ref[:, cols] * share).astype(bf16)
        dk = dot_nn(ds, qs)
        yield
        dq = gather_heads(dot_tn(ds, edge_rows(k_ref, cols, gk)))
        yield
        dv_buf[:, cols] = (dv + dva_ref[:, cols]).astype(bf16)
        dk_buf[:, cols] = (dk + dka_ref[:, cols]).astype(bf16)
        me, mo = me_ref[:gq, cols].astype(f32), mo_ref[:gq, cols].astype(f32)
        before, after = pick(even, mo, me), pick(even, me, mo)
        dq_buf[:gq, cols] = (dq[gq:] + before + dqe_ref[:gq, cols].astype(f32)).astype(bf16)
        dq_buf[gq:, cols] = (dq[:gq] + after + dqe_ref[gq:, cols].astype(f32)).astype(bf16)
        yield

    def copies(at):
        cols = pl.ds(pl.multiple_of(at * (BATCH * LANES), LANES), BATCH * LANES)
        moves = []
        for buf, ref in ((dk_buf, dk_out), (dv_buf, dv_out)):
            moves += [(buf, (0, gk), ref, (last_k, gk)), (buf, (gk, edge), ref, (0, edge))]
        moves += [(dq_buf, (0, gq), dq_out, (0, gq)), (dq_buf, (gq, gq), dq_out, (last_q, gq))]
        return [
            pltpu.make_async_copy(src.at[pl.ds(*a), cols], dst.at[pl.ds(*b), cols], sems.at[at, j])
            for j, (src, a, dst, b) in enumerate(moves)
        ]

    turns = q_ref.shape[1] // LANES // BATCH

    @pl.loop(0, turns)
    def _(at):
        units = []
        for c in range(BATCH):
            units.append(unit(pl.ds(pl.multiple_of(at * (BATCH * LANES) + c * LANES, LANES), LANES)))
        run_skewed(units)
        for copy in copies(at):
            copy.start()

    @pl.loop(0, turns)
    def _(at):
        for copy in copies(at):
            copy.wait()


inside = pl.BlockSpec(memory_space=pltpu.VMEM)
anywhere = pl.BlockSpec(memory_space=pl.ANY)
off_chip = pl.BlockSpec(memory_space=pltpu.HBM)
scalars = pl.BlockSpec(memory_space=pltpu.SMEM)


def call(kernel, ins, outs, scratch=(), aliases=None, flops=0, nbytes=0):
    return pl.pallas_call(
        kernel,
        out_shape=[shape for _, shape in outs],
        in_specs=list(ins),
        out_specs=[spec for spec, _ in outs],
        scratch_shapes=list(scratch),
        input_output_aliases=aliases or {},
        compiler_params=pltpu.CompilerParams(vmem_limit_bytes=40 * 1024 * 1024),
        cost_estimate=pl.CostEstimate(flops=flops, bytes_accessed=nbytes, transcendentals=0),
    )


def shards(dec_query, enc_key, enc_value, saved_out, d_out, dec_start, enc_start):
    q, k, v, o, g = dec_query[0], enc_key[0], enc_value[0], saved_out[0], d_out[0]
    q_rows, feats = q.shape
    k_rows = k.shape[0]
    pos = lax.axis_index("seq")
    count = lax.axis_size("seq")
    n_ex = (dec_start.shape[1] - 1) // count
    gq, gk = q_rows // n_ex, k_rows // n_ex
    edge = gk // 2
    groups = feats // LANES
    bf16, f32 = jnp.bfloat16, jnp.float32
    shape = (n_ex, gq, gk, count)

    def swap_even(x):
        return lax.ppermute(x, "seq", [(i, i ^ 1) for i in range(count) if i ^ 1 < count])

    def swap_odd(x):
        pairs = []
        for i in range(1, count - 1, 2):
            pairs += [(i, i + 1), (i + 1, i)]
        return lax.ppermute(x, "seq", pairs)

    place = pos.astype(jnp.int32)[None]
    table = (dec_start, enc_start, place)
    tables = [scalars] * 3

    def like(rows, kind=bf16):
        return jax.ShapeDtypeStruct((rows, feats), kind)

    def vmem(rows):
        return pltpu.VMEM((rows, feats), bf16)

    def out(rows, kind=bf16):
        return (inside, like(rows, kind))

    placed = (pltpu.with_memory_space_constraint(x, pltpu.HBM) for x in (dec_start, enc_start, q, o, g, k))
    raw_e, raw_o, own, q, o, g = call(
        functools.partial(stats_kernel, shape), [scalars] + [off_chip] * 6,
        [out(2 * gq + 8)] * 2 + [out(2, f32)] + [out(q_rows)] * 3,
        scratch=[vmem(gk + edge), pltpu.SMEM(dec_start.shape, jnp.int32), pltpu.SMEM(enc_start.shape, jnp.int32), pltpu.SemaphoreType.DMA((17,))],
        flops=int(4e8), nbytes=int(2e6),
    )(place, *placed)
    raw_e, raw_o = swap_even(raw_e), swap_odd(raw_o)

    big = [(anywhere, like(q_rows)), (anywhere, like(k_rows)), (anywhere, like(k_rows))]
    dq, dk, dv, dqe, dke, dve = call(
        functools.partial(interior_kernel, shape), tables + [anywhere] + [inside] * 5,
        big + [out(2 * gq), out(gk), out(gk)],
        scratch=[vmem(q_rows), vmem(k_rows), vmem(k_rows), pltpu.SemaphoreType.DMA((groups // BATCH, 3))],
        flops=int(4e9), nbytes=int(8e6),
    )(*table, own, q, o, g, k, v)

    to_e, to_o, p_far, ds_far = call(
        functools.partial(remote_kernel, shape), tables + [anywhere] + [inside] * 4,
        [out(gq + 8)] * 2 + [out(gk + edge)] * 2,
        flops=int(8e8), nbytes=int(3e6),
    )(*table, dqe, raw_e, raw_o, k, v)
    back_e, back_o = swap_even(to_e), swap_odd(to_o)

    p_own, ds_own, dka, dva = call(
        functools.partial(ready_kernel, shape), tables + [inside] * 11, [out(gk + edge, f32)] * 4,
        flops=int(1e9), nbytes=int(6e6),
    )(*table, raw_e, raw_o, own, q, g, k, v, p_far, ds_far, dke, dve)
    dq, dk, dv = call(
        functools.partial(edge_kernel, shape), tables + [inside] * 11 + [anywhere] * 3, big,
        scratch=[vmem(2 * gq), vmem(gk + edge), vmem(gk + edge), pltpu.SemaphoreType.DMA((groups // BATCH, 6))],
        aliases={14: 0, 15: 1, 16: 2},
        flops=int(1e9), nbytes=int(6e6),
    )(*table, back_e, back_o, own, q, g, k, p_own, ds_own, dka, dva, dqe, dq, dk, dv)
    return dq[None], dk[None], dv[None]


def solution(mesh):
    spec = P(("grp", "dp"), "seq", None)
    return jax.shard_map(
        shards,
        mesh=mesh,
        in_specs=(spec,) * 5 + (P(("grp", "dp"), None),) * 2,
        out_specs=(spec,) * 3,
        check_vma=False,
    )
```

time: 36.8 us -> 33.9 us (0.921)
  the two profiles are of different devices: /device:TPU:8 before, /device:TPU:16 now
where the time goes in v3:
time: 33.9 us; the launch traced here: 33.7 us
  Pallas kernels  18.4 us (54%)
  starting transfers between devices  7.75 us (23%)
  waiting for transfers between devices  5.27 us (16%)
  local copies, waits for them, and re-layouts  1.6 us (5%)
  between operations  0.74 us (2%)
    pallas_call x1, Pallas kernels, shards(): call(functools.partial(interior_kernel, shape), tables + [anywhere] + [in...  6.98 us
    ppermute x2, starting transfers between devices, swap_odd(): return lax.ppermute(x, 'seq', pairs)  4.58 us
    ppermute x2, waiting for transfers between devices, swap_even(): lax.ppermute(x, 'seq', [(i, i ^ 1) for i in range(count) if i ^ 1 < count])  3.55 us
    ppermute x2, starting transfers between devices, swap_even(): lax.ppermute(x, 'seq', [(i, i ^ 1) for i in range(count) if i ^ 1 < count])  3.17 us
    pallas_call x1, Pallas kernels, shards(): call(functools.partial(ready_kernel, shape), tables + [inside] * 11, [out...  3.17 us
    pallas_call x1, Pallas kernels, shards(): call(functools.partial(stats_kernel, shape), [scalars] + [off_chip] * 6,...  2.79 us
    pallas_call x1, Pallas kernels, shards(): call(functools.partial(edge_kernel, shape), tables + [inside] * 11 + [any...  2.76 us
    pallas_call x1, Pallas kernels, shards(): call(functools.partial(remote_kernel, shape), tables + [anywhere] + [insi...  2.68 us
  transfers between devices with their start and end apart: 4, of which 3 were waited for; matrix products, arithmetic and copies ran while one was open for 0% of the time, Pallas kernels for 30%

profile of v3, /device:TPU:16, one launch (start us, length us, event | category | flops | bytes accessed | tf_op | source)
XLA Modules:
  0.0 33.7 jit_solution(8291813082469577976)
XLA Ops:
  0.6 0.0 copy-start.3
  0.6 0.0 copy-start.2
  0.7 0.0 copy-start
  0.7 2.8 %shard_map.94 = (bf16[72,2048]{1,0:T(8,128)(2,1)S(1)}, bf16[72,2048]{1,0:T(8,128)(2,1)S(1)}, f32[2,2048]{1,0:T(2,128)S(1)}, bf16[128,2048]{1,0:T(8,128)(2,1)S(1)...) custom-call(s32[1]{0:T(128)} %bitcast.pos_ref.refs_2_, s32[1,33]{1,0:T(1,128)} %refs_0_.7, ...), custom_call_target="tpu_custom_call" | custom-call | flops 400000000 | bytes 2000000 | tf_op jit(solution)/shard_map/pallas_call | solution.py:502
  3.5 1.6 %collective-permute-start = (bf16[72,2048]{1,0:T(8,128)(2,1)S(1)}, bf16[72,2048]{1,0:T(8,128)(2,1)S(1)}, u32[]{:S(2)}, u32[]{:S(2)}) collective-permute-start(bf16[72,2048]{1,0:T(8,128)(2,1)S(1)} %get-tuple-element.31), channel_id=1, source_target_pairs={{0,2},{2,0},{4,6},{6,4},{8,10},{10,8},{12,14},{14,12},{1,3},{3,1},... | collective-permute-start | bytes 884744 | tf_op jit(solution)/shard_map/ppermute | solution.py:480
  5.0 2.3 %collective-permute-start.1 = (bf16[72,2048]{1,0:T(8,128)(2,1)S(1)}, bf16[72,2048]{1,0:T(8,128)(2,1)S(1)}, u32[]{:S(2)}, u32[]{:S(2)}) collective-permute-start(bf16[72,2048]{1,0:T(8,128)(2,1)S(1)} %get-tuple-element.32), channel_id=1, source_target_pairs={{2,4},{4,2},{6,8},{8,6},{10,12},{12,10},{3,5},{5,3},{7,9},{9,7},{1... | collective-permute-start | bytes 884744 | tf_op jit(solution)/shard_map/ppermute | solution.py:486
  7.3 0.0 copy-done.3
  7.4 0.0 copy-done.2
  7.4 0.0 copy-done
  7.4 0.0 copy-start.1
  7.4 1.6 %copy-done.1 = bf16[1,512,2048]{2,1,0:T(8,128)(2,1)S(1)} copy-done((bf16[1,512,2048]{2,1,0:T(8,128)(2,1)S(1)}, bf16[1,512,2048]{2,1,0:T(8,128)(2,1)}, u32[]{:S(2)}) %copy-start.1) | copy-done | bytes 2097176
  9.0 7.0 %shard_map.95 = (bf16[128,2048]{1,0:T(8,128)(2,1)}, bf16[512,2048]{1,0:T(8,128)(2,1)}, bf16[512,2048]{1,0:T(8,128)(2,1)}, bf16[64,2048]{1,0:T(8,128)(2,1)S(1)}, ...) custom-call(s32[1,33]{1,0:T(1,128)S(1)} %copy-done.2, s32[1,33]{1,0:T(1,128)S(1)} %copy-done.3, ...), custom_call_target="tpu_custom_call" | custom-call | flops 4000000000 | bytes 8000000 | tf_op jit(solution)/shard_map/pallas_call | solution.py:511
  16.0 2.6 %collective-permute-done.refs_4_.refs_3_ = bf16[72,2048]{1,0:T(8,128)(2,1)S(1)} collective-permute-done((bf16[72,2048]{1,0:T(8,128)(2,1)S(1)}, bf16[72,2048]{1,0:T(8,128)(2,1)S(1)}, u32[]{:S(2)}, u32[]{:S(2)}) %collective-permute-start) | collective-permute-done | bytes 294944 | tf_op jit(solution)/shard_map/ppermute | solution.py:480
  18.6 0.0 collective-permute-done.1.refs_5_.refs_4_
  18.6 2.7 %shard_map.96 = (bf16[40,2048]{1,0:T(8,128)(2,1)S(1)}, bf16[40,2048]{1,0:T(8,128)(2,1)S(1)}, bf16[192,2048]{1,0:T(8,128)(2,1)S(1)}, bf16[192,2048]{1,0:T(8,128)(2,1)S(1)}) custom-call(s32[1,33]{1,0:T(1,128)S(1)} %copy-done.2, s32[1,33]{1,0:T(1,128)S(1)} %copy-done.3, s32[1]{0:T(128)} %bitcast.pos_ref.refs_2_, ...), custom_call_target="tpu_custom_call" | custom-call | flops 800000000 | bytes 3000000 | tf_op jit(solution)/shard_map/pallas_call | solution.py:518
  21.3 1.6 %collective-permute-start.2 = (bf16[40,2048]{1,0:T(8,128)(2,1)S(1)}, bf16[40,2048]{1,0:T(8,128)(2,1)S(1)}, u32[]{:S(2)}, u32[]{:S(2)}) collective-permute-start(bf16[40,2048]{1,0:T(8,128)(2,1)S(1)} %get-tuple-element.33), channel_id=1, source_target_pairs={{0,2},{2,0},{4,6},{6,4},{8,10},{10,8},{12,14},{14,12},{1,3},{3,1},... | collective-permute-start | bytes 491528 | tf_op jit(solution)/shard_map/ppermute | solution.py:480
  22.9 2.3 %collective-permute-start.3 = (bf16[40,2048]{1,0:T(8,128)(2,1)S(1)}, bf16[40,2048]{1,0:T(8,128)(2,1)S(1)}, u32[]{:S(2)}, u32[]{:S(2)}) collective-permute-start(bf16[40,2048]{1,0:T(8,128)(2,1)S(1)} %get-tuple-element.34), channel_id=1, source_target_pairs={{2,4},{4,2},{6,8},{8,6},{10,12},{12,10},{3,5},{5,3},{7,9},{9,7},{1... | collective-permute-start | bytes 491528 | tf_op jit(solution)/shard_map/ppermute | solution.py:486
  25.2 3.2 %shard_map.97 = (f32[192,2048]{1,0:T(8,128)S(1)}, f32[192,2048]{1,0:T(8,128)S(1)}, f32[192,2048]{1,0:T(8,128)S(1)}, f32[192,2048]{1,0:T(8,128)S(1)}) custom-call(s32[1,33]{1,0:T(1,128)S(1)} %copy-done.2, s32[1,33]{1,0:T(1,128)S(1)} %copy-done.3, s32[1]{0:T(128)} %bitcast.pos_ref.refs_2_, bf16[72,2048]{1,0:T(8,128)(2,1)S(1)} %collective-permute-done.refs_4_.refs_3_, ...), custom_call_target="tpu_custom_call" | custom-call | flops 1000000000 | bytes 6000000 | tf_op jit(solution)/shard_map/pallas_call | solution.py:525
  28.3 0.9 %collective-permute-done.2.refs_3_ = bf16[40,2048]{1,0:T(8,128)(2,1)S(1)} collective-permute-done((bf16[40,2048]{1,0:T(8,128)(2,1)S(1)}, bf16[40,2048]{1,0:T(8,128)(2,1)S(1)}, u32[]{:S(2)}, u32[]{:S(2)}) %collective-permute-start.2) | collective-permute-done | bytes 163872 | tf_op jit(solution)/shard_map/ppermute | solution.py:480
  29.3 1.7 %collective-permute-done.3.refs_4_ = bf16[40,2048]{1,0:T(8,128)(2,1)S(1)} collective-permute-done((bf16[40,2048]{1,0:T(8,128)(2,1)S(1)}, bf16[40,2048]{1,0:T(8,128)(2,1)S(1)}, u32[]{:S(2)}, u32[]{:S(2)}) %collective-permute-start.3) | collective-permute-done | bytes 163872 | tf_op jit(solution)/shard_map/ppermute | solution.py:486
  31.0 2.8 %shard_map.98 = (bf16[128,2048]{1,0:T(8,128)(2,1)}, bf16[512,2048]{1,0:T(8,128)(2,1)}, bf16[512,2048]{1,0:T(8,128)(2,1)}) custom-call(s32[1,33]{1,0:T(1,128)S(1)} %copy-done.2, s32[1,33]{1,0:T(1,128)S(1)} %copy-done.3, s32[1]{0:T(128)} %bitcast.pos_ref.refs_2_, ...), custom_call_target="tpu_custom_call", output_to_operand_aliasing={{0}: (14, {}), {1}: (15, {}), {2}: (16, {})} | custom-call | flops 1000000000 | bytes 6000000 | tf_op jit(solution)/shard_map/pallas_call | solution.py:529
Async XLA Ops:
  0.6 6.7 %copy-start.3 = (s32[1,33]{1,0:T(1,128)S(1)}, s32[1,33]{1,0:T(1,128)}, u32[]{:S(2)}) copy-start(s32[1,33]{1,0:T(1,128)} %refs_1_.7) | copy-start | bytes 400
  0.6 6.7 %copy-start.2 = (s32[1,33]{1,0:T(1,128)S(1)}, s32[1,33]{1,0:T(1,128)}, u32[]{:S(2)}) copy-start(s32[1,33]{1,0:T(1,128)} %refs_0_.7) | copy-start | bytes 400
  0.7 6.7 %copy-start = (bf16[1,512,2048]{2,1,0:T(8,128)(2,1)S(1)}, bf16[1,512,2048]{2,1,0:T(8,128)(2,1)}, u32[]{:S(2)}) copy-start(bf16[1,512,2048]{2,1,0:T(8,128)(2,1)} %param.8) | copy-start | bytes 6291460
  3.5 15.1 %collective-permute-start = (bf16[72,2048]{1,0:T(8,128)(2,1)S(1)}, bf16[72,2048]{1,0:T(8,128)(2,1)S(1)}, u32[]{:S(2)}, u32[]{:S(2)}) collective-permute-start(bf16[72,2048]{1,0:T(8,128)(2,1)S(1)} %get-tuple-element.31), channel_id=1, source_target_pairs={{0,2},{2,0},{4,6},{6,4},{8,10},{10,8},{12,14},{14,12},{1,3},{3,1},... | collective-permute-start | bytes 884744 | tf_op jit(solution)/shard_map/ppermute | solution.py:480
  5.0 13.6 %collective-permute-start.1 = (bf16[72,2048]{1,0:T(8,128)(2,1)S(1)}, bf16[72,2048]{1,0:T(8,128)(2,1)S(1)}, u32[]{:S(2)}, u32[]{:S(2)}) collective-permute-start(bf16[72,2048]{1,0:T(8,128)(2,1)S(1)} %get-tuple-element.32), channel_id=1, source_target_pairs={{2,4},{4,2},{6,8},{8,6},{10,12},{12,10},{3,5},{5,3},{7,9},{9,7},{1... | collective-permute-start | bytes 884744 | tf_op jit(solution)/shard_map/ppermute | solution.py:486
  7.4 1.6 %copy-start.1 = (bf16[1,512,2048]{2,1,0:T(8,128)(2,1)S(1)}, bf16[1,512,2048]{2,1,0:T(8,128)(2,1)}, u32[]{:S(2)}) copy-start(bf16[1,512,2048]{2,1,0:T(8,128)(2,1)} %param.9) | copy-start | bytes 6291460
  21.3 8.0 %collective-permute-start.2 = (bf16[40,2048]{1,0:T(8,128)(2,1)S(1)}, bf16[40,2048]{1,0:T(8,128)(2,1)S(1)}, u32[]{:S(2)}, u32[]{:S(2)}) collective-permute-start(bf16[40,2048]{1,0:T(8,128)(2,1)S(1)} %get-tuple-element.33), channel_id=1, source_target_pairs={{0,2},{2,0},{4,6},{6,4},{8,10},{10,8},{12,14},{14,12},{1,3},{3,1},... | collective-permute-start | bytes 491528 | tf_op jit(solution)/shard_map/ppermute | solution.py:480
  22.9 8.1 %collective-permute-start.3 = (bf16[40,2048]{1,0:T(8,128)(2,1)S(1)}, bf16[40,2048]{1,0:T(8,128)(2,1)S(1)}, u32[]{:S(2)}, u32[]{:S(2)}) collective-permute-start(bf16[40,2048]{1,0:T(8,128)(2,1)S(1)} %get-tuple-element.34), channel_id=1, source_target_pairs={{2,4},{4,2},{6,8},{8,6},{10,12},{12,10},{3,5},{5,3},{7,9},{9,7},{1... | collective-permute-start | bytes 491528 | tf_op jit(solution)/shard_map/ppermute | solution.py:486

commit v4 on v3

v4 whole, which is shorter than its diff:
```python
import functools

import jax
import jax.numpy as jnp
from jax import lax
from jax.experimental import pallas as pl
from jax.experimental.pallas import tpu as pltpu
from jax.sharding import PartitionSpec as P

H = 32
HD = 64
LANES = 256
PER = LANES // HD

low = -1e30
high = 1e30
BATCH = 4


def dot_nt(a, b):
    return lax.dot_general(a, b, (((1,), (1,)), ((), ())), preferred_element_type=jnp.float32)


def dot_nn(a, b):
    return lax.dot_general(a, b, (((1,), (0,)), ((), ())), preferred_element_type=jnp.float32)


def dot_tn(a, b):
    return lax.dot_general(a, b, (((0,), (0,)), ((), ())), preferred_element_type=jnp.float32)


def spread(rows):
    half = LANES // 2
    side = lax.broadcasted_iota(jnp.int32, (rows.shape[0], half), 1) // HD
    empty = jnp.zeros((rows.shape[0], half), rows.dtype)
    out = []
    for h in range(PER):
        at, within = divmod(h * HD, half)
        piece = jnp.where(side == within // HD, rows[:, at * half : (at + 1) * half], empty)
        out.append(jnp.concatenate([piece if at == x else empty for x in range(LANES // half)], axis=1))
    return jnp.concatenate(out, axis=0)


def gather_heads(full):
    slots, half = full.shape[0] // PER, LANES // 2
    side = lax.broadcasted_iota(jnp.int32, (slots, half), 1) // HD
    out = []
    for at in range(LANES // half):
        lanes = slice(at * half, (at + 1) * half)
        heads = [h for h in range(PER) if h * HD // half == at]
        part = full[heads[0] * slots : (heads[0] + 1) * slots, lanes]
        for n, h in enumerate(heads[1:], 1):
            part = jnp.where(side == n, full[h * slots : (h + 1) * slots, lanes], part)
        out.append(part)
    return jnp.concatenate(out, axis=1)


def slot_of(slots):
    return lax.rem(lax.broadcasted_iota(jnp.int32, (1, PER * slots), 1), slots)


def row_dots(outs, spread_grads):
    slots = outs.shape[0]
    full = dot_nt(outs, spread_grads)
    row = lax.broadcasted_iota(jnp.int32, full.shape, 0)
    lane = lax.rem(lax.broadcasted_iota(jnp.int32, full.shape, 1), slots)
    return jnp.sum(jnp.where(row == lane, full, 0.0), axis=0, keepdims=True)


def log_add(a, b):
    top = jnp.maximum(a, b)
    return top + jnp.log(jnp.exp(a - top) + jnp.exp(b - top))


def row_ids(rows, lanes):
    return lax.broadcasted_iota(jnp.int32, (rows, lanes), 0)


def run_skewed(units):
    live, queue = [], list(units)
    while queue or live:
        if queue:
            live.append(queue.pop(0))
        for unit in list(live):
            try:
                next(unit)
            except StopIteration:
                live.remove(unit)


def each_group(groups, batch, units_of, after=None):
    @pl.loop(0, groups // batch)
    def _(at):
        units = []
        for c in range(batch):
            units += units_of(Group(at * batch, c))
        run_skewed(units)
        if after is not None:
            after(at)


class Group:
    def __init__(self, base, c):
        self.base, self.c = base, c
        self.cols = self.lanes(LANES)

    def lanes(self, width):
        return pl.ds(pl.multiple_of(self.base * width + self.c * width, width), width)

    def row(self, per, i):
        return pl.ds(pl.multiple_of(self.base * per, per) + (self.c * per + i), 1)


class Bounds:
    def __init__(self, shape, table):
        self.n_ex, self.gq, self.gk, self.count = shape
        self.dec_ref, self.enc_ref, pos_ref = table
        self.pos = pos_ref[0]
        self.even = lax.rem(self.pos, 2) == 0
        self.has_next = self.pos < self.count - 1

    def dec(self, i):
        return self.dec_ref[0, self.pos * self.n_ex + i] - self.pos * (self.n_ex * self.gq)

    def enc(self, i):
        return self.enc_ref[0, self.pos * self.n_ex + i] - self.pos * (self.n_ex * self.gk)

    def prior(self):
        at = jnp.maximum(self.pos * self.n_ex - 1, 0)
        rows = self.dec_ref[0, at] - self.pos * (self.n_ex * self.gq) + self.gq
        return jnp.where(self.pos > 0, rows, self.gq)

    def far_lanes(self, side, slot):
        return slot < self.dec(self.n_ex) - self.n_ex * self.gq if side == 0 else slot >= self.prior()

    def own_lanes(self, side, slot):
        return slot >= self.dec(self.n_ex - 1) - (self.n_ex - 1) * self.gq if side == 0 else slot < self.dec(0)

    def edge_mask(self, side, s):
        edge = self.gk // 2
        row = row_ids(edge, s.shape[1])
        if side == 1:
            return jnp.where(row < self.enc(0), s, low)
        first = self.enc(self.n_ex - 1) - (self.n_ex - 1) * self.gk
        return jnp.concatenate([jnp.where(row >= first, s[:edge], low), s[edge:]], axis=0)

    def edge_rows(self, side, ref, cols):
        return ref[ref.shape[0] - self.gk :, cols] if side == 0 else ref[: self.gk // 2, cols]

    def own_rows(self, side, ref, cols):
        return ref[ref.shape[0] - self.gq :, cols] if side == 0 else ref[: self.gq, cols]

    def part(self, side):
        return slice(0, self.gk) if side == 0 else slice(self.gk, self.gk + self.gk // 2)

    def from_side(self, side, even_ref, odd_ref, at):
        e, o = even_ref[at], odd_ref[at]
        return jnp.where(self.even, e, o) if side == 0 else jnp.where(self.even, o, e)


def exp_sum(s0, s1, s2):
    top = jnp.max(jnp.maximum(jnp.maximum(s0, s1), s2), axis=0, keepdims=True)
    e0, e1, e2 = jnp.exp(s0 - top), jnp.exp(s1 - top), jnp.exp(s2 - top)
    return top, e0, e1, e2, jnp.sum(e0 + e1 + e2, axis=0, keepdims=True)


def exp_top(s):
    top = jnp.max(s, axis=0, keepdims=True)
    e = jnp.exp(s - top)
    return top, e, jnp.sum(e, axis=0, keepdims=True)


def interior_kernel(shape, *refs):
    table, (_, q_ref, o_ref, g_ref, k_ref, v_ref), refs = refs[:3], refs[3:9], refs[9:]
    dq_out, dk_out, dv_out, dqe_ref, dke_ref, dve_ref, dq_buf, dk_buf, dv_buf, sems = refs
    bounds = Bounds(shape, table)
    n_ex, gq, gk = bounds.n_ex, bounds.gq, bounds.gk
    slots = 2 * gq
    edge = gk // 2
    win = gk + edge
    slot = slot_of(slots)
    bf16 = jnp.bfloat16

    def unit(i, cols, held):
        q0, k0 = i * gq, i * gk
        d_lo, d_hi = bounds.dec(i) - q0, bounds.dec(i + 1) - q0
        e_lo, e_hi = bounds.enc(i) - k0, bounds.enc(i + 1) - k0 - gk
        keys = k_ref[k0 : k0 + win, cols]
        qs = spread(q_ref[q0 : q0 + slots, cols])
        s = dot_nt(keys, qs)
        gs = spread(g_ref[q0 : q0 + slots, cols])
        dots = row_dots(o_ref[q0 : q0 + slots, cols], gs)
        dp = dot_nt(v_ref[k0 : k0 + win, cols], gs)
        yield
        row = row_ids(edge, LANES)
        s0 = jnp.where(row >= e_lo, s[:edge], low)
        s2 = jnp.where(row < e_hi, s[gk:], low)
        _, e0, e1, e2, total = exp_sum(s0, s[edge:gk], s2)
        yield
        inv = jnp.where((slot >= d_lo) & (slot < d_hi), 1.0 / total, 0.0)
        p = jnp.concatenate([e0, e1, e2], axis=0) * inv
        p_low = p.astype(bf16)
        yield
        dv = dot_nn(p_low, gs)
        ds = (p * (dp - dots)).astype(bf16)
        yield
        dk = dot_nn(ds, qs)
        dq = gather_heads(dot_tn(ds, keys))
        yield
        for which, (ref, ext, part) in enumerate(((dk_buf, dke_ref, dk), (dv_buf, dve_ref, dv))):
            first = part[:edge]
            if i > 0:
                first = first + held[(i - 1, which)]
                ref[k0 : k0 + edge, cols] = first.astype(bf16)
            else:
                ext[:edge, cols] = first.astype(bf16)
            ref[k0 + edge : k0 + gk, cols] = part[edge:gk].astype(bf16)
            if i < n_ex - 2:
                held[(i, which)] = part[gk:]
            else:
                ext[edge:, cols] = part[gk:].astype(bf16)
        first = dq[:gq]
        if i > 0:
            dq_buf[q0 : q0 + gq, cols] = (first + held[(i - 1, 2)]).astype(bf16)
        else:
            dqe_ref[:gq, cols] = first.astype(bf16)
        if i < n_ex - 2:
            held[(i, 2)] = dq[gq:]
        else:
            dqe_ref[gq:, cols] = dq[gq:].astype(bf16)
        yield

    def copies(at):
        cols = pl.ds(pl.multiple_of(at * (BATCH * LANES), LANES), BATCH * LANES)
        out = []
        k_rows, q_rows = pl.ds(edge, (n_ex - 1) * gk - edge), pl.ds(gq, (n_ex - 2) * gq)
        for j, (buf, ref, rows) in enumerate(((dk_buf, dk_out, k_rows), (dv_buf, dv_out, k_rows), (dq_buf, dq_out, q_rows))):
            out.append(pltpu.make_async_copy(buf.at[rows, cols], ref.at[rows, cols], sems.at[at, j]))
        return out

    @pl.loop(0, q_ref.shape[1] // LANES // BATCH)
    def _(at):
        units = []
        for c in range(BATCH):
            cols = pl.ds(pl.multiple_of(at * (BATCH * LANES) + c * LANES, LANES), LANES)
            held = {}
            units += [unit(i, cols, held) for i in range(n_ex - 1)]
        run_skewed(units)
        for copy in copies(at):
            copy.start()

    @pl.loop(0, q_ref.shape[1] // LANES // BATCH)
    def _(at):
        for copy in copies(at):
            copy.wait()


def three_parts(x):
    hi = x.astype(jnp.bfloat16).astype(jnp.float32)
    mid = (x - hi).astype(jnp.bfloat16).astype(jnp.float32)
    return [hi, mid, x - hi - mid]


def stats_kernel(shape, pos_ref, dec_hbm, enc_hbm, q_hbm, o_hbm, g_hbm, k_hbm, me_ref, mo_ref, stat_ref, q_ref, o_ref, g_ref, k_ref, pack_ref, dec_ref, enc_ref, sems):
    bounds = Bounds(shape, (dec_ref, enc_ref, pos_ref))
    n_ex, gq, gk = bounds.n_ex, bounds.gq, bounds.gk
    edge = gk // 2
    last = (n_ex - 1) * gq
    feats = q_ref.shape[1]
    at_e = pl.multiple_of(jnp.where(bounds.even, last, 0), gq)
    at_o = pl.multiple_of(jnp.where(bounds.even, 0, last), gq)

    jobs = [
        (dec_hbm, dec_ref, None, None), (enc_hbm, enc_ref, None, None),
        (k_hbm, k_ref, (n_ex - 1) * gk, (0, gk)), (k_hbm, k_ref, 0, (gk, edge)),
    ]
    for src, dst in ((q_hbm, q_ref), (g_hbm, g_ref), (o_hbm, o_ref)):
        jobs += [(src, dst, last, (last, gq)), (src, dst, 0, (0, gq))]
    first = len(jobs)
    jobs += [(q_hbm, me_ref, at_e, (0, gq)), (g_hbm, me_ref, at_e, (gq, gq)), (q_hbm, mo_ref, at_o, (0, gq)), (g_hbm, mo_ref, at_o, (gq, gq))]
    jobs += [(src, dst, gq, (gq, last - gq)) for src, dst in ((q_hbm, q_ref), (g_hbm, g_ref), (o_hbm, o_ref))]
    copies = []
    for i, (src, dst, at, to) in enumerate(jobs):
        if to is not None:
            src, dst = src.at[pl.ds(at, to[1])], dst.at[pl.ds(*to), pl.ds(0, feats)]
        copies.append(pltpu.make_async_copy(src, dst, sems.at[i]))
    for copy in copies:
        copy.start()
    for copy in copies[:first]:
        copy.wait()

    slots = PER * gq
    per = 2 * gq * LANES // feats

    def unit(group):
        cols = group.cols
        s, dots = [], []
        for side in (0, 1):
            keys = k_ref[bounds.part(side), cols]
            s.append(dot_nt(keys, spread(bounds.own_rows(side, q_ref, cols))))
        yield
        for side in (0, 1):
            gs = spread(bounds.own_rows(side, g_ref, cols))
            dots.append(row_dots(bounds.own_rows(side, o_ref, cols), gs))
        yield
        for side in (0, 1):
            top, _, total = exp_top(bounds.edge_mask(side, s[side]))
            logs = top + jnp.log(total)
            stat_ref[2 * side : 2 * side + 1, group.lanes(slots)] = logs
            stat_ref[2 * side + 1 : 2 * side + 2, group.lanes(slots)] = dots[side]
            for i, part in enumerate(three_parts(logs) + three_parts(dots[side])):
                pack_ref[side, group.row(per, i), :] = part
        yield

    each_group(feats // LANES, BATCH, lambda group: [unit(group)])
    for copy in copies[first:]:
        copy.wait()
    after, before = pack_ref[0].astype(jnp.bfloat16), pack_ref[1].astype(jnp.bfloat16)
    me_ref[:, feats:] = jnp.where(bounds.even, after, before)
    mo_ref[:, feats:] = jnp.where(bounds.even, before, after)


def unpack(ref, group, per, i):
    return ref[group.row(per, i), :] + ref[group.row(per, i + 1), :] + ref[group.row(per, i + 2), :]


def remote_kernel(shape, *refs):
    *table, _, re_ref, ro_ref, k_ref, v_ref, me_ref, mo_ref, p_ref, ds_ref, got_ref, pack_ref = refs
    bounds = Bounds(shape, table)
    gq, gk = bounds.gq, bounds.gk
    even = bounds.even
    feats = k_ref.shape[1]
    slots = PER * gq
    slot = slot_of(gq)
    bf16, f32 = jnp.bfloat16, jnp.float32
    per_in, per_out = 2 * gq * LANES // feats, gq * LANES // feats
    extra = (slice(None), slice(feats, None))
    for side in (0, 1):
        got_ref[side] = bounds.from_side(side, re_ref, ro_ref, extra).astype(f32)
    pack_ref[...] = jnp.zeros_like(pack_ref)

    def unit(group):
        cols = group.cols
        work = []
        for side in (0, 1):
            far = bounds.from_side(side, re_ref, ro_ref, (slice(None), cols))
            keys = bounds.edge_rows(side, k_ref, cols)
            s = dot_nt(keys, spread(far[:gq]))
            dp = dot_nt(bounds.edge_rows(side, v_ref, cols), spread(far[gq:]))
            work.append((keys, s, dp))
        yield
        tops = [exp_top(bounds.edge_mask(side, work[side][1])) for side in (0, 1)]
        yield
        ds = []
        for side in (0, 1):
            top, e, total = tops[side]
            mine = top + jnp.log(total)
            whole = log_add(mine, unpack(got_ref.at[side], group, per_in, 0))
            dots = unpack(got_ref.at[side], group, per_in, 3)
            p = e * jnp.where(bounds.far_lanes(side, slot), jnp.exp(top - whole), 0.0)
            ds.append((p * (work[side][2] - dots)).astype(bf16))
            p_ref[bounds.part(side), group.lanes(slots)] = p.astype(bf16)
            ds_ref[bounds.part(side), group.lanes(slots)] = ds[side]
            for i, part in enumerate(three_parts(mine)):
                pack_ref[side, group.row(per_out, i), :] = part
        yield
        after, before = (gather_heads(dot_tn(ds[side], work[side][0])).astype(bf16) for side in (0, 1))
        yield
        me_ref[:, cols] = jnp.where(even, after, before)
        mo_ref[:, cols] = jnp.where(even, before, after)
        yield

    each_group(feats // LANES, BATCH, lambda group: [unit(group)])
    after, before = pack_ref[0].astype(bf16), pack_ref[1].astype(bf16)
    me_ref[:, feats:] = jnp.where(even, after, before)
    mo_ref[:, feats:] = jnp.where(even, before, after)


def ready_kernel(shape, *refs):
    *table, re_ref, ro_ref, own_ref, q_ref, g_ref, k_ref, v_ref, p_far, ds_far, dke_ref, dve_ref, p_ref, ds_ref, dk_ref, dv_ref = refs
    bounds = Bounds(shape, table)
    gq, gk = bounds.gq, bounds.gk
    edge = gk // 2
    slots = PER * gq
    slot = slot_of(gq)
    f32 = jnp.float32

    def far_unit(group):
        cols, lanes = group.cols, group.lanes(slots)
        far = [bounds.from_side(side, re_ref, ro_ref, (slice(None), cols)) for side in (0, 1)]
        for ref, ext, src, rows in ((dv_ref, dve_ref, p_far, slice(gq, None)), (dk_ref, dke_ref, ds_far, slice(0, gq))):
            a, b = (dot_nn(src[bounds.part(side), lanes], spread(far[side][rows])) for side in (0, 1))
            yield
            ref[:edge, cols] = a[:edge] + ext[edge:, cols].astype(f32)
            ref[edge:gk, cols] = a[edge:]
            ref[gk:, cols] = b + ext[:edge, cols].astype(f32)
        yield

    def own_unit(group):
        cols, lanes = group.cols, group.lanes(slots)
        work = []
        for side in (0, 1):
            s = dot_nt(bounds.edge_rows(side, k_ref, cols), spread(bounds.own_rows(side, q_ref, cols)))
            dp = dot_nt(bounds.edge_rows(side, v_ref, cols), spread(bounds.own_rows(side, g_ref, cols)))
            work.append((s, dp))
        yield
        for side in (0, 1):
            s, dp = work[side]
            logs = jnp.where(bounds.own_lanes(side, slot), own_ref[2 * side : 2 * side + 1, lanes], high)
            p = jnp.exp(bounds.edge_mask(side, s) - logs)
            p_ref[bounds.part(side), lanes] = p
            ds_ref[bounds.part(side), lanes] = p * (dp - own_ref[2 * side + 1 : 2 * side + 2, lanes])
        yield

    each_group(q_ref.shape[1] // LANES, 4, lambda group: [own_unit(group), far_unit(group)])


def edge_kernel(shape, *refs):
    *table, me_ref, mo_ref, own_ref, q_ref, g_ref, k_ref, p_ref, ds_ref, dka_ref, dva_ref, dqe_ref = refs[:14]
    _, _, _, dq_out, dk_out, dv_out, dq_buf, dk_buf, dv_buf, got_ref, sems = refs[14:]
    bounds = Bounds(shape, table)
    n_ex, gq, gk = bounds.n_ex, bounds.gq, bounds.gk
    edge = gk // 2
    feats = q_ref.shape[1]
    slots = PER * gq
    slot = slot_of(gq)
    bf16, f32 = jnp.bfloat16, jnp.float32
    last_q, last_k = (n_ex - 1) * gq, (n_ex - 1) * gk
    per = gq * LANES // feats
    extra = (slice(None), slice(feats, None))
    for side in (0, 1):
        got_ref[side] = bounds.from_side(side, me_ref, mo_ref, extra).astype(f32)

    def unit(group):
        cols, lanes = group.cols, group.lanes(slots)
        shares = []
        for side in (0, 1):
            other = unpack(got_ref.at[side], group, per, 0)
            if side == 0:
                other = jnp.where(bounds.has_next, other, low)
            own = own_ref[2 * side : 2 * side + 1, lanes]
            share = jnp.where(bounds.own_lanes(side, slot), jnp.exp(own - log_add(own, other)), 0.0)
            shares.append(share)
            part = bounds.part(side)
            dv = dot_nn((p_ref[part, lanes] * share).astype(bf16), spread(bounds.own_rows(side, g_ref, cols)))
            dv_buf[part, cols] = (dv + dva_ref[part, cols]).astype(bf16)
        yield
        ds = []
        for side in (0, 1):
            part = bounds.part(side)
            ds.append((ds_ref[part, lanes] * shares[side]).astype(bf16))
            dk = dot_nn(ds[side], spread(bounds.own_rows(side, q_ref, cols)))
            dk_buf[part, cols] = (dk + dka_ref[part, cols]).astype(bf16)
        yield
        for side in (0, 1):
            dq = gather_heads(dot_tn(ds[side], bounds.edge_rows(side, k_ref, cols)))
            back = bounds.from_side(side, me_ref, mo_ref, (slice(None), cols)).astype(f32)
            rows = slice(gq, 2 * gq) if side == 0 else slice(0, gq)
            dq_buf[rows, cols] = (dq + back + dqe_ref[rows, cols].astype(f32)).astype(bf16)
        yield

    def copies(at):
        cols = pl.ds(pl.multiple_of(at * (BATCH * LANES), LANES), BATCH * LANES)
        moves = []
        for buf, ref in ((dk_buf, dk_out), (dv_buf, dv_out)):
            moves += [(buf, (0, gk), ref, (last_k, gk)), (buf, (gk, edge), ref, (0, edge))]
        moves += [(dq_buf, (0, gq), dq_out, (0, gq)), (dq_buf, (gq, gq), dq_out, (last_q, gq))]
        return [
            pltpu.make_async_copy(src.at[pl.ds(*a), cols], dst.at[pl.ds(*b), cols], sems.at[at, j])
            for j, (src, a, dst, b) in enumerate(moves)
        ]

    def send(at):
        for copy in copies(at):
            copy.start()

    each_group(feats // LANES, BATCH, lambda group: [unit(group)], send)

    @pl.loop(0, feats // LANES // BATCH)
    def _(at):
        for copy in copies(at):
            copy.wait()


inside = pl.BlockSpec(memory_space=pltpu.VMEM)
anywhere = pl.BlockSpec(memory_space=pl.ANY)
off_chip = pl.BlockSpec(memory_space=pltpu.HBM)
scalars = pl.BlockSpec(memory_space=pltpu.SMEM)


def call(kernel, ins, outs, scratch=(), aliases=None, flops=0, nbytes=0):
    return pl.pallas_call(
        kernel,
        out_shape=[shape for _, shape in outs],
        in_specs=list(ins),
        out_specs=[spec for spec, _ in outs],
        scratch_shapes=list(scratch),
        input_output_aliases=aliases or {},
        compiler_params=pltpu.CompilerParams(vmem_limit_bytes=40 * 1024 * 1024),
        cost_estimate=pl.CostEstimate(flops=flops, bytes_accessed=nbytes, transcendentals=0),
    )


def shards(dec_query, enc_key, enc_value, saved_out, d_out, dec_start, enc_start):
    q, k, v, o, g = dec_query[0], enc_key[0], enc_value[0], saved_out[0], d_out[0]
    q_rows, feats = q.shape
    k_rows = k.shape[0]
    pos = lax.axis_index("seq")
    count = lax.axis_size("seq")
    n_ex = (dec_start.shape[1] - 1) // count
    gq, gk = q_rows // n_ex, k_rows // n_ex
    edge = gk // 2
    groups = feats // LANES
    bf16, f32 = jnp.bfloat16, jnp.float32
    shape = (n_ex, gq, gk, count)

    def swap_even(x):
        return lax.ppermute(x, "seq", [(i, i ^ 1) for i in range(count) if i ^ 1 < count])

    def swap_odd(x):
        pairs = []
        for i in range(1, count - 1, 2):
            pairs += [(i, i + 1), (i + 1, i)]
        return lax.ppermute(x, "seq", pairs)

    place = pos.astype(jnp.int32)[None]
    table = (dec_start, enc_start, place)
    tables = [scalars] * 3

    packed = groups * PER * gq

    def like(rows, kind=bf16, width=feats):
        return jax.ShapeDtypeStruct((rows, width), kind)

    def vmem(rows):
        return pltpu.VMEM((rows, feats), bf16)

    def out(rows, kind=bf16, width=feats):
        return (inside, like(rows, kind, width))

    def pack(rows):
        return pltpu.VMEM((2, rows, PER * gq), f32)

    placed = (pltpu.with_memory_space_constraint(x, pltpu.HBM) for x in (dec_start, enc_start, q, o, g, k))
    raw_e, raw_o, own, q, o, g = call(
        functools.partial(stats_kernel, shape), [scalars] + [off_chip] * 6,
        [out(2 * gq, bf16, feats + PER * gq)] * 2 + [out(4, f32, packed)] + [out(q_rows)] * 3,
        scratch=[vmem(gk + edge), pack(2 * gq), pltpu.SMEM(dec_start.shape, jnp.int32), pltpu.SMEM(enc_start.shape, jnp.int32), pltpu.SemaphoreType.DMA((17,))],
        flops=int(4e8), nbytes=int(2e6),
    )(place, *placed)
    raw_e, raw_o = swap_even(raw_e), swap_odd(raw_o)

    big = [(anywhere, like(q_rows)), (anywhere, like(k_rows)), (anywhere, like(k_rows))]
    dq, dk, dv, dqe, dke, dve = call(
        functools.partial(interior_kernel, shape), tables + [anywhere] + [inside] * 5,
        big + [out(2 * gq), out(gk), out(gk)],
        scratch=[vmem(q_rows), vmem(k_rows), vmem(k_rows), pltpu.SemaphoreType.DMA((groups // BATCH, 3))],
        flops=int(4e9), nbytes=int(8e6),
    )(*table, own, q, o, g, k, v)

    to_e, to_o, p_far, ds_far = call(
        functools.partial(remote_kernel, shape), tables + [anywhere] + [inside] * 4,
        [out(gq, bf16, feats + PER * gq)] * 2 + [out(gk + edge, bf16, packed)] * 2,
        scratch=[pack(2 * gq), pack(gq)],
        flops=int(8e8), nbytes=int(3e6),
    )(*table, dqe, raw_e, raw_o, k, v)
    back_e, back_o = swap_even(to_e), swap_odd(to_o)

    p_own, ds_own, dka, dva = call(
        functools.partial(ready_kernel, shape), tables + [inside] * 11, [out(gk + edge, f32, packed)] * 2 + [out(gk + edge, f32)] * 2,
        flops=int(1e9), nbytes=int(6e6),
    )(*table, raw_e, raw_o, own, q, g, k, v, p_far, ds_far, dke, dve)
    dq, dk, dv = call(
        functools.partial(edge_kernel, shape), tables + [inside] * 11 + [anywhere] * 3, big,
        scratch=[vmem(2 * gq), vmem(gk + edge), vmem(gk + edge), pack(gq), pltpu.SemaphoreType.DMA((groups // BATCH, 6))],
        aliases={14: 0, 15: 1, 16: 2},
        flops=int(1e9), nbytes=int(6e6),
    )(*table, back_e, back_o, own, q, g, k, p_own, ds_own, dka, dva, dqe, dq, dk, dv)
    return dq[None], dk[None], dv[None]


def solution(mesh):
    spec = P(("grp", "dp"), "seq", None)
    return jax.shard_map(
        shards,
        mesh=mesh,
        in_specs=(spec,) * 5 + (P(("grp", "dp"), None),) * 2,
        out_specs=(spec,) * 3,
        check_vma=False,
    )
```

time: 33.9 us -> 32.3 us (0.953)
  Pallas kernels: 18.4 us -> 16.3 us
  waiting for transfers between devices: 5.27 us -> 5.74 us
    ppermute x2, waiting for transfers between devices: 1.72 us -> 3.74 us  [swap_odd(): return lax.ppermute(x, 'seq', pairs)]
    ppermute x2, waiting for transfers between devices: 3.55 us -> 2 us  [swap_even(): lax.ppermute(x, 'seq', [(i, i ^ 1) for i in range(count) if i ^ 1 < count])]
    pallas_call x1, Pallas kernels: 3.17 us -> 1.76 us  [shards(): call(functools.partial(ready_kernel, shape), tables + [inside] * 11, [out...]
  transfers between devices with their start and end apart: 4 -> 4, of which waited for: 3 -> 2; matrix products, arithmetic and copies ran while one was open for 0% -> 0% of each run, Pallas kernels for 30% -> 27%
where the time goes in v4:
time: 32.3 us; the launch traced here: 32.2 us
  Pallas kernels  16.3 us (50%)
  starting transfers between devices  7.75 us (24%)
  waiting for transfers between devices  5.74 us (18%)
  local copies, waits for them, and re-layouts  1.6 us (5%)
  between operations  0.74 us (2%)
    pallas_call x1, Pallas kernels, shards(): call(functools.partial(interior_kernel, shape), tables + [anywhere] + [in...  6.96 us
    ppermute x2, starting transfers between devices, swap_odd(): return lax.ppermute(x, 'seq', pairs)  4.58 us
    ppermute x2, waiting for transfers between devices, swap_odd(): return lax.ppermute(x, 'seq', pairs)  3.74 us
    ppermute x2, starting transfers between devices, swap_even(): lax.ppermute(x, 'seq', [(i, i ^ 1) for i in range(count) if i ^ 1 < count])  3.17 us
    pallas_call x1, Pallas kernels, shards(): call(functools.partial(stats_kernel, shape), [scalars] + [off_chip] * 6,...  2.63 us
    pallas_call x1, Pallas kernels, shards(): call(functools.partial(edge_kernel, shape), tables + [inside] * 11 + [any...  2.61 us
    pallas_call x1, Pallas kernels, shards(): call(functools.partial(remote_kernel, shape), tables + [anywhere] + [insi...  2.36 us
    ppermute x2, waiting for transfers between devices, swap_even(): lax.ppermute(x, 'seq', [(i, i ^ 1) for i in range(count) if i ^ 1 < count])  2 us
  transfers between devices with their start and end apart: 4, of which 2 were waited for; matrix products, arithmetic and copies ran while one was open for 0% of the time, Pallas kernels for 27%

profile of v4, /device:TPU:16, one launch (start us, length us, event | category | flops | bytes accessed | tf_op | source)
XLA Modules:
  0.0 32.2 jit_solution(5963978118719540390)
XLA Ops:
  0.6 0.0 copy-start.3
  0.6 0.0 copy-start.2
  0.7 0.0 copy-start
  0.7 2.6 %shard_map.94 = (bf16[64,2176]{1,0:T(8,128)(2,1)S(1)}, bf16[64,2176]{1,0:T(8,128)(2,1)S(1)}, f32[4,1024]{1,0:T(4,128)S(1)}, bf16[128,2048]{1,0:T(8,128)(2,1)S(1)...) custom-call(s32[1]{0:T(128)} %bitcast.pos_ref.refs_2_, s32[1,33]{1,0:T(1,128)} %refs_0_.7, ...), custom_call_target="tpu_custom_call" | custom-call | flops 400000000 | bytes 2000000 | tf_op jit(solution)/shard_map/pallas_call | solution.py:545
  3.3 1.6 %collective-permute-start = (bf16[64,2176]{1,0:T(8,128)(2,1)S(1)}, bf16[64,2176]{1,0:T(8,128)(2,1)S(1)}, u32[]{:S(2)}, u32[]{:S(2)}) collective-permute-start(bf16[64,2176]{1,0:T(8,128)(2,1)S(1)} %get-tuple-element.31), channel_id=1, source_target_pairs={{0,2},{2,0},{4,6},{6,4},{8,10},{10,8},{12,14},{14,12},{1,3},{3,1},... | collective-permute-start | bytes 835592 | tf_op jit(solution)/shard_map/ppermute | solution.py:518
  4.9 2.3 %collective-permute-start.1 = (bf16[64,2176]{1,0:T(8,128)(2,1)S(1)}, bf16[64,2176]{1,0:T(8,128)(2,1)S(1)}, u32[]{:S(2)}, u32[]{:S(2)}) collective-permute-start(bf16[64,2176]{1,0:T(8,128)(2,1)S(1)} %get-tuple-element.32), channel_id=1, source_target_pairs={{2,4},{4,2},{6,8},{8,6},{10,12},{12,10},{3,5},{5,3},{7,9},{9,7},{1... | collective-permute-start | bytes 835592 | tf_op jit(solution)/shard_map/ppermute | solution.py:524
  7.2 0.0 copy-done.3
  7.2 0.0 copy-done.2
  7.2 0.0 copy-done
  7.2 0.0 copy-start.1
  7.2 1.6 %copy-done.1 = bf16[1,512,2048]{2,1,0:T(8,128)(2,1)S(1)} copy-done((bf16[1,512,2048]{2,1,0:T(8,128)(2,1)S(1)}, bf16[1,512,2048]{2,1,0:T(8,128)(2,1)}, u32[]{:S(2)}) %copy-start.1) | copy-done | bytes 2097176
  8.8 7.0 %shard_map.95 = (bf16[128,2048]{1,0:T(8,128)(2,1)}, bf16[512,2048]{1,0:T(8,128)(2,1)}, bf16[512,2048]{1,0:T(8,128)(2,1)}, bf16[64,2048]{1,0:T(8,128)(2,1)S(1)}, ...) custom-call(s32[1,33]{1,0:T(1,128)S(1)} %copy-done.2, s32[1,33]{1,0:T(1,128)S(1)} %copy-done.3, ...), custom_call_target="tpu_custom_call" | custom-call | flops 4000000000 | bytes 8000000 | tf_op jit(solution)/shard_map/pallas_call | solution.py:554
  15.8 2.0 %collective-permute-done.refs_4_.refs_3_ = bf16[64,2176]{1,0:T(8,128)(2,1)S(1)} collective-permute-done((bf16[64,2176]{1,0:T(8,128)(2,1)S(1)}, bf16[64,2176]{1,0:T(8,128)(2,1)S(1)}, u32[]{:S(2)}, u32[]{:S(2)}) %collective-permute-start) | collective-permute-done | bytes 278560 | tf_op jit(solution)/shard_map/ppermute | solution.py:518
  17.7 0.0 collective-permute-done.1.refs_5_.refs_4_
  17.7 2.4 %shard_map.96 = (bf16[32,2176]{1,0:T(8,128)(2,1)S(1)}, bf16[32,2176]{1,0:T(8,128)(2,1)S(1)}, bf16[192,1024]{1,0:T(8,128)(2,1)S(1)}, bf16[192,1024]{1,0:T(8,128)(2,1)S(1)}) custom-call(s32[1,33]{1,0:T(1,128)S(1)} %copy-done.2, s32[1,33]{1,0:T(1,128)S(1)} %copy-done.3, s32[1]{0:T(128)} %bitcast.pos_ref.refs_2_, ...), custom_call_target="tpu_custom_call" | custom-call | flops 800000000 | bytes 3000000 | tf_op jit(solution)/shard_map/pallas_call | solution.py:561
  20.1 1.6 %collective-permute-start.2 = (bf16[32,2176]{1,0:T(8,128)(2,1)S(1)}, bf16[32,2176]{1,0:T(8,128)(2,1)S(1)}, u32[]{:S(2)}, u32[]{:S(2)}) collective-permute-start(bf16[32,2176]{1,0:T(8,128)(2,1)S(1)} %get-tuple-element.33), channel_id=1, source_target_pairs={{0,2},{2,0},{4,6},{6,4},{8,10},{10,8},{12,14},{14,12},{1,3},{3,1},... | collective-permute-start | bytes 417800 | tf_op jit(solution)/shard_map/ppermute | solution.py:518
  21.7 2.3 %collective-permute-start.3 = (bf16[32,2176]{1,0:T(8,128)(2,1)S(1)}, bf16[32,2176]{1,0:T(8,128)(2,1)S(1)}, u32[]{:S(2)}, u32[]{:S(2)}) collective-permute-start(bf16[32,2176]{1,0:T(8,128)(2,1)S(1)} %get-tuple-element.34), channel_id=1, source_target_pairs={{2,4},{4,2},{6,8},{8,6},{10,12},{12,10},{3,5},{5,3},{7,9},{9,7},{1... | collective-permute-start | bytes 417800 | tf_op jit(solution)/shard_map/ppermute | solution.py:524
  24.0 1.8 %shard_map.97 = (f32[192,1024]{1,0:T(8,128)S(1)}, f32[192,1024]{1,0:T(8,128)S(1)}, f32[192,2048]{1,0:T(8,128)S(1)}, f32[192,2048]{1,0:T(8,128)S(1)}) custom-call(s32[1,33]{1,0:T(1,128)S(1)} %copy-done.2, s32[1,33]{1,0:T(1,128)S(1)} %copy-done.3, s32[1]{0:T(128)} %bitcast.pos_ref.refs_2_, bf16[64,2176]{1,0:T(8,128)(2,1)S(1)} %collective-permute-done.refs_4_.refs_3_, ...), custom_call_target="tpu_custom_call" | custom-call | flops 1000000000 | bytes 6000000 | tf_op jit(solution)/shard_map/pallas_call | solution.py:569
  25.8 0.0 collective-permute-done.2.refs_3_
  25.8 3.7 %collective-permute-done.3.refs_4_ = bf16[32,2176]{1,0:T(8,128)(2,1)S(1)} collective-permute-done((bf16[32,2176]{1,0:T(8,128)(2,1)S(1)}, bf16[32,2176]{1,0:T(8,128)(2,1)S(1)}, u32[]{:S(2)}, u32[]{:S(2)}) %collective-permute-start.3) | collective-permute-done | bytes 139296 | tf_op jit(solution)/shard_map/ppermute | solution.py:524
  29.5 2.6 %shard_map.98 = (bf16[128,2048]{1,0:T(8,128)(2,1)}, bf16[512,2048]{1,0:T(8,128)(2,1)}, bf16[512,2048]{1,0:T(8,128)(2,1)}) custom-call(s32[1,33]{1,0:T(1,128)S(1)} %copy-done.2, s32[1,33]{1,0:T(1,128)S(1)} %copy-done.3, s32[1]{0:T(128)} %bitcast.pos_ref.refs_2_, ...), custom_call_target="tpu_custom_call", output_to_operand_aliasing={{0}: (14, {}), {1}: (15, {}), {2}: (16, {})} | custom-call | flops 1000000000 | bytes 6000000 | tf_op jit(solution)/shard_map/pallas_call | solution.py:573
Async XLA Ops:
  0.6 6.6 %copy-start.3 = (s32[1,33]{1,0:T(1,128)S(1)}, s32[1,33]{1,0:T(1,128)}, u32[]{:S(2)}) copy-start(s32[1,33]{1,0:T(1,128)} %refs_1_.7) | copy-start | bytes 400
  0.6 6.6 %copy-start.2 = (s32[1,33]{1,0:T(1,128)S(1)}, s32[1,33]{1,0:T(1,128)}, u32[]{:S(2)}) copy-start(s32[1,33]{1,0:T(1,128)} %refs_0_.7) | copy-start | bytes 400
  0.7 6.6 %copy-start = (bf16[1,512,2048]{2,1,0:T(8,128)(2,1)S(1)}, bf16[1,512,2048]{2,1,0:T(8,128)(2,1)}, u32[]{:S(2)}) copy-start(bf16[1,512,2048]{2,1,0:T(8,128)(2,1)} %param.8) | copy-start | bytes 6291460
  3.3 14.4 %collective-permute-start = (bf16[64,2176]{1,0:T(8,128)(2,1)S(1)}, bf16[64,2176]{1,0:T(8,128)(2,1)S(1)}, u32[]{:S(2)}, u32[]{:S(2)}) collective-permute-start(bf16[64,2176]{1,0:T(8,128)(2,1)S(1)} %get-tuple-element.31), channel_id=1, source_target_pairs={{0,2},{2,0},{4,6},{6,4},{8,10},{10,8},{12,14},{14,12},{1,3},{3,1},... | collective-permute-start | bytes 835592 | tf_op jit(solution)/shard_map/ppermute | solution.py:518
  4.9 12.8 %collective-permute-start.1 = (bf16[64,2176]{1,0:T(8,128)(2,1)S(1)}, bf16[64,2176]{1,0:T(8,128)(2,1)S(1)}, u32[]{:S(2)}, u32[]{:S(2)}) collective-permute-start(bf16[64,2176]{1,0:T(8,128)(2,1)S(1)} %get-tuple-element.32), channel_id=1, source_target_pairs={{2,4},{4,2},{6,8},{8,6},{10,12},{12,10},{3,5},{5,3},{7,9},{9,7},{1... | collective-permute-start | bytes 835592 | tf_op jit(solution)/shard_map/ppermute | solution.py:524
  7.2 1.6 %copy-start.1 = (bf16[1,512,2048]{2,1,0:T(8,128)(2,1)S(1)}, bf16[1,512,2048]{2,1,0:T(8,128)(2,1)}, u32[]{:S(2)}) copy-start(bf16[1,512,2048]{2,1,0:T(8,128)(2,1)} %param.9) | copy-start | bytes 6291460
  20.1 5.7 %collective-permute-start.2 = (bf16[32,2176]{1,0:T(8,128)(2,1)S(1)}, bf16[32,2176]{1,0:T(8,128)(2,1)S(1)}, u32[]{:S(2)}, u32[]{:S(2)}) collective-permute-start(bf16[32,2176]{1,0:T(8,128)(2,1)S(1)} %get-tuple-element.33), channel_id=1, source_target_pairs={{0,2},{2,0},{4,6},{6,4},{8,10},{10,8},{12,14},{14,12},{1,3},{3,1},... | collective-permute-start | bytes 417800 | tf_op jit(solution)/shard_map/ppermute | solution.py:518
  21.7 7.8 %collective-permute-start.3 = (bf16[32,2176]{1,0:T(8,128)(2,1)S(1)}, bf16[32,2176]{1,0:T(8,128)(2,1)S(1)}, u32[]{:S(2)}, u32[]{:S(2)}) collective-permute-start(bf16[32,2176]{1,0:T(8,128)(2,1)S(1)} %get-tuple-element.34), channel_id=1, source_target_pairs={{2,4},{4,2},{6,8},{8,6},{10,12},{12,10},{3,5},{5,3},{7,9},{9,7},{1... | collective-permute-start | bytes 417800 | tf_op jit(solution)/shard_map/ppermute | solution.py:524

commit v5 on v4

--- a/solution.py
+++ b/solution.py
@@ -15,6 +15,7 @@
 low = -1e30
 high = 1e30
 BATCH = 4
+CHUNK = 2
 
 
 def dot_nt(a, b):
@@ -286,33 +287,39 @@
         copies.append(pltpu.make_async_copy(src, dst, sems.at[i]))
     for copy in copies:
         copy.start()
-    for copy in copies[:first]:
+    for copy in copies[:6]:
         copy.wait()
 
     slots = PER * gq
     per = 2 * gq * LANES // feats
 
-    def unit(group):
-        cols = group.cols
-        s, dots = [], []
-        for side in (0, 1):
-            keys = k_ref[bounds.part(side), cols]
-            s.append(dot_nt(keys, spread(bounds.own_rows(side, q_ref, cols))))
-        yield
-        for side in (0, 1):
-            gs = spread(bounds.own_rows(side, g_ref, cols))
-            dots.append(row_dots(bounds.own_rows(side, o_ref, cols), gs))
+    def keep(group, side, kind, value):
+        stat_ref[2 * side + kind : 2 * side + kind + 1, group.lanes(slots)] = value
+        for i, part in enumerate(three_parts(value)):
+            pack_ref[side, group.row(per, 3 * kind + i), :] = part
+
+    def log_unit(group):
+        s = []
+        for side in (0, 1):
+            keys = k_ref[bounds.part(side), group.cols]
+            s.append(dot_nt(keys, spread(bounds.own_rows(side, q_ref, group.cols))))
         yield
         for side in (0, 1):
             top, _, total = exp_top(bounds.edge_mask(side, s[side]))
-            logs = top + jnp.log(total)
-            stat_ref[2 * side : 2 * side + 1, group.lanes(slots)] = logs
-            stat_ref[2 * side + 1 : 2 * side + 2, group.lanes(slots)] = dots[side]
-            for i, part in enumerate(three_parts(logs) + three_parts(dots[side])):
-                pack_ref[side, group.row(per, i), :] = part
-        yield
-
-    each_group(feats // LANES, BATCH, lambda group: [unit(group)])
+            keep(group, side, 0, top + jnp.log(total))
+        yield
+
+    def dot_unit(group):
+        for side in (0, 1):
+            gs = spread(bounds.own_rows(side, g_ref, group.cols))
+            keep(group, side, 1, row_dots(bounds.own_rows(side, o_ref, group.cols), gs))
+        yield
+
+    groups = feats // LANES
+    each_group(groups, groups, lambda group: [log_unit(group)])
+    for copy in copies[6:first]:
+        copy.wait()
+    each_group(groups, groups, lambda group: [dot_unit(group)])
     for copy in copies[first:]:
         copy.wait()
     after, before = pack_ref[0].astype(jnp.bfloat16), pack_ref[1].astype(jnp.bfloat16)
@@ -370,7 +377,7 @@
         mo_ref[:, cols] = jnp.where(even, before, after)
         yield
 
-    each_group(feats // LANES, BATCH, lambda group: [unit(group)])
+    each_group(feats // LANES, feats // LANES, lambda group: [unit(group)])
     after, before = pack_ref[0].astype(bf16), pack_ref[1].astype(bf16)
     me_ref[:, feats:] = jnp.where(even, after, before)
     mo_ref[:, feats:] = jnp.where(even, before, after)
@@ -457,10 +464,13 @@
             back = bounds.from_side(side, me_ref, mo_ref, (slice(None), cols)).astype(f32)
             rows = slice(gq, 2 * gq) if side == 0 else slice(0, gq)
             dq_buf[rows, cols] = (dq + back + dqe_ref[rows, cols].astype(f32)).astype(bf16)
+        if (group.c + 1) % CHUNK == 0:
+            for copy in copies(group.c // CHUNK):
+                copy.start()
         yield
 
     def copies(at):
-        cols = pl.ds(pl.multiple_of(at * (BATCH * LANES), LANES), BATCH * LANES)
+        cols = pl.ds(at * (CHUNK * LANES), CHUNK * LANES)
         moves = []
         for buf, ref in ((dk_buf, dk_out), (dv_buf, dv_out)):
             moves += [(buf, (0, gk), ref, (last_k, gk)), (buf, (gk, edge), ref, (0, edge))]
@@ -470,14 +480,8 @@
             for j, (src, a, dst, b) in enumerate(moves)
         ]
 
-    def send(at):
-        for copy in copies(at):
-            copy.start()
-
-    each_group(feats // LANES, BATCH, lambda group: [unit(group)], send)
-
-    @pl.loop(0, feats // LANES // BATCH)
-    def _(at):
+    each_group(feats // LANES, feats // LANES, lambda group: [unit(group)])
+    for at in range(feats // LANES // CHUNK):
         for copy in copies(at):
             copy.wait()
 
@@ -572,7 +576,7 @@
     )(*table, raw_e, raw_o, own, q, g, k, v, p_far, ds_far, dke, dve)
     dq, dk, dv = call(
         functools.partial(edge_kernel, shape), tables + [inside] * 11 + [anywhere] * 3, big,
-        scratch=[vmem(2 * gq), vmem(gk + edge), vmem(gk + edge), pack(gq), pltpu.SemaphoreType.DMA((groups // BATCH, 6))],
+        scratch=[vmem(2 * gq), vmem(gk + edge), vmem(gk + edge), pack(gq), pltpu.SemaphoreType.DMA((groups // CHUNK, 6))],
         aliases={14: 0, 15: 1, 16: 2},
         flops=int(1e9), nbytes=int(6e6),
     )(*table, back_e, back_o, own, q, g, k, p_own, ds_own, dka, dva, dqe, dq, dk, dv)

time: 32.3 us -> 31.6 us (0.978)
  Pallas kernels: 16.3 us -> 15.7 us
    pallas_call x1, Pallas kernels: 2.36 us -> 1.97 us  [shards(): call(functools.partial(remote_kernel, shape), tables + [anywhere] + [insi...]
  transfers between devices with their start and end apart: 4 -> 4, of which waited for: 2 -> 2; matrix products, arithmetic and copies ran while one was open for 0% -> 0% of each run, Pallas kernels for 27% -> 28%
where the time goes in v5:
time: 31.6 us; the launch traced here: 31.5 us
  Pallas kernels  15.7 us (50%)
  starting transfers between devices  7.75 us (25%)
  waiting for transfers between devices  5.73 us (18%)
  local copies, waits for them, and re-layouts  1.6 us (5%)
  between operations  0.74 us (2%)
    pallas_call x1, Pallas kernels, shards(): call(functools.partial(interior_kernel, shape), tables + [anywhere] + [in...  6.95 us
    ppermute x2, starting transfers between devices, swap_odd(): return lax.ppermute(x, 'seq', pairs)  4.58 us
    ppermute x2, waiting for transfers between devices, swap_odd(): return lax.ppermute(x, 'seq', pairs)  3.74 us
    ppermute x2, starting transfers between devices, swap_even(): lax.ppermute(x, 'seq', [(i, i ^ 1) for i in range(count) if i ^ 1 < count])  3.17 us
    pallas_call x1, Pallas kernels, shards(): call(functools.partial(stats_kernel, shape), [scalars] + [off_chip] * 6,...  2.54 us
    pallas_call x1, Pallas kernels, shards(): call(functools.partial(edge_kernel, shape), tables + [inside] * 11 + [any...  2.44 us
    ppermute x2, waiting for transfers between devices, swap_even(): lax.ppermute(x, 'seq', [(i, i ^ 1) for i in range(count) if i ^ 1 < count])  1.99 us
    pallas_call x1, Pallas kernels, shards(): call(functools.partial(remote_kernel, shape), tables + [anywhere] + [insi...  1.97 us
  transfers between devices with their start and end apart: 4, of which 2 were waited for; matrix products, arithmetic and copies ran while one was open for 0% of the time, Pallas kernels for 28%

profile of v5, /device:TPU:16, one launch (start us, length us, event | category | flops | bytes accessed | tf_op | source)
XLA Modules:
  0.0 31.5 jit_solution(7865889245691450149)
XLA Ops:
  0.6 0.0 copy-start.3
  0.6 0.0 copy-start.2
  0.7 0.0 copy-start
  0.7 2.5 %shard_map.94 = (bf16[64,2176]{1,0:T(8,128)(2,1)S(1)}, bf16[64,2176]{1,0:T(8,128)(2,1)S(1)}, f32[4,1024]{1,0:T(4,128)S(1)}, bf16[128,2048]{1,0:T(8,128)(2,1)S(1)...) custom-call(s32[1]{0:T(128)} %bitcast.pos_ref.refs_2_, s32[1,33]{1,0:T(1,128)} %refs_0_.7, ...), custom_call_target="tpu_custom_call" | custom-call | flops 400000000 | bytes 2000000 | tf_op jit(solution)/shard_map/pallas_call | solution.py:549
  3.2 1.6 %collective-permute-start = (bf16[64,2176]{1,0:T(8,128)(2,1)S(1)}, bf16[64,2176]{1,0:T(8,128)(2,1)S(1)}, u32[]{:S(2)}, u32[]{:S(2)}) collective-permute-start(bf16[64,2176]{1,0:T(8,128)(2,1)S(1)} %get-tuple-element.31), channel_id=1, source_target_pairs={{0,2},{2,0},{4,6},{6,4},{8,10},{10,8},{12,14},{14,12},{1,3},{3,1},... | collective-permute-start | bytes 835592 | tf_op jit(solution)/shard_map/ppermute | solution.py:522
  4.8 2.3 %collective-permute-start.1 = (bf16[64,2176]{1,0:T(8,128)(2,1)S(1)}, bf16[64,2176]{1,0:T(8,128)(2,1)S(1)}, u32[]{:S(2)}, u32[]{:S(2)}) collective-permute-start(bf16[64,2176]{1,0:T(8,128)(2,1)S(1)} %get-tuple-element.32), channel_id=1, source_target_pairs={{2,4},{4,2},{6,8},{8,6},{10,12},{12,10},{3,5},{5,3},{7,9},{9,7},{1... | collective-permute-start | bytes 835592 | tf_op jit(solution)/shard_map/ppermute | solution.py:528
  7.1 0.0 copy-done.3
  7.1 0.0 copy-done.2
  7.1 0.0 copy-done
  7.1 0.0 copy-start.1
  7.1 1.6 %copy-done.1 = bf16[1,512,2048]{2,1,0:T(8,128)(2,1)S(1)} copy-done((bf16[1,512,2048]{2,1,0:T(8,128)(2,1)S(1)}, bf16[1,512,2048]{2,1,0:T(8,128)(2,1)}, u32[]{:S(2)}) %copy-start.1) | copy-done | bytes 2097176
  8.7 7.0 %shard_map.95 = (bf16[128,2048]{1,0:T(8,128)(2,1)}, bf16[512,2048]{1,0:T(8,128)(2,1)}, bf16[512,2048]{1,0:T(8,128)(2,1)}, bf16[64,2048]{1,0:T(8,128)(2,1)S(1)}, ...) custom-call(s32[1,33]{1,0:T(1,128)S(1)} %copy-done.2, s32[1,33]{1,0:T(1,128)S(1)} %copy-done.3, ...), custom_call_target="tpu_custom_call" | custom-call | flops 4000000000 | bytes 8000000 | tf_op jit(solution)/shard_map/pallas_call | solution.py:558
  15.7 2.0 %collective-permute-done.refs_4_.refs_3_ = bf16[64,2176]{1,0:T(8,128)(2,1)S(1)} collective-permute-done((bf16[64,2176]{1,0:T(8,128)(2,1)S(1)}, bf16[64,2176]{1,0:T(8,128)(2,1)S(1)}, u32[]{:S(2)}, u32[]{:S(2)}) %collective-permute-start) | collective-permute-done | bytes 278560 | tf_op jit(solution)/shard_map/ppermute | solution.py:522
  17.6 0.0 collective-permute-done.1.refs_5_.refs_4_
  17.6 2.0 %shard_map.96 = (bf16[32,2176]{1,0:T(8,128)(2,1)S(1)}, bf16[32,2176]{1,0:T(8,128)(2,1)S(1)}, bf16[192,1024]{1,0:T(8,128)(2,1)S(1)}, bf16[192,1024]{1,0:T(8,128)(2,1)S(1)}) custom-call(s32[1,33]{1,0:T(1,128)S(1)} %copy-done.2, s32[1,33]{1,0:T(1,128)S(1)} %copy-done.3, s32[1]{0:T(128)} %bitcast.pos_ref.refs_2_, ...), custom_call_target="tpu_custom_call" | custom-call | flops 800000000 | bytes 3000000 | tf_op jit(solution)/shard_map/pallas_call | solution.py:565
  19.6 1.6 %collective-permute-start.2 = (bf16[32,2176]{1,0:T(8,128)(2,1)S(1)}, bf16[32,2176]{1,0:T(8,128)(2,1)S(1)}, u32[]{:S(2)}, u32[]{:S(2)}) collective-permute-start(bf16[32,2176]{1,0:T(8,128)(2,1)S(1)} %get-tuple-element.33), channel_id=1, source_target_pairs={{0,2},{2,0},{4,6},{6,4},{8,10},{10,8},{12,14},{14,12},{1,3},{3,1},... | collective-permute-start | bytes 417800 | tf_op jit(solution)/shard_map/ppermute | solution.py:522
  21.2 2.3 %collective-permute-start.3 = (bf16[32,2176]{1,0:T(8,128)(2,1)S(1)}, bf16[32,2176]{1,0:T(8,128)(2,1)S(1)}, u32[]{:S(2)}, u32[]{:S(2)}) collective-permute-start(bf16[32,2176]{1,0:T(8,128)(2,1)S(1)} %get-tuple-element.34), channel_id=1, source_target_pairs={{2,4},{4,2},{6,8},{8,6},{10,12},{12,10},{3,5},{5,3},{7,9},{9,7},{1... | collective-permute-start | bytes 417800 | tf_op jit(solution)/shard_map/ppermute | solution.py:528
  23.5 1.8 %shard_map.97 = (f32[192,1024]{1,0:T(8,128)S(1)}, f32[192,1024]{1,0:T(8,128)S(1)}, f32[192,2048]{1,0:T(8,128)S(1)}, f32[192,2048]{1,0:T(8,128)S(1)}) custom-call(s32[1,33]{1,0:T(1,128)S(1)} %copy-done.2, s32[1,33]{1,0:T(1,128)S(1)} %copy-done.3, s32[1]{0:T(128)} %bitcast.pos_ref.refs_2_, bf16[64,2176]{1,0:T(8,128)(2,1)S(1)} %collective-permute-done.refs_4_.refs_3_, ...), custom_call_target="tpu_custom_call" | custom-call | flops 1000000000 | bytes 6000000 | tf_op jit(solution)/shard_map/pallas_call | solution.py:573
  25.3 0.0 collective-permute-done.2.refs_3_
  25.3 3.7 %collective-permute-done.3.refs_4_ = bf16[32,2176]{1,0:T(8,128)(2,1)S(1)} collective-permute-done((bf16[32,2176]{1,0:T(8,128)(2,1)S(1)}, bf16[32,2176]{1,0:T(8,128)(2,1)S(1)}, u32[]{:S(2)}, u32[]{:S(2)}) %collective-permute-start.3) | collective-permute-done | bytes 139296 | tf_op jit(solution)/shard_map/ppermute | solution.py:528
  29.0 2.4 %shard_map.98 = (bf16[128,2048]{1,0:T(8,128)(2,1)}, bf16[512,2048]{1,0:T(8,128)(2,1)}, bf16[512,2048]{1,0:T(8,128)(2,1)}) custom-call(s32[1,33]{1,0:T(1,128)S(1)} %copy-done.2, s32[1,33]{1,0:T(1,128)S(1)} %copy-done.3, s32[1]{0:T(128)} %bitcast.pos_ref.refs_2_, ...), custom_call_target="tpu_custom_call", output_to_operand_aliasing={{0}: (14, {}), {1}: (15, {}), {2}: (16, {})} | custom-call | flops 1000000000 | bytes 6000000 | tf_op jit(solution)/shard_map/pallas_call | solution.py:577
Async XLA Ops:
  0.6 6.5 %copy-start.3 = (s32[1,33]{1,0:T(1,128)S(1)}, s32[1,33]{1,0:T(1,128)}, u32[]{:S(2)}) copy-start(s32[1,33]{1,0:T(1,128)} %refs_1_.7) | copy-start | bytes 400
  0.6 6.5 %copy-start.2 = (s32[1,33]{1,0:T(1,128)S(1)}, s32[1,33]{1,0:T(1,128)}, u32[]{:S(2)}) copy-start(s32[1,33]{1,0:T(1,128)} %refs_0_.7) | copy-start | bytes 400
  0.7 6.5 %copy-start = (bf16[1,512,2048]{2,1,0:T(8,128)(2,1)S(1)}, bf16[1,512,2048]{2,1,0:T(8,128)(2,1)}, u32[]{:S(2)}) copy-start(bf16[1,512,2048]{2,1,0:T(8,128)(2,1)} %param.8) | copy-start | bytes 6291460
  3.2 14.4 %collective-permute-start = (bf16[64,2176]{1,0:T(8,128)(2,1)S(1)}, bf16[64,2176]{1,0:T(8,128)(2,1)S(1)}, u32[]{:S(2)}, u32[]{:S(2)}) collective-permute-start(bf16[64,2176]{1,0:T(8,128)(2,1)S(1)} %get-tuple-element.31), channel_id=1, source_target_pairs={{0,2},{2,0},{4,6},{6,4},{8,10},{10,8},{12,14},{14,12},{1,3},{3,1},... | collective-permute-start | bytes 835592 | tf_op jit(solution)/shard_map/ppermute | solution.py:522
  4.8 12.8 %collective-permute-start.1 = (bf16[64,2176]{1,0:T(8,128)(2,1)S(1)}, bf16[64,2176]{1,0:T(8,128)(2,1)S(1)}, u32[]{:S(2)}, u32[]{:S(2)}) collective-permute-start(bf16[64,2176]{1,0:T(8,128)(2,1)S(1)} %get-tuple-element.32), channel_id=1, source_target_pairs={{2,4},{4,2},{6,8},{8,6},{10,12},{12,10},{3,5},{5,3},{7,9},{9,7},{1... | collective-permute-start | bytes 835592 | tf_op jit(solution)/shard_map/ppermute | solution.py:528
  7.1 1.6 %copy-start.1 = (bf16[1,512,2048]{2,1,0:T(8,128)(2,1)S(1)}, bf16[1,512,2048]{2,1,0:T(8,128)(2,1)}, u32[]{:S(2)}) copy-start(bf16[1,512,2048]{2,1,0:T(8,128)(2,1)} %param.9) | copy-start | bytes 6291460
  19.6 5.7 %collective-permute-start.2 = (bf16[32,2176]{1,0:T(8,128)(2,1)S(1)}, bf16[32,2176]{1,0:T(8,128)(2,1)S(1)}, u32[]{:S(2)}, u32[]{:S(2)}) collective-permute-start(bf16[32,2176]{1,0:T(8,128)(2,1)S(1)} %get-tuple-element.33), channel_id=1, source_target_pairs={{0,2},{2,0},{4,6},{6,4},{8,10},{10,8},{12,14},{14,12},{1,3},{3,1},... | collective-permute-start | bytes 417800 | tf_op jit(solution)/shard_map/ppermute | solution.py:522
  21.2 7.8 %collective-permute-start.3 = (bf16[32,2176]{1,0:T(8,128)(2,1)S(1)}, bf16[32,2176]{1,0:T(8,128)(2,1)S(1)}, u32[]{:S(2)}, u32[]{:S(2)}) collective-permute-start(bf16[32,2176]{1,0:T(8,128)(2,1)S(1)} %get-tuple-element.34), channel_id=1, source_target_pairs={{2,4},{4,2},{6,8},{8,6},{10,12},{12,10},{3,5},{5,3},{7,9},{9,7},{1... | collective-permute-start | bytes 417800 | tf_op jit(solution)/shard_map/ppermute | solution.py:528

commit v6 on v5

--- a/solution.py
+++ b/solution.py
@@ -77,11 +77,11 @@
     return lax.broadcasted_iota(jnp.int32, (rows, lanes), 0)
 
 
-def run_skewed(units):
+def run_skewed(units, rate=1):
     live, queue = [], list(units)
     while queue or live:
-        if queue:
-            live.append(queue.pop(0))
+        live += queue[:rate]
+        queue = queue[rate:]
         for unit in list(live):
             try:
                 next(unit)
@@ -89,15 +89,13 @@
                 live.remove(unit)
 
 
-def each_group(groups, batch, units_of, after=None):
+def each_group(groups, batch, units_of, rate=1):
     @pl.loop(0, groups // batch)
     def _(at):
         units = []
         for c in range(batch):
             units += units_of(Group(at * batch, c))
-        run_skewed(units)
-        if after is not None:
-            after(at)
+        run_skewed(units, rate)
 
 
 class Group:
@@ -377,7 +375,7 @@
         mo_ref[:, cols] = jnp.where(even, before, after)
         yield
 
-    each_group(feats // LANES, feats // LANES, lambda group: [unit(group)])
+    each_group(feats // LANES, feats // LANES, lambda group: [unit(group)], rate=4)
     after, before = pack_ref[0].astype(bf16), pack_ref[1].astype(bf16)
     me_ref[:, feats:] = jnp.where(even, after, before)
     mo_ref[:, feats:] = jnp.where(even, before, after)

time: 31.6 us -> 31.4 us (level)
  no operation moved by 1% of the time
where the time goes in v6:
time: 31.4 us; the launch traced here: 31.2 us
  Pallas kernels  15.4 us (49%)
  starting transfers between devices  7.75 us (25%)
  waiting for transfers between devices  5.73 us (18%)
  local copies, waits for them, and re-layouts  1.6 us (5%)
  between operations  0.74 us (2%)
    pallas_call x1, Pallas kernels, shards(): call(functools.partial(interior_kernel, shape), tables + [anywhere] + [in...  6.95 us
    ppermute x2, starting transfers between devices, swap_odd(): return lax.ppermute(x, 'seq', pairs)  4.58 us
    ppermute x2, waiting for transfers between devices, swap_odd(): return lax.ppermute(x, 'seq', pairs)  3.74 us
    ppermute x2, starting transfers between devices, swap_even(): lax.ppermute(x, 'seq', [(i, i ^ 1) for i in range(count) if i ^ 1 < count])  3.17 us
    pallas_call x1, Pallas kernels, shards(): call(functools.partial(stats_kernel, shape), [scalars] + [off_chip] * 6,...  2.54 us
    pallas_call x1, Pallas kernels, shards(): call(functools.partial(edge_kernel, shape), tables + [inside] * 11 + [any...  2.44 us
    ppermute x2, waiting for transfers between devices, swap_even(): lax.ppermute(x, 'seq', [(i, i ^ 1) for i in range(count) if i ^ 1 < count])  1.99 us
    pallas_call x1, Pallas kernels, shards(): call(functools.partial(ready_kernel, shape), tables + [inside] * 11, [out...  1.76 us
  transfers between devices with their start and end apart: 4, of which 2 were waited for; matrix products, arithmetic and copies ran while one was open for 0% of the time, Pallas kernels for 28%

profile of v6, /device:TPU:16, one launch (start us, length us, event | category | flops | bytes accessed | tf_op | source)
XLA Modules:
  0.0 31.2 jit_solution(16534523032887777682)
XLA Ops:
  0.6 0.0 copy-start.3
  0.6 0.0 copy-start.2
  0.7 0.0 copy-start
  0.7 2.5 %shard_map.94 = (bf16[64,2176]{1,0:T(8,128)(2,1)S(1)}, bf16[64,2176]{1,0:T(8,128)(2,1)S(1)}, f32[4,1024]{1,0:T(4,128)S(1)}, bf16[128,2048]{1,0:T(8,128)(2,1)S(1)...) custom-call(s32[1]{0:T(128)} %bitcast.pos_ref.refs_2_, s32[1,33]{1,0:T(1,128)} %refs_0_.7, ...), custom_call_target="tpu_custom_call" | custom-call | flops 400000000 | bytes 2000000 | tf_op jit(solution)/shard_map/pallas_call | solution.py:547
  3.2 1.6 %collective-permute-start = (bf16[64,2176]{1,0:T(8,128)(2,1)S(1)}, bf16[64,2176]{1,0:T(8,128)(2,1)S(1)}, u32[]{:S(2)}, u32[]{:S(2)}) collective-permute-start(bf16[64,2176]{1,0:T(8,128)(2,1)S(1)} %get-tuple-element.31), channel_id=1, source_target_pairs={{0,2},{2,0},{4,6},{6,4},{8,10},{10,8},{12,14},{14,12},{1,3},{3,1},... | collective-permute-start | bytes 835592 | tf_op jit(solution)/shard_map/ppermute | solution.py:520
  4.8 2.3 %collective-permute-start.1 = (bf16[64,2176]{1,0:T(8,128)(2,1)S(1)}, bf16[64,2176]{1,0:T(8,128)(2,1)S(1)}, u32[]{:S(2)}, u32[]{:S(2)}) collective-permute-start(bf16[64,2176]{1,0:T(8,128)(2,1)S(1)} %get-tuple-element.32), channel_id=1, source_target_pairs={{2,4},{4,2},{6,8},{8,6},{10,12},{12,10},{3,5},{5,3},{7,9},{9,7},{1... | collective-permute-start | bytes 835592 | tf_op jit(solution)/shard_map/ppermute | solution.py:526
  7.1 0.0 copy-done.3
  7.1 0.0 copy-done.2
  7.1 0.0 copy-done
  7.1 0.0 copy-start.1
  7.1 1.6 %copy-done.1 = bf16[1,512,2048]{2,1,0:T(8,128)(2,1)S(1)} copy-done((bf16[1,512,2048]{2,1,0:T(8,128)(2,1)S(1)}, bf16[1,512,2048]{2,1,0:T(8,128)(2,1)}, u32[]{:S(2)}) %copy-start.1) | copy-done | bytes 2097176
  8.7 7.0 %shard_map.95 = (bf16[128,2048]{1,0:T(8,128)(2,1)}, bf16[512,2048]{1,0:T(8,128)(2,1)}, bf16[512,2048]{1,0:T(8,128)(2,1)}, bf16[64,2048]{1,0:T(8,128)(2,1)S(1)}, ...) custom-call(s32[1,33]{1,0:T(1,128)S(1)} %copy-done.2, s32[1,33]{1,0:T(1,128)S(1)} %copy-done.3, ...), custom_call_target="tpu_custom_call" | custom-call | flops 4000000000 | bytes 8000000 | tf_op jit(solution)/shard_map/pallas_call | solution.py:556
  15.7 2.0 %collective-permute-done.refs_4_.refs_3_ = bf16[64,2176]{1,0:T(8,128)(2,1)S(1)} collective-permute-done((bf16[64,2176]{1,0:T(8,128)(2,1)S(1)}, bf16[64,2176]{1,0:T(8,128)(2,1)S(1)}, u32[]{:S(2)}, u32[]{:S(2)}) %collective-permute-start) | collective-permute-done | bytes 278560 | tf_op jit(solution)/shard_map/ppermute | solution.py:520
  17.6 0.0 collective-permute-done.1.refs_5_.refs_4_
  17.6 1.7 %shard_map.96 = (bf16[32,2176]{1,0:T(8,128)(2,1)S(1)}, bf16[32,2176]{1,0:T(8,128)(2,1)S(1)}, bf16[192,1024]{1,0:T(8,128)(2,1)S(1)}, bf16[192,1024]{1,0:T(8,128)(2,1)S(1)}) custom-call(s32[1,33]{1,0:T(1,128)S(1)} %copy-done.2, s32[1,33]{1,0:T(1,128)S(1)} %copy-done.3, s32[1]{0:T(128)} %bitcast.pos_ref.refs_2_, ...), custom_call_target="tpu_custom_call" | custom-call | flops 800000000 | bytes 3000000 | tf_op jit(solution)/shard_map/pallas_call | solution.py:563
  19.4 1.6 %collective-permute-start.2 = (bf16[32,2176]{1,0:T(8,128)(2,1)S(1)}, bf16[32,2176]{1,0:T(8,128)(2,1)S(1)}, u32[]{:S(2)}, u32[]{:S(2)}) collective-permute-start(bf16[32,2176]{1,0:T(8,128)(2,1)S(1)} %get-tuple-element.33), channel_id=1, source_target_pairs={{0,2},{2,0},{4,6},{6,4},{8,10},{10,8},{12,14},{14,12},{1,3},{3,1},... | collective-permute-start | bytes 417800 | tf_op jit(solution)/shard_map/ppermute | solution.py:520
  21.0 2.3 %collective-permute-start.3 = (bf16[32,2176]{1,0:T(8,128)(2,1)S(1)}, bf16[32,2176]{1,0:T(8,128)(2,1)S(1)}, u32[]{:S(2)}, u32[]{:S(2)}) collective-permute-start(bf16[32,2176]{1,0:T(8,128)(2,1)S(1)} %get-tuple-element.34), channel_id=1, source_target_pairs={{2,4},{4,2},{6,8},{8,6},{10,12},{12,10},{3,5},{5,3},{7,9},{9,7},{1... | collective-permute-start | bytes 417800 | tf_op jit(solution)/shard_map/ppermute | solution.py:526
  23.3 1.8 %shard_map.97 = (f32[192,1024]{1,0:T(8,128)S(1)}, f32[192,1024]{1,0:T(8,128)S(1)}, f32[192,2048]{1,0:T(8,128)S(1)}, f32[192,2048]{1,0:T(8,128)S(1)}) custom-call(s32[1,33]{1,0:T(1,128)S(1)} %copy-done.2, s32[1,33]{1,0:T(1,128)S(1)} %copy-done.3, s32[1]{0:T(128)} %bitcast.pos_ref.refs_2_, bf16[64,2176]{1,0:T(8,128)(2,1)S(1)} %collective-permute-done.refs_4_.refs_3_, ...), custom_call_target="tpu_custom_call" | custom-call | flops 1000000000 | bytes 6000000 | tf_op jit(solution)/shard_map/pallas_call | solution.py:571
  25.0 0.0 collective-permute-done.2.refs_3_
  25.1 3.7 %collective-permute-done.3.refs_4_ = bf16[32,2176]{1,0:T(8,128)(2,1)S(1)} collective-permute-done((bf16[32,2176]{1,0:T(8,128)(2,1)S(1)}, bf16[32,2176]{1,0:T(8,128)(2,1)S(1)}, u32[]{:S(2)}, u32[]{:S(2)}) %collective-permute-start.3) | collective-permute-done | bytes 139296 | tf_op jit(solution)/shard_map/ppermute | solution.py:526
  28.8 2.4 %shard_map.98 = (bf16[128,2048]{1,0:T(8,128)(2,1)}, bf16[512,2048]{1,0:T(8,128)(2,1)}, bf16[512,2048]{1,0:T(8,128)(2,1)}) custom-call(s32[1,33]{1,0:T(1,128)S(1)} %copy-done.2, s32[1,33]{1,0:T(1,128)S(1)} %copy-done.3, s32[1]{0:T(128)} %bitcast.pos_ref.refs_2_, ...), custom_call_target="tpu_custom_call", output_to_operand_aliasing={{0}: (14, {}), {1}: (15, {}), {2}: (16, {})} | custom-call | flops 1000000000 | bytes 6000000 | tf_op jit(solution)/shard_map/pallas_call | solution.py:575
Async XLA Ops:
  0.6 6.5 %copy-start.3 = (s32[1,33]{1,0:T(1,128)S(1)}, s32[1,33]{1,0:T(1,128)}, u32[]{:S(2)}) copy-start(s32[1,33]{1,0:T(1,128)} %refs_1_.7) | copy-start | bytes 400
  0.6 6.5 %copy-start.2 = (s32[1,33]{1,0:T(1,128)S(1)}, s32[1,33]{1,0:T(1,128)}, u32[]{:S(2)}) copy-start(s32[1,33]{1,0:T(1,128)} %refs_0_.7) | copy-start | bytes 400
  0.7 6.5 %copy-start = (bf16[1,512,2048]{2,1,0:T(8,128)(2,1)S(1)}, bf16[1,512,2048]{2,1,0:T(8,128)(2,1)}, u32[]{:S(2)}) copy-start(bf16[1,512,2048]{2,1,0:T(8,128)(2,1)} %param.8) | copy-start | bytes 6291460
  3.2 14.4 %collective-permute-start = (bf16[64,2176]{1,0:T(8,128)(2,1)S(1)}, bf16[64,2176]{1,0:T(8,128)(2,1)S(1)}, u32[]{:S(2)}, u32[]{:S(2)}) collective-permute-start(bf16[64,2176]{1,0:T(8,128)(2,1)S(1)} %get-tuple-element.31), channel_id=1, source_target_pairs={{0,2},{2,0},{4,6},{6,4},{8,10},{10,8},{12,14},{14,12},{1,3},{3,1},... | collective-permute-start | bytes 835592 | tf_op jit(solution)/shard_map/ppermute | solution.py:520
  4.8 12.8 %collective-permute-start.1 = (bf16[64,2176]{1,0:T(8,128)(2,1)S(1)}, bf16[64,2176]{1,0:T(8,128)(2,1)S(1)}, u32[]{:S(2)}, u32[]{:S(2)}) collective-permute-start(bf16[64,2176]{1,0:T(8,128)(2,1)S(1)} %get-tuple-element.32), channel_id=1, source_target_pairs={{2,4},{4,2},{6,8},{8,6},{10,12},{12,10},{3,5},{5,3},{7,9},{9,7},{1... | collective-permute-start | bytes 835592 | tf_op jit(solution)/shard_map/ppermute | solution.py:526
  7.1 1.6 %copy-start.1 = (bf16[1,512,2048]{2,1,0:T(8,128)(2,1)S(1)}, bf16[1,512,2048]{2,1,0:T(8,128)(2,1)}, u32[]{:S(2)}) copy-start(bf16[1,512,2048]{2,1,0:T(8,128)(2,1)} %param.9) | copy-start | bytes 6291460
  19.4 5.7 %collective-permute-start.2 = (bf16[32,2176]{1,0:T(8,128)(2,1)S(1)}, bf16[32,2176]{1,0:T(8,128)(2,1)S(1)}, u32[]{:S(2)}, u32[]{:S(2)}) collective-permute-start(bf16[32,2176]{1,0:T(8,128)(2,1)S(1)} %get-tuple-element.33), channel_id=1, source_target_pairs={{0,2},{2,0},{4,6},{6,4},{8,10},{10,8},{12,14},{14,12},{1,3},{3,1},... | collective-permute-start | bytes 417800 | tf_op jit(solution)/shard_map/ppermute | solution.py:520
  21.0 7.8 %collective-permute-start.3 = (bf16[32,2176]{1,0:T(8,128)(2,1)S(1)}, bf16[32,2176]{1,0:T(8,128)(2,1)S(1)}, u32[]{:S(2)}, u32[]{:S(2)}) collective-permute-start(bf16[32,2176]{1,0:T(8,128)(2,1)S(1)} %get-tuple-element.34), channel_id=1, source_target_pairs={{2,4},{4,2},{6,8},{8,6},{10,12},{12,10},{3,5},{5,3},{7,9},{9,7},{1... | collective-permute-start | bytes 417800 | tf_op jit(solution)/shard_map/ppermute | solution.py:526

commit v7 on v6

--- a/solution.py
+++ b/solution.py
@@ -270,8 +270,8 @@
     at_o = pl.multiple_of(jnp.where(bounds.even, 0, last), gq)
 
     jobs = [
+        (k_hbm, k_ref, (n_ex - 1) * gk, (0, gk)), (k_hbm, k_ref, 0, (gk, edge)),
         (dec_hbm, dec_ref, None, None), (enc_hbm, enc_ref, None, None),
-        (k_hbm, k_ref, (n_ex - 1) * gk, (0, gk)), (k_hbm, k_ref, 0, (gk, edge)),
     ]
     for src, dst in ((q_hbm, q_ref), (g_hbm, g_ref), (o_hbm, o_ref)):
         jobs += [(src, dst, last, (last, gq)), (src, dst, 0, (0, gq))]
@@ -375,7 +375,7 @@
         mo_ref[:, cols] = jnp.where(even, before, after)
         yield
 
-    each_group(feats // LANES, feats // LANES, lambda group: [unit(group)], rate=4)
+    each_group(feats // LANES, feats // LANES, lambda group: [unit(group)], rate=8)
     after, before = pack_ref[0].astype(bf16), pack_ref[1].astype(bf16)
     me_ref[:, feats:] = jnp.where(even, after, before)
     mo_ref[:, feats:] = jnp.where(even, before, after)

time: 31.4 us -> 31.4 us (level)
  no operation moved by 1% of the time
where the time goes in v7:
time: 31.4 us; the launch traced here: 31.2 us
  Pallas kernels  15.4 us (49%)
  starting transfers between devices  7.75 us (25%)
  waiting for transfers between devices  5.73 us (18%)
  local copies, waits for them, and re-layouts  1.6 us (5%)
  between operations  0.74 us (2%)
    pallas_call x1, Pallas kernels, shards(): call(functools.partial(interior_kernel, shape), tables + [anywhere] + [in...  6.96 us
    ppermute x2, starting transfers between devices, swap_odd(): return lax.ppermute(x, 'seq', pairs)  4.58 us
    ppermute x2, waiting for transfers between devices, swap_odd(): return lax.ppermute(x, 'seq', pairs)  3.74 us
    ppermute x2, starting transfers between devices, swap_even(): lax.ppermute(x, 'seq', [(i, i ^ 1) for i in range(count) if i ^ 1 < count])  3.17 us
    pallas_call x1, Pallas kernels, shards(): call(functools.partial(stats_kernel, shape), [scalars] + [off_chip] * 6,...  2.53 us
    pallas_call x1, Pallas kernels, shards(): call(functools.partial(edge_kernel, shape), tables + [inside] * 11 + [any...  2.43 us
    ppermute x2, waiting for transfers between devices, swap_even(): lax.ppermute(x, 'seq', [(i, i ^ 1) for i in range(count) if i ^ 1 < count])  1.99 us
    pallas_call x1, Pallas kernels, shards(): call(functools.partial(ready_kernel, shape), tables + [inside] * 11, [out...  1.76 us
  transfers between devices with their start and end apart: 4, of which 2 were waited for; matrix products, arithmetic and copies ran while one was open for 0% of the time, Pallas kernels for 28%

profile of v7, /device:TPU:16, one launch (start us, length us, event | category | flops | bytes accessed | tf_op | source)
XLA Modules:
  0.0 31.2 jit_solution(1363419851083100466)
XLA Ops:
  0.6 0.0 copy-start.3
  0.6 0.0 copy-start.2
  0.7 0.0 copy-start
  0.7 2.5 %shard_map.94 = (bf16[64,2176]{1,0:T(8,128)(2,1)S(1)}, bf16[64,2176]{1,0:T(8,128)(2,1)S(1)}, f32[4,1024]{1,0:T(4,128)S(1)}, bf16[128,2048]{1,0:T(8,128)(2,1)S(1)...) custom-call(s32[1]{0:T(128)} %bitcast.pos_ref.refs_2_, s32[1,33]{1,0:T(1,128)} %refs_0_.7, ...), custom_call_target="tpu_custom_call" | custom-call | flops 400000000 | bytes 2000000 | tf_op jit(solution)/shard_map/pallas_call | solution.py:547
  3.2 1.6 %collective-permute-start = (bf16[64,2176]{1,0:T(8,128)(2,1)S(1)}, bf16[64,2176]{1,0:T(8,128)(2,1)S(1)}, u32[]{:S(2)}, u32[]{:S(2)}) collective-permute-start(bf16[64,2176]{1,0:T(8,128)(2,1)S(1)} %get-tuple-element.31), channel_id=1, source_target_pairs={{0,2},{2,0},{4,6},{6,4},{8,10},{10,8},{12,14},{14,12},{1,3},{3,1},... | collective-permute-start | bytes 835592 | tf_op jit(solution)/shard_map/ppermute | solution.py:520
  4.8 2.3 %collective-permute-start.1 = (bf16[64,2176]{1,0:T(8,128)(2,1)S(1)}, bf16[64,2176]{1,0:T(8,128)(2,1)S(1)}, u32[]{:S(2)}, u32[]{:S(2)}) collective-permute-start(bf16[64,2176]{1,0:T(8,128)(2,1)S(1)} %get-tuple-element.32), channel_id=1, source_target_pairs={{2,4},{4,2},{6,8},{8,6},{10,12},{12,10},{3,5},{5,3},{7,9},{9,7},{1... | collective-permute-start | bytes 835592 | tf_op jit(solution)/shard_map/ppermute | solution.py:526
  7.1 0.0 copy-done.3
  7.1 0.0 copy-done.2
  7.1 0.0 copy-done
  7.1 0.0 copy-start.1
  7.1 1.6 %copy-done.1 = bf16[1,512,2048]{2,1,0:T(8,128)(2,1)S(1)} copy-done((bf16[1,512,2048]{2,1,0:T(8,128)(2,1)S(1)}, bf16[1,512,2048]{2,1,0:T(8,128)(2,1)}, u32[]{:S(2)}) %copy-start.1) | copy-done | bytes 2097176
  8.7 7.0 %shard_map.95 = (bf16[128,2048]{1,0:T(8,128)(2,1)}, bf16[512,2048]{1,0:T(8,128)(2,1)}, bf16[512,2048]{1,0:T(8,128)(2,1)}, bf16[64,2048]{1,0:T(8,128)(2,1)S(1)}, ...) custom-call(s32[1,33]{1,0:T(1,128)S(1)} %copy-done.2, s32[1,33]{1,0:T(1,128)S(1)} %copy-done.3, ...), custom_call_target="tpu_custom_call" | custom-call | flops 4000000000 | bytes 8000000 | tf_op jit(solution)/shard_map/pallas_call | solution.py:556
  15.7 2.0 %collective-permute-done.refs_4_.refs_3_ = bf16[64,2176]{1,0:T(8,128)(2,1)S(1)} collective-permute-done((bf16[64,2176]{1,0:T(8,128)(2,1)S(1)}, bf16[64,2176]{1,0:T(8,128)(2,1)S(1)}, u32[]{:S(2)}, u32[]{:S(2)}) %collective-permute-start) | collective-permute-done | bytes 278560 | tf_op jit(solution)/shard_map/ppermute | solution.py:520
  17.6 0.0 collective-permute-done.1.refs_5_.refs_4_
  17.6 1.7 %shard_map.96 = (bf16[32,2176]{1,0:T(8,128)(2,1)S(1)}, bf16[32,2176]{1,0:T(8,128)(2,1)S(1)}, bf16[192,1024]{1,0:T(8,128)(2,1)S(1)}, bf16[192,1024]{1,0:T(8,128)(2,1)S(1)}) custom-call(s32[1,33]{1,0:T(1,128)S(1)} %copy-done.2, s32[1,33]{1,0:T(1,128)S(1)} %copy-done.3, s32[1]{0:T(128)} %bitcast.pos_ref.refs_2_, ...), custom_call_target="tpu_custom_call" | custom-call | flops 800000000 | bytes 3000000 | tf_op jit(solution)/shard_map/pallas_call | solution.py:563
  19.4 1.6 %collective-permute-start.2 = (bf16[32,2176]{1,0:T(8,128)(2,1)S(1)}, bf16[32,2176]{1,0:T(8,128)(2,1)S(1)}, u32[]{:S(2)}, u32[]{:S(2)}) collective-permute-start(bf16[32,2176]{1,0:T(8,128)(2,1)S(1)} %get-tuple-element.33), channel_id=1, source_target_pairs={{0,2},{2,0},{4,6},{6,4},{8,10},{10,8},{12,14},{14,12},{1,3},{3,1},... | collective-permute-start | bytes 417800 | tf_op jit(solution)/shard_map/ppermute | solution.py:520
  20.9 2.3 %collective-permute-start.3 = (bf16[32,2176]{1,0:T(8,128)(2,1)S(1)}, bf16[32,2176]{1,0:T(8,128)(2,1)S(1)}, u32[]{:S(2)}, u32[]{:S(2)}) collective-permute-start(bf16[32,2176]{1,0:T(8,128)(2,1)S(1)} %get-tuple-element.34), channel_id=1, source_target_pairs={{2,4},{4,2},{6,8},{8,6},{10,12},{12,10},{3,5},{5,3},{7,9},{9,7},{1... | collective-permute-start | bytes 417800 | tf_op jit(solution)/shard_map/ppermute | solution.py:526
  23.2 1.8 %shard_map.97 = (f32[192,1024]{1,0:T(8,128)S(1)}, f32[192,1024]{1,0:T(8,128)S(1)}, f32[192,2048]{1,0:T(8,128)S(1)}, f32[192,2048]{1,0:T(8,128)S(1)}) custom-call(s32[1,33]{1,0:T(1,128)S(1)} %copy-done.2, s32[1,33]{1,0:T(1,128)S(1)} %copy-done.3, s32[1]{0:T(128)} %bitcast.pos_ref.refs_2_, bf16[64,2176]{1,0:T(8,128)(2,1)S(1)} %collective-permute-done.refs_4_.refs_3_, ...), custom_call_target="tpu_custom_call" | custom-call | flops 1000000000 | bytes 6000000 | tf_op jit(solution)/shard_map/pallas_call | solution.py:571
  25.0 0.0 collective-permute-done.2.refs_3_
  25.0 3.7 %collective-permute-done.3.refs_4_ = bf16[32,2176]{1,0:T(8,128)(2,1)S(1)} collective-permute-done((bf16[32,2176]{1,0:T(8,128)(2,1)S(1)}, bf16[32,2176]{1,0:T(8,128)(2,1)S(1)}, u32[]{:S(2)}, u32[]{:S(2)}) %collective-permute-start.3) | collective-permute-done | bytes 139296 | tf_op jit(solution)/shard_map/ppermute | solution.py:526
  28.8 2.4 %shard_map.98 = (bf16[128,2048]{1,0:T(8,128)(2,1)}, bf16[512,2048]{1,0:T(8,128)(2,1)}, bf16[512,2048]{1,0:T(8,128)(2,1)}) custom-call(s32[1,33]{1,0:T(1,128)S(1)} %copy-done.2, s32[1,33]{1,0:T(1,128)S(1)} %copy-done.3, s32[1]{0:T(128)} %bitcast.pos_ref.refs_2_, ...), custom_call_target="tpu_custom_call", output_to_operand_aliasing={{0}: (14, {}), {1}: (15, {}), {2}: (16, {})} | custom-call | flops 1000000000 | bytes 6000000 | tf_op jit(solution)/shard_map/pallas_call | solution.py:575
Async XLA Ops:
  0.6 6.5 %copy-start.3 = (s32[1,33]{1,0:T(1,128)S(1)}, s32[1,33]{1,0:T(1,128)}, u32[]{:S(2)}) copy-start(s32[1,33]{1,0:T(1,128)} %refs_1_.7) | copy-start | bytes 400
  0.6 6.5 %copy-start.2 = (s32[1,33]{1,0:T(1,128)S(1)}, s32[1,33]{1,0:T(1,128)}, u32[]{:S(2)}) copy-start(s32[1,33]{1,0:T(1,128)} %refs_0_.7) | copy-start | bytes 400
  0.7 6.5 %copy-start = (bf16[1,512,2048]{2,1,0:T(8,128)(2,1)S(1)}, bf16[1,512,2048]{2,1,0:T(8,128)(2,1)}, u32[]{:S(2)}) copy-start(bf16[1,512,2048]{2,1,0:T(8,128)(2,1)} %param.8) | copy-start | bytes 6291460
  3.2 14.4 %collective-permute-start = (bf16[64,2176]{1,0:T(8,128)(2,1)S(1)}, bf16[64,2176]{1,0:T(8,128)(2,1)S(1)}, u32[]{:S(2)}, u32[]{:S(2)}) collective-permute-start(bf16[64,2176]{1,0:T(8,128)(2,1)S(1)} %get-tuple-element.31), channel_id=1, source_target_pairs={{0,2},{2,0},{4,6},{6,4},{8,10},{10,8},{12,14},{14,12},{1,3},{3,1},... | collective-permute-start | bytes 835592 | tf_op jit(solution)/shard_map/ppermute | solution.py:520
  4.8 12.8 %collective-permute-start.1 = (bf16[64,2176]{1,0:T(8,128)(2,1)S(1)}, bf16[64,2176]{1,0:T(8,128)(2,1)S(1)}, u32[]{:S(2)}, u32[]{:S(2)}) collective-permute-start(bf16[64,2176]{1,0:T(8,128)(2,1)S(1)} %get-tuple-element.32), channel_id=1, source_target_pairs={{2,4},{4,2},{6,8},{8,6},{10,12},{12,10},{3,5},{5,3},{7,9},{9,7},{1... | collective-permute-start | bytes 835592 | tf_op jit(solution)/shard_map/ppermute | solution.py:526
  7.1 1.6 %copy-start.1 = (bf16[1,512,2048]{2,1,0:T(8,128)(2,1)S(1)}, bf16[1,512,2048]{2,1,0:T(8,128)(2,1)}, u32[]{:S(2)}) copy-start(bf16[1,512,2048]{2,1,0:T(8,128)(2,1)} %param.9) | copy-start | bytes 6291460
  19.4 5.7 %collective-permute-start.2 = (bf16[32,2176]{1,0:T(8,128)(2,1)S(1)}, bf16[32,2176]{1,0:T(8,128)(2,1)S(1)}, u32[]{:S(2)}, u32[]{:S(2)}) collective-permute-start(bf16[32,2176]{1,0:T(8,128)(2,1)S(1)} %get-tuple-element.33), channel_id=1, source_target_pairs={{0,2},{2,0},{4,6},{6,4},{8,10},{10,8},{12,14},{14,12},{1,3},{3,1},... | collective-permute-start | bytes 417800 | tf_op jit(solution)/shard_map/ppermute | solution.py:520
  20.9 7.8 %collective-permute-start.3 = (bf16[32,2176]{1,0:T(8,128)(2,1)S(1)}, bf16[32,2176]{1,0:T(8,128)(2,1)S(1)}, u32[]{:S(2)}, u32[]{:S(2)}) collective-permute-start(bf16[32,2176]{1,0:T(8,128)(2,1)S(1)} %get-tuple-element.34), channel_id=1, source_target_pairs={{2,4},{4,2},{6,8},{8,6},{10,12},{12,10},{3,5},{5,3},{7,9},{9,7},{1... | collective-permute-start | bytes 417800 | tf_op jit(solution)/shard_map/ppermute | solution.py:526
